TPU v7x, 512 devices: a whole 4x8x8 slice. The times are simulated.
512 devices in a mesh: py: 16 (over x, z_lo, core), px: 32 (over y, z_hi).
Axes of the slice: x: 4, y: 8, z: 8 (z_hi: 4, z_lo: 2; z = z_hi * 2 + z_lo), core: 2. Of those that a mesh axis runs over, the one named last changes fastest.
Arguments:
- forcing: float32 [1024, 32, 1024], P('px', 'py')
- inv_density: float32 [1024, 32, 1024], P('px', 'py'), may hold values from 0.5 to 4
- stretch_x: float32 [1024], P('px'), may hold values from 0.5 to 2
- stretch_y: float32 [32], P('py'), may hold values from 0.5 to 2
- stretch_z: float32 [1024], replicated, may hold values from 0.5 to 2
- lines_z0: float32 [4, 256, 256], replicated
- lines_x0: float32 [4, 256, 256], replicated
- lines_z1: float32 [2, 256, 256], replicated
- lines_x1: float32 [2, 256, 256], replicated
- coarse_inverse: float32 [512, 512], P(('py', 'px')), as said below
Outputs:
- pressure_adjoint: float32 [1024, 32, 1024], P('px', 'py')
Inputs may be any that keep to these rules, and one draw needn't show every extreme that they name: coarse_inverse is symmetric.
All inputs are finite; a program needn't handle non-finite values.
Results may differ from a plain program's by a relative error of at most 0.0001.
Values sent between devices are 32-bit elements; how exact they have to be, the bound alone decides.
No kernel may reach another device: no remote copies, remote signals or barrier semaphores. Data moves between devices by JAX's collectives and lax.ppermute only.
A program may use at most 64 MiB of HBM per device.

v0:
```python
import jax
import jax.numpy as jnp
from jax import lax
from jax.sharding import PartitionSpec as P

shift_term = 0.1
highest = lax.Precision.HIGHEST


def with_halo(array, sides, width):
    for axis, dim in sides:
        peers, length = (lax.axis_size(axis), array.shape[dim])
        up = [(i, (i + 1) % peers) for i in range(peers - 1)]
        down = [(j, i) for i, j in up]
        last = lax.slice_in_dim(array, length - width, length, axis=dim)
        initial = lax.slice_in_dim(array, 0, width, axis=dim)
        before = lax.ppermute(last, axis, up)
        after = lax.ppermute(initial, axis, down)
        array = jnp.concatenate([before, array, after], axis=dim)
    return array


def pad_axis(field, axis):
    widths = [(0, 0), (0, 0), (0, 0)]
    widths[axis] = (1, 1)
    return jnp.pad(field, widths)


def beside_sum(padded, axis):
    length = padded.shape[axis] - 2
    return lax.slice_in_dim(padded, 2, length + 2, axis=axis) + lax.slice_in_dim(
        padded, 0, length, axis=axis
    )


def with_rim(field):
    return with_halo(field, (("py", 1), ("px", 0)), 1)


def operate(field, level):
    density, coef_x, coef_y, coef_z = (level[0], level[1], level[2], level[3])
    padded = with_rim(field)
    twice = 2.0 * field
    near_x = beside_sum(padded[:, 1:-1], 0)
    near_y = beside_sum(padded[1:-1], 1)
    near_z = beside_sum(pad_axis(field, 2), 2)
    stencil = (
        coef_x[:, None, None] * (twice - near_x)
        + coef_y[None, :, None] * (twice - near_y)
        + coef_z[None, None, :] * (twice - near_z)
    )
    return shift_term * field + density * stencil


def diagonal(density, coef_x, coef_y, coef_z):
    return shift_term + 2.0 * density * (
        coef_x[:, None, None] + coef_y[None, :, None] + coef_z[None, None, :]
    )


def lines_along_z(field, blocks):
    first, second, third = field.shape
    count = blocks.shape[0]
    grouped = field.reshape(first * second, count, third // count)
    return jnp.einsum("nkb,kcb->nkc", grouped, blocks, precision=highest).reshape(
        first, second, third
    )


def lines_along_x(field, blocks):
    piece = lax.all_to_all(field, "px", split_axis=2, concat_axis=0, tiled=True)
    rows, items, depth = piece.shape
    count = blocks.shape[0]
    grouped = piece.reshape(count, rows // count, items * depth)
    solved = jnp.einsum("kcb,kbn->kcn", blocks, grouped, precision=highest).reshape(
        rows, items, depth
    )
    return lax.all_to_all(solved, "px", split_axis=0, concat_axis=2, tiled=True)


def sweep(iterate, rhs, level, from_zero):
    if from_zero:
        residual = rhs
    else:
        residual = rhs - operate(iterate, level)
    iterate = iterate + lines_along_z(residual / level[4], level[5])
    residual = rhs - operate(iterate, level)
    scaled = residual / level[4]
    return iterate + lines_along_x(scaled, level[6])


def restrict_padded(padded, axis):
    length = padded.shape[axis] - 2

    def take(start):
        return lax.slice_in_dim(padded, start, start + length - 1, stride=2, axis=axis)

    return (take(0) + 3.0 * take(1) + 3.0 * take(2) + take(3)) * 0.125


def prolong_padded(padded, axis):
    length = padded.shape[axis] - 2
    lower = lax.slice_in_dim(padded, 0, length, axis=axis)
    middle = lax.slice_in_dim(padded, 1, length + 1, axis=axis)
    upper = lax.slice_in_dim(padded, 2, length + 2, axis=axis)
    even = (3.0 * middle + lower) * 0.25
    odd = (3.0 * middle + upper) * 0.25
    stacked = jnp.stack([even, odd], axis=axis + 1)
    shape = list(even.shape)
    shape[axis] = 2 * length
    return stacked.reshape(shape)


def halve(vector):
    return vector.reshape(-1, 2).sum(axis=1) * 0.125


def coarsen(density, coef_x, coef_y, coef_z):
    first, second, third = density.shape
    dense_one = density.reshape(first // 2, 2, second // 2, 2, third // 2, 2).mean(axis=(1, 3, 5))
    return (dense_one, halve(coef_x), halve(coef_y), halve(coef_z))


def per_device(
    forcing,
    inv_density,
    stretch_x,
    stretch_y,
    stretch_z,
    lines_z0,
    lines_x0,
    lines_z1,
    lines_x1,
    coarse_inverse,
):
    fine = (
        inv_density,
        stretch_x,
        stretch_y,
        stretch_z,
        diagonal(inv_density, stretch_x, stretch_y, stretch_z),
        lines_z0,
        lines_x0,
    )
    dense_one, coef_x1, coef_y1, coef_z1 = coarsen(inv_density, stretch_x, stretch_y, stretch_z)
    middle = (
        dense_one,
        coef_x1,
        coef_y1,
        coef_z1,
        diagonal(dense_one, coef_x1, coef_y1, coef_z1),
        lines_z1,
        lines_x1,
    )
    iterate = jnp.zeros_like(forcing)
    iterate = sweep(iterate, forcing, fine, 0 == 0)
    residual = forcing - operate(iterate, fine)
    padded = with_rim(residual)
    right_one = restrict_padded(restrict_padded(padded, 0), 1)
    right_one = restrict_padded(pad_axis(right_one, 2), 2)
    level_one = sweep(jnp.zeros_like(right_one), right_one, middle, True)
    residual_one = right_one - operate(level_one, middle)
    local_mean = jnp.mean(residual_one)
    values = lax.all_gather(local_mean.reshape(1), ("py", "px"), axis=0, tiled=True)
    correction = jnp.dot(coarse_inverse, values, precision=highest)[0]
    level_one = level_one + correction
    level_one = sweep(level_one, right_one, middle, False)
    padded = with_rim(level_one)
    raised = prolong_padded(prolong_padded(padded, 0), 1)
    raised = prolong_padded(pad_axis(raised, 2), 2)
    iterate = iterate + raised
    iterate = sweep(iterate, forcing, fine, False)
    return iterate


def solution(mesh):
    placed = (
        P("px", "py", None),
        P("px", "py", None),
        P("px"),
        P("py"),
        P(),
        P(),
        P(),
        P(),
        P(),
        P(("py", "px"), None),
    )
    return jax.shard_map(
        per_device, mesh=mesh, in_specs=placed, out_specs=P("px", "py", None), check_vma=False
    )
```

profile of v0, /device:TPU:72, one launch (start us, length us, event | category | flops | bytes accessed | tf_op | source)
XLA Modules:
  0.0 552.7 jit_solution(6550047984583528404)
XLA Ops:
  6.1 3.6 collective-permute-start.1
  12.3 6.1 %collective-permute-start.3 = (f32[1,4,1024]{2,0,1:T(1,128)S(1)}, f32[1,4,1024]{2,0,1:T(1,128)S(1)}, u32[]{:S(2)}, u32[]{:S(2)}) collective-permute-start(f32[1,4,1024]{2,0,1:T(1,128)S(1)} %get-tuple-element.16), channel_id=1, source_target_pairs={{0,1},{1,2},{2,3},{3,4},{4,5},{5,6},{6,7},{7,8},{8,9},{9,10},{10,1... | collective-permute-start | bytes 49160 | tf_op jit(solution)/shard_map/ppermute | solution.py:17
  18.4 5.8 %collective-permute-start.2 = (f32[1,4,1024]{2,0,1:T(1,128)S(1)}, f32[1,4,1024]{2,0,1:T(1,128)S(1)}, u32[]{:S(2)}, u32[]{:S(2)}) collective-permute-start(f32[1,4,1024]{2,0,1:T(1,128)S(1)} %get-tuple-element.15), channel_id=1, source_target_pairs={{1,0},{2,1},{3,2},{4,3},{5,4},{6,5},{7,6},{8,7},{9,8},{10,9},{11,1... | collective-permute-start | bytes 49160 | tf_op jit(solution)/shard_map/ppermute | solution.py:18
  29.6 26.9 %all_to_all.132 = f32[32,1,2048]{2,1,0:T(1,128)S(1)} all-to-all(f32[32,1,2048]{2,1,0:T(1,128)S(1)} %reshape.419), channel_id=1, replica_groups=mesh['py'=16,'px'=32] {'px'}, dimensions={0} | all-to-all | bytes 524288 | tf_op jit(solution)/shard_map/all_to_all | solution.py:71
  68.5 19.5 %all_to_all.133 = f32[32,1,2048]{2,1,0:T(1,128)S(1)} all-to-all(f32[32,1,2048]{2,1,0:T(1,128)S(1)} %reshape.421), channel_id=1, replica_groups=mesh['py'=16,'px'=32] {'px'}, dimensions={0} | all-to-all | bytes 524288 | tf_op jit(solution)/shard_map/all_to_all | solution.py:78
  95.5 3.6 collective-permute-start.5
  104.1 6.4 %collective-permute-start.6 = (f32[1,4,1024]{2,0,1:T(1,128)S(1)}, f32[1,4,1024]{2,0,1:T(1,128)S(1)}, u32[]{:S(2)}, u32[]{:S(2)}) collective-permute-start(f32[1,4,1024]{2,0,1:T(1,128)S(1)} %get-tuple-element.13), channel_id=1, source_target_pairs={{1,0},{2,1},{3,2},{4,3},{5,4},{6,5},{7,6},{8,7},{9,8},{10,9},{11,1... | collective-permute-start | bytes 49160 | tf_op jit(solution)/shard_map/ppermute | solution.py:18
  118.5 3.8 collective-permute-done.8
  122.4 5.9 %collective-permute-start.11 = (f32[1,4,1024]{2,0,1:T(1,128)S(1)}, f32[1,4,1024]{2,0,1:T(1,128)S(1)}, u32[]{:S(2)}, u32[]{:S(2)}) collective-permute-start(f32[1,4,1024]{2,0,1:T(1,128)S(1)} %get-tuple-element.12), channel_id=1, source_target_pairs={{1,0},{2,1},{3,2},{4,3},{5,4},{6,5},{7,6},{8,7},{9,8},{10,9},{11,1... | collective-permute-start | bytes 49160 | tf_op jit(solution)/shard_map/ppermute | solution.py:18
  130.5 9.7 %reduce_sum.53 = f32[16,2,512,2]{3,2,1,0:T(8,128)} reshape(f32[32,1024]{1,0:T(8,128)S(1)} %reduce_sum.52) | data formatting | bytes 262144 | tf_op jit(solution)/shard_map/reduce_sum | solution.py:120
  140.3 4.6 reduce_sum.54
  157.7 3.6 collective-permute-start.13
  165.5 6.9 %collective-permute-start.14 = (f32[1,3,512]{2,0,1:T(1,128)S(1)}, f32[1,3,512]{2,0,1:T(1,128)S(1)}, u32[]{:S(2)}, u32[]{:S(2)}) collective-permute-start(f32[1,3,512]{2,0,1:T(1,128)S(1)} %get-tuple-element.41), channel_id=1, source_target_pairs={{1,0},{2,1},{3,2},{4,3},{5,4},{6,5},{7,6},{8,7},{9,8},{10,9},{11,1... | collective-permute-start | bytes 18440 | tf_op jit(solution)/shard_map/ppermute | solution.py:18
  177.1 22.5 %all_to_all.134 = f32[32,1,256]{2,1,0:T(1,128)S(1)} all-to-all(f32[32,1,256]{2,1,0:T(1,128)S(1)} %reshape.423), channel_id=1, replica_groups=mesh['py'=16,'px'=32] {'px'}, dimensions={0} | all-to-all | bytes 65536 | tf_op jit(solution)/shard_map/all_to_all | solution.py:71
  208.0 15.4 %all_to_all.135 = f32[32,1,256]{2,1,0:T(1,128)S(1)} all-to-all(f32[32,1,256]{2,1,0:T(1,128)S(1)} %reshape.425), channel_id=1, replica_groups=mesh['py'=16,'px'=32] {'px'}, dimensions={0} | all-to-all | bytes 65536 | tf_op jit(solution)/shard_map/all_to_all | solution.py:78
  236.7 6.3 %collective-permute-start.18 = (f32[1,3,512]{2,0,1:T(1,128)S(1)}, f32[1,3,512]{2,0,1:T(1,128)S(1)}, u32[]{:S(2)}, u32[]{:S(2)}) collective-permute-start(f32[1,3,512]{2,0,1:T(1,128)S(1)} %get-tuple-element.39), channel_id=1, source_target_pairs={{1,0},{2,1},{3,2},{4,3},{5,4},{6,5},{7,6},{8,7},{9,8},{10,9},{11,1... | collective-permute-start | bytes 18440 | tf_op jit(solution)/shard_map/ppermute | solution.py:18
  245.8 97.2 %all-reduce.10 = f32[512]{0:T(512)S(1)} all-reduce(f32[512]{0:T(512)S(1)} %dynamic-update-slice), channel_id=1, replica_groups=mesh['py'=16,'px'=32] {'py','px'}, use_global_device_ids=true, to_apply=%add.10 | all-reduce | flops 512 | bytes 4096
  344.3 3.5 collective-permute-start.21
  349.7 3.3 collective-permute-done.20
  355.4 6.5 %collective-permute-start.22 = (f32[1,3,512]{2,0,1:T(1,128)S(1)}, f32[1,3,512]{2,0,1:T(1,128)S(1)}, u32[]{:S(2)}, u32[]{:S(2)}) collective-permute-start(f32[1,3,512]{2,0,1:T(1,128)S(1)} %get-tuple-element.37), channel_id=1, source_target_pairs={{1,0},{2,1},{3,2},{4,3},{5,4},{6,5},{7,6},{8,7},{9,8},{10,9},{11,1... | collective-permute-start | bytes 18440 | tf_op jit(solution)/shard_map/ppermute | solution.py:18
  371.8 4.4 collective-permute-start.27
  376.2 4.7 collective-permute-start.26
  384.3 22.9 %all_to_all.136 = f32[32,1,256]{2,1,0:T(1,128)S(1)} all-to-all(f32[32,1,256]{2,1,0:T(1,128)S(1)} %reshape.427), channel_id=1, replica_groups=mesh['py'=16,'px'=32] {'px'}, dimensions={0} | all-to-all | bytes 65536 | tf_op jit(solution)/shard_map/all_to_all | solution.py:71
  411.2 15.2 %all_to_all.137 = f32[32,1,256]{2,1,0:T(1,128)S(1)} all-to-all(f32[32,1,256]{2,1,0:T(1,128)S(1)} %reshape.429), channel_id=1, replica_groups=mesh['py'=16,'px'=32] {'px'}, dimensions={0} | all-to-all | bytes 65536 | tf_op jit(solution)/shard_map/all_to_all | solution.py:78
  438.1 6.7 %collective-permute-start.31 = (f32[1,3,512]{2,0,1:T(1,128)S(1)}, f32[1,3,512]{2,0,1:T(1,128)S(1)}, u32[]{:S(2)}, u32[]{:S(2)}) collective-permute-start(f32[1,3,512]{2,0,1:T(1,128)S(1)} %get-tuple-element.34), channel_id=1, source_target_pairs={{1,0},{2,1},{3,2},{4,3},{5,4},{6,5},{7,6},{8,7},{9,8},{10,9},{11,1... | collective-permute-start | bytes 18440 | tf_op jit(solution)/shard_map/ppermute | solution.py:18
  449.2 3.6 collective-permute-start.33
  458.9 6.5 %collective-permute-start.34 = (f32[1,4,1024]{2,0,1:T(1,128)S(1)}, f32[1,4,1024]{2,0,1:T(1,128)S(1)}, u32[]{:S(2)}, u32[]{:S(2)}) collective-permute-start(f32[1,4,1024]{2,0,1:T(1,128)S(1)} %get-tuple-element.9), channel_id=1, source_target_pairs={{1,0},{2,1},{3,2},{4,3},{5,4},{6,5},{7,6},{8,7},{9,8},{10,9},{11,1... | collective-permute-start | bytes 49160 | tf_op jit(solution)/shard_map/ppermute | solution.py:18
  469.4 5.1 collective-permute-start.36
  478.9 4.1 collective-permute-start.39
  483.0 4.8 collective-permute-start.38
  491.5 24.6 %all_to_all.138 = f32[32,1,2048]{2,1,0:T(1,128)S(1)} all-to-all(f32[32,1,2048]{2,1,0:T(1,128)S(1)} %reshape.431), channel_id=1, replica_groups=mesh['py'=16,'px'=32] {'px'}, dimensions={0} | all-to-all | bytes 524288 | tf_op jit(solution)/shard_map/all_to_all | solution.py:71
  525.6 20.5 %all_to_all.139 = f32[32,1,2048]{2,1,0:T(1,128)S(1)} all-to-all(f32[32,1,2048]{2,1,0:T(1,128)S(1)} %reshape.433), channel_id=1, replica_groups=mesh['py'=16,'px'=32] {'px'}, dimensions={0} | all-to-all | bytes 524288 | tf_op jit(solution)/shard_map/all_to_all | solution.py:78
  (237 shorter events, 165.5 us)
Async XLA Ops:
  4.2 6.3 %collective-permute-start = (f32[32,1,1024]{2,0,1:T(8,128)S(1)}, f32[32,1,1024]{2,0,1:T(8,128)S(1)}, u32[]{:S(2)}, u32[]{:S(2)}) collective-permute-start(f32[32,1,1024]{2,0,1:T(8,128)S(1)} %get-tuple-element.26), channel_id=1, source_target_pairs={{0,32},{32,64},{64,96},{96,128},{128,160},{160,192},{192,224},{224... | collective-permute-start | bytes 393224 | tf_op jit(solution)/shard_map/ppermute | solution.py:17
  6.1 6.1 %collective-permute-start.1 = (f32[32,1,1024]{2,0,1:T(8,128)S(1)}, f32[32,1,1024]{2,0,1:T(8,128)S(1)}, u32[]{:S(2)}, u32[]{:S(2)}) collective-permute-start(f32[32,1,1024]{2,0,1:T(8,128)S(1)} %get-tuple-element.25), channel_id=1, source_target_pairs={{32,0},{64,32},{96,64},{128,96},{160,128},{192,160},{224,192},{256... | collective-permute-start | bytes 393224 | tf_op jit(solution)/shard_map/ppermute | solution.py:18
  12.3 11.9 %collective-permute-start.3 = (f32[1,4,1024]{2,0,1:T(1,128)S(1)}, f32[1,4,1024]{2,0,1:T(1,128)S(1)}, u32[]{:S(2)}, u32[]{:S(2)}) collective-permute-start(f32[1,4,1024]{2,0,1:T(1,128)S(1)} %get-tuple-element.16), channel_id=1, source_target_pairs={{0,1},{1,2},{2,3},{3,4},{4,5},{5,6},{6,7},{7,8},{8,9},{9,10},{10,1... | collective-permute-start | bytes 49160 | tf_op jit(solution)/shard_map/ppermute | solution.py:17
  18.4 8.1 %collective-permute-start.2 = (f32[1,4,1024]{2,0,1:T(1,128)S(1)}, f32[1,4,1024]{2,0,1:T(1,128)S(1)}, u32[]{:S(2)}, u32[]{:S(2)}) collective-permute-start(f32[1,4,1024]{2,0,1:T(1,128)S(1)} %get-tuple-element.15), channel_id=1, source_target_pairs={{1,0},{2,1},{3,2},{4,3},{5,4},{6,5},{7,6},{8,7},{9,8},{10,9},{11,1... | collective-permute-start | bytes 49160 | tf_op jit(solution)/shard_map/ppermute | solution.py:18
  93.5 6.3 %collective-permute-start.4 = (f32[32,1,1024]{2,0,1:T(8,128)S(1)}, f32[32,1,1024]{2,0,1:T(8,128)S(1)}, u32[]{:S(2)}, u32[]{:S(2)}) collective-permute-start(f32[32,1,1024]{2,0,1:T(8,128)S(1)} %get-tuple-element.24), channel_id=1, source_target_pairs={{0,32},{32,64},{64,96},{96,128},{128,160},{160,192},{192,224},{224... | collective-permute-start | bytes 393224 | tf_op jit(solution)/shard_map/ppermute | solution.py:17
  95.5 6.1 %collective-permute-start.5 = (f32[32,1,1024]{2,0,1:T(8,128)S(1)}, f32[32,1,1024]{2,0,1:T(8,128)S(1)}, u32[]{:S(2)}, u32[]{:S(2)}) collective-permute-start(f32[32,1,1024]{2,0,1:T(8,128)S(1)} %get-tuple-element.23), channel_id=1, source_target_pairs={{32,0},{64,32},{96,64},{128,96},{160,128},{192,160},{224,192},{256... | collective-permute-start | bytes 393224 | tf_op jit(solution)/shard_map/ppermute | solution.py:18
  101.7 10.7 %collective-permute-start.7 = (f32[1,4,1024]{2,0,1:T(1,128)S(1)}, f32[1,4,1024]{2,0,1:T(1,128)S(1)}, u32[]{:S(2)}, u32[]{:S(2)}) collective-permute-start(f32[1,4,1024]{2,0,1:T(1,128)S(1)} %get-tuple-element.14), channel_id=1, source_target_pairs={{0,1},{1,2},{2,3},{3,4},{4,5},{5,6},{6,7},{7,8},{8,9},{9,10},{10,1... | collective-permute-start | bytes 49160 | tf_op jit(solution)/shard_map/ppermute | solution.py:17
  104.1 8.3 %collective-permute-start.6 = (f32[1,4,1024]{2,0,1:T(1,128)S(1)}, f32[1,4,1024]{2,0,1:T(1,128)S(1)}, u32[]{:S(2)}, u32[]{:S(2)}) collective-permute-start(f32[1,4,1024]{2,0,1:T(1,128)S(1)} %get-tuple-element.13), channel_id=1, source_target_pairs={{1,0},{2,1},{3,2},{4,3},{5,4},{6,5},{7,6},{8,7},{9,8},{10,9},{11,1... | collective-permute-start | bytes 49160 | tf_op jit(solution)/shard_map/ppermute | solution.py:18
  112.8 5.7 %collective-permute-start.9 = (f32[32,1,1024]{2,0,1:T(8,128)S(1)}, f32[32,1,1024]{2,0,1:T(8,128)S(1)}, u32[]{:S(2)}, u32[]{:S(2)}) collective-permute-start(f32[32,1,1024]{2,0,1:T(8,128)S(1)} %get-tuple-element.22), channel_id=1, source_target_pairs={{32,0},{64,32},{96,64},{128,96},{160,128},{192,160},{224,192},{256... | collective-permute-start | bytes 393224 | tf_op jit(solution)/shard_map/ppermute | solution.py:18
  116.0 6.3 %collective-permute-start.8 = (f32[32,1,1024]{2,0,1:T(8,128)S(1)}, f32[32,1,1024]{2,0,1:T(8,128)S(1)}, u32[]{:S(2)}, u32[]{:S(2)}) collective-permute-start(f32[32,1,1024]{2,0,1:T(8,128)S(1)} %get-tuple-element.21), channel_id=1, source_target_pairs={{0,32},{32,64},{64,96},{96,128},{128,160},{160,192},{192,224},{224... | collective-permute-start | bytes 393224 | tf_op jit(solution)/shard_map/ppermute | solution.py:17
  122.4 24.1 %collective-permute-start.11 = (f32[1,4,1024]{2,0,1:T(1,128)S(1)}, f32[1,4,1024]{2,0,1:T(1,128)S(1)}, u32[]{:S(2)}, u32[]{:S(2)}) collective-permute-start(f32[1,4,1024]{2,0,1:T(1,128)S(1)} %get-tuple-element.12), channel_id=1, source_target_pairs={{1,0},{2,1},{3,2},{4,3},{5,4},{6,5},{7,6},{8,7},{9,8},{10,9},{11,1... | collective-permute-start | bytes 49160 | tf_op jit(solution)/shard_map/ppermute | solution.py:18
  128.3 18.2 %collective-permute-start.10 = (f32[1,4,1024]{2,0,1:T(1,128)S(1)}, f32[1,4,1024]{2,0,1:T(1,128)S(1)}, u32[]{:S(2)}, u32[]{:S(2)}) collective-permute-start(f32[1,4,1024]{2,0,1:T(1,128)S(1)} %get-tuple-element.11), channel_id=1, source_target_pairs={{0,1},{1,2},{2,3},{3,4},{4,5},{5,6},{6,7},{7,8},{8,9},{9,10},{10,1... | collective-permute-start | bytes 49160 | tf_op jit(solution)/shard_map/ppermute | solution.py:17
  155.8 5.6 %collective-permute-start.12 = (f32[16,1,512]{2,0,1:T(8,128)S(1)}, f32[16,1,512]{2,0,1:T(8,128)S(1)}, u32[]{:S(2)}, u32[]{:S(2)}) collective-permute-start(f32[16,1,512]{2,0,1:T(8,128)S(1)} %reshape.396), channel_id=1, source_target_pairs={{0,32},{32,64},{64,96},{96,128},{128,160},{160,192},{192,224},{224... | collective-permute-start | bytes 98312 | tf_op jit(solution)/shard_map/ppermute | solution.py:17
  157.7 5.8 %collective-permute-start.13 = (f32[16,1,512]{2,0,1:T(8,128)S(1)}, f32[16,1,512]{2,0,1:T(8,128)S(1)}, u32[]{:S(2)}, u32[]{:S(2)}) collective-permute-start(f32[16,1,512]{2,0,1:T(8,128)S(1)} %reshape.396), channel_id=1, source_target_pairs={{32,0},{64,32},{96,64},{128,96},{160,128},{192,160},{224,192},{256... | collective-permute-start | bytes 98312 | tf_op jit(solution)/shard_map/ppermute | solution.py:18
  163.5 8.9 %collective-permute-start.15 = (f32[1,3,512]{2,0,1:T(1,128)S(1)}, f32[1,3,512]{2,0,1:T(1,128)S(1)}, u32[]{:S(2)}, u32[]{:S(2)}) collective-permute-start(f32[1,3,512]{2,0,1:T(1,128)S(1)} %get-tuple-element.42), channel_id=1, source_target_pairs={{0,1},{1,2},{2,3},{3,4},{4,5},{5,6},{6,7},{7,8},{8,9},{9,10},{10,1... | collective-permute-start | bytes 18440 | tf_op jit(solution)/shard_map/ppermute | solution.py:17
  165.5 8.2 %collective-permute-start.14 = (f32[1,3,512]{2,0,1:T(1,128)S(1)}, f32[1,3,512]{2,0,1:T(1,128)S(1)}, u32[]{:S(2)}, u32[]{:S(2)}) collective-permute-start(f32[1,3,512]{2,0,1:T(1,128)S(1)} %get-tuple-element.41), channel_id=1, source_target_pairs={{1,0},{2,1},{3,2},{4,3},{5,4},{6,5},{7,6},{8,7},{9,8},{10,9},{11,1... | collective-permute-start | bytes 18440 | tf_op jit(solution)/shard_map/ppermute | solution.py:18
  234.1 8.9 %collective-permute-start.19 = (f32[1,3,512]{2,0,1:T(1,128)S(1)}, f32[1,3,512]{2,0,1:T(1,128)S(1)}, u32[]{:S(2)}, u32[]{:S(2)}) collective-permute-start(f32[1,3,512]{2,0,1:T(1,128)S(1)} %get-tuple-element.40), channel_id=1, source_target_pairs={{0,1},{1,2},{2,3},{3,4},{4,5},{5,6},{6,7},{7,8},{8,9},{9,10},{10,1... | collective-permute-start | bytes 18440 | tf_op jit(solution)/shard_map/ppermute | solution.py:17
  236.7 7.7 %collective-permute-start.18 = (f32[1,3,512]{2,0,1:T(1,128)S(1)}, f32[1,3,512]{2,0,1:T(1,128)S(1)}, u32[]{:S(2)}, u32[]{:S(2)}) collective-permute-start(f32[1,3,512]{2,0,1:T(1,128)S(1)} %get-tuple-element.39), channel_id=1, source_target_pairs={{1,0},{2,1},{3,2},{4,3},{5,4},{6,5},{7,6},{8,7},{9,8},{10,9},{11,1... | collective-permute-start | bytes 18440 | tf_op jit(solution)/shard_map/ppermute | solution.py:18
  344.3 5.5 collective-permute-start.21
  353.0 8.9 %collective-permute-start.23 = (f32[1,3,512]{2,0,1:T(1,128)S(1)}, f32[1,3,512]{2,0,1:T(1,128)S(1)}, u32[]{:S(2)}, u32[]{:S(2)}) collective-permute-start(f32[1,3,512]{2,0,1:T(1,128)S(1)} %get-tuple-element.38), channel_id=1, source_target_pairs={{0,1},{1,2},{2,3},{3,4},{4,5},{5,6},{6,7},{7,8},{8,9},{9,10},{10,1... | collective-permute-start | bytes 18440 | tf_op jit(solution)/shard_map/ppermute | solution.py:17
  355.4 7.8 %collective-permute-start.22 = (f32[1,3,512]{2,0,1:T(1,128)S(1)}, f32[1,3,512]{2,0,1:T(1,128)S(1)}, u32[]{:S(2)}, u32[]{:S(2)}) collective-permute-start(f32[1,3,512]{2,0,1:T(1,128)S(1)} %get-tuple-element.37), channel_id=1, source_target_pairs={{1,0},{2,1},{3,2},{4,3},{5,4},{6,5},{7,6},{8,7},{9,8},{10,9},{11,1... | collective-permute-start | bytes 18440 | tf_op jit(solution)/shard_map/ppermute | solution.py:18
  371.8 9.1 %collective-permute-start.27 = (f32[1,3,512]{2,0,1:T(1,128)S(1)}, f32[1,3,512]{2,0,1:T(1,128)S(1)}, u32[]{:S(2)}, u32[]{:S(2)}) collective-permute-start(f32[1,3,512]{2,0,1:T(1,128)S(1)} %get-tuple-element.36), channel_id=1, source_target_pairs={{0,1},{1,2},{2,3},{3,4},{4,5},{5,6},{6,7},{7,8},{8,9},{9,10},{10,1... | collective-permute-start | bytes 18440 | tf_op jit(solution)/shard_map/ppermute | solution.py:17
  376.2 6.4 %collective-permute-start.26 = (f32[1,3,512]{2,0,1:T(1,128)S(1)}, f32[1,3,512]{2,0,1:T(1,128)S(1)}, u32[]{:S(2)}, u32[]{:S(2)}) collective-permute-start(f32[1,3,512]{2,0,1:T(1,128)S(1)} %get-tuple-element.35), channel_id=1, source_target_pairs={{1,0},{2,1},{3,2},{4,3},{5,4},{6,5},{7,6},{8,7},{9,8},{10,9},{11,1... | collective-permute-start | bytes 18440 | tf_op jit(solution)/shard_map/ppermute | solution.py:18
  435.5 9.3 %collective-permute-start.30 = (f32[1,3,512]{2,0,1:T(1,128)S(1)}, f32[1,3,512]{2,0,1:T(1,128)S(1)}, u32[]{:S(2)}, u32[]{:S(2)}) collective-permute-start(f32[1,3,512]{2,0,1:T(1,128)S(1)} %get-tuple-element.33), channel_id=1, source_target_pairs={{0,1},{1,2},{2,3},{3,4},{4,5},{5,6},{6,7},{7,8},{8,9},{9,10},{10,1... | collective-permute-start | bytes 18440 | tf_op jit(solution)/shard_map/ppermute | solution.py:17
  438.1 7.7 %collective-permute-start.31 = (f32[1,3,512]{2,0,1:T(1,128)S(1)}, f32[1,3,512]{2,0,1:T(1,128)S(1)}, u32[]{:S(2)}, u32[]{:S(2)}) collective-permute-start(f32[1,3,512]{2,0,1:T(1,128)S(1)} %get-tuple-element.34), channel_id=1, source_target_pairs={{1,0},{2,1},{3,2},{4,3},{5,4},{6,5},{7,6},{8,7},{9,8},{10,9},{11,1... | collective-permute-start | bytes 18440 | tf_op jit(solution)/shard_map/ppermute | solution.py:18
  447.2 6.3 %collective-permute-start.32 = (f32[32,1,1024]{2,0,1:T(8,128)S(1)}, f32[32,1,1024]{2,0,1:T(8,128)S(1)}, u32[]{:S(2)}, u32[]{:S(2)}) collective-permute-start(f32[32,1,1024]{2,0,1:T(8,128)S(1)} %get-tuple-element.20), channel_id=1, source_target_pairs={{0,32},{32,64},{64,96},{96,128},{128,160},{160,192},{192,224},{224... | collective-permute-start | bytes 393224 | tf_op jit(solution)/shard_map/ppermute | solution.py:17
  449.2 7.1 %collective-permute-start.33 = (f32[32,1,1024]{2,0,1:T(8,128)S(1)}, f32[32,1,1024]{2,0,1:T(8,128)S(1)}, u32[]{:S(2)}, u32[]{:S(2)}) collective-permute-start(f32[32,1,1024]{2,0,1:T(8,128)S(1)} %get-tuple-element.19), channel_id=1, source_target_pairs={{32,0},{64,32},{96,64},{128,96},{160,128},{192,160},{224,192},{256... | collective-permute-start | bytes 393224 | tf_op jit(solution)/shard_map/ppermute | solution.py:18
  456.3 9.1 %collective-permute-start.35 = (f32[1,4,1024]{2,0,1:T(1,128)S(1)}, f32[1,4,1024]{2,0,1:T(1,128)S(1)}, u32[]{:S(2)}, u32[]{:S(2)}) collective-permute-start(f32[1,4,1024]{2,0,1:T(1,128)S(1)} %get-tuple-element.10), channel_id=1, source_target_pairs={{0,1},{1,2},{2,3},{3,4},{4,5},{5,6},{6,7},{7,8},{8,9},{9,10},{10,1... | collective-permute-start | bytes 49160 | tf_op jit(solution)/shard_map/ppermute | solution.py:17
  458.9 7.9 %collective-permute-start.34 = (f32[1,4,1024]{2,0,1:T(1,128)S(1)}, f32[1,4,1024]{2,0,1:T(1,128)S(1)}, u32[]{:S(2)}, u32[]{:S(2)}) collective-permute-start(f32[1,4,1024]{2,0,1:T(1,128)S(1)} %get-tuple-element.9), channel_id=1, source_target_pairs={{1,0},{2,1},{3,2},{4,3},{5,4},{6,5},{7,6},{8,7},{9,8},{10,9},{11,1... | collective-permute-start | bytes 49160 | tf_op jit(solution)/shard_map/ppermute | solution.py:18
  469.4 7.0 %collective-permute-start.36 = (f32[32,1,1024]{2,0,1:T(8,128)S(1)}, f32[32,1,1024]{2,0,1:T(8,128)S(1)}, u32[]{:S(2)}, u32[]{:S(2)}) collective-permute-start(f32[32,1,1024]{2,0,1:T(8,128)S(1)} %get-tuple-element.18), channel_id=1, source_target_pairs={{0,32},{32,64},{64,96},{96,128},{128,160},{160,192},{192,224},{224... | collective-permute-start | bytes 393224 | tf_op jit(solution)/shard_map/ppermute | solution.py:17
  478.9 8.9 %collective-permute-start.39 = (f32[1,4,1024]{2,0,1:T(1,128)S(1)}, f32[1,4,1024]{2,0,1:T(1,128)S(1)}, u32[]{:S(2)}, u32[]{:S(2)}) collective-permute-start(f32[1,4,1024]{2,0,1:T(1,128)S(1)} %get-tuple-element.8), channel_id=1, source_target_pairs={{0,1},{1,2},{2,3},{3,4},{4,5},{5,6},{6,7},{7,8},{8,9},{9,10},{10,1... | collective-permute-start | bytes 49160 | tf_op jit(solution)/shard_map/ppermute | solution.py:17
  483.0 6.5 %collective-permute-start.38 = (f32[1,4,1024]{2,0,1:T(1,128)S(1)}, f32[1,4,1024]{2,0,1:T(1,128)S(1)}, u32[]{:S(2)}, u32[]{:S(2)}) collective-permute-start(f32[1,4,1024]{2,0,1:T(1,128)S(1)} %get-tuple-element.7), channel_id=1, source_target_pairs={{1,0},{2,1},{3,2},{4,3},{5,4},{6,5},{7,6},{8,7},{9,8},{10,9},{11,1... | collective-permute-start | bytes 49160 | tf_op jit(solution)/shard_map/ppermute | solution.py:18
  (18 other events, 782.7 us)
where the time goes:
time: 562 us; the launch traced here: 553 us
  blocking collectives  265 us (47%)
  starting transfers between devices  144 us (26%)
  local copies, waits for them, and re-layouts  59.1 us (11%)
  waiting for transfers between devices  41.1 us (7%)
  other arithmetic  30.7 us (5%)
  matrix products  9.99 us (2%)
    unnamed x1, blocking collectives  97.2 us
    all_to_all x4, blocking collectives, lines_along_x(): piece = lax.all_to_all(field, 'px', split_axis=2, concat_axis=0, tiled=True)  96.9 us
    ppermute x20, starting transfers between devices, with_halo(): after = lax.ppermute(initial, axis, down)  89.4 us
    all_to_all x4, blocking collectives, lines_along_x(): return lax.all_to_all(solved, 'px', split_axis=0, concat_axis=2, tiled=True)  70.6 us
    ppermute x20, starting transfers between devices, with_halo(): before = lax.ppermute(last, axis, up)  54.8 us
    ppermute x20, waiting for transfers between devices, with_halo(): after = lax.ppermute(initial, axis, down)  23.5 us
    ppermute x20, waiting for transfers between devices, with_halo(): before = lax.ppermute(last, axis, up)  17.7 us
    unnamed x42, local copies, waits for them, and re-layouts  12.5 us
  transfers between devices with their start and end apart: 40, of which 22 were waited for; matrix products, arithmetic and copies ran while one was open for 3% of the time, Pallas kernels for 0%

commit v1 on v0

v1 whole, which is shorter than its diff:
```python
import functools

import jax
import jax.numpy as jnp
from jax import lax
from jax.experimental import pallas as pl
from jax.experimental.pallas import tpu as pltpu
from jax.sharding import PartitionSpec as P

shift_term = 0.1
highest = lax.Precision.HIGHEST
f32 = jnp.float32

N_PY, N_PX = 16, 32
FX, FZ = 32, 1024
MX, MZ = 16, 512
FH, MH = 8, 4
FE, ME = FX + 2 * FH, MX + 2 * MH


def roll(v, shift, axis):
    return pltpu.roll(v, shift % v.shape[axis], axis)


def dyn(ref, start, size):
    return ref[pl.ds(pl.multiple_of(start, 8), size), :]


def dot(a, b):
    return jnp.dot(a, b, precision=highest, preferred_element_type=f32)


def dot_nt(a, b):
    return lax.dot_general(
        a, b, (((1,), (1,)), ((), ())), precision=highest, preferred_element_type=f32
    )


def iota(shape, axis):
    return lax.broadcasted_iota(jnp.int32, shape, axis)


def near_z(v):
    lane = iota(v.shape, 1)
    last = v.shape[1] - 1
    below = jnp.where(lane == 0, 0.0, roll(v, 1, 1))
    above = jnp.where(lane == last, 0.0, roll(v, -1, 1))
    return below + above


def near_x(v):
    return roll(v, 1, 0) + roll(v, -1, 0)


def operate(v, v_near_x, v_near_y, rho, cx, cy, cz):
    twice = 2.0 * v
    stencil = cx * (twice - v_near_x) + cy * (twice - v_near_y) + cz * (twice - near_z(v))
    return shift_term * v + rho * stencil


def diagonal(rho, cx, cy, cz):
    return shift_term + 2.0 * rho * (cx + cy + cz)


def solve_z(w, blocks):
    count = blocks.shape[0]
    size = blocks.shape[1]
    parts = [dot_nt(w[:, k * size : (k + 1) * size], blocks[k]) for k in range(count)]
    return jnp.concatenate(parts, axis=1)


def pair_columns(v, scale):
    fine, coarse = iota((256, 128), 0), iota((256, 128), 1)
    pick = jnp.where(fine // 2 == coarse, scale, 0.0).astype(f32)
    return jnp.concatenate(
        [dot(v[:, 256 * k : 256 * (k + 1)], pick) for k in range(v.shape[1] // 256)], axis=1
    )


def even_columns(v, scale):
    fine, coarse = iota((256, 128), 0), iota((256, 128), 1)
    pick = jnp.where(fine == 2 * coarse, scale, 0.0).astype(f32)
    return jnp.concatenate(
        [dot(v[:, 256 * k : 256 * (k + 1)], pick) for k in range(v.shape[1] // 256)], axis=1
    )


def restrict_columns(v):
    lane = iota(v.shape, 1)
    last = v.shape[1] - 1
    one = jnp.where(lane == last, 0.0, roll(v, -1, 1))
    two = jnp.where(lane >= last - 1, 0.0, roll(v, -2, 1))
    below = jnp.where(lane == 0, 0.0, roll(v, 1, 1))
    return even_columns(below + 3.0 * v + 3.0 * one + two, 0.125)


def raise_columns(v):
    lane = iota(v.shape, 1)
    last = v.shape[1] - 1
    below = jnp.where(lane == 0, 0.0, roll(v, 1, 1))
    above = jnp.where(lane == last, 0.0, roll(v, -1, 1))
    even = 3.0 * v + below
    odd = 3.0 * v + above
    coarse, fine = iota((128, 256), 0), iota((128, 256), 1)
    at_even = jnp.where(fine == 2 * coarse, 0.25, 0.0).astype(f32)
    at_odd = jnp.where(fine == 2 * coarse + 1, 0.25, 0.0).astype(f32)
    parts = []
    for k in range(v.shape[1] // 128):
        cut = slice(128 * k, 128 * (k + 1))
        parts.append(dot(even[:, cut], at_even) + dot(odd[:, cut], at_odd))
    return jnp.concatenate(parts, axis=1)


def restrict_rows(v):
    coarse, fine = iota((ME, FE), 0), iota((ME, FE), 1)
    away = fine - 2 * coarse
    weight = jnp.where((away == 0) | (away == 1), 0.375, 0.0)
    weight = weight + jnp.where((away == -1) | (away == 2), 0.125, 0.0)
    return dot(weight.astype(f32), v)


def pair_rows(v):
    coarse, fine = iota((ME, FE), 0), iota((ME, FE), 1)
    return dot(jnp.where(fine // 2 == coarse, 1.0, 0.0).astype(f32), v)


def raise_rows(v):
    fine, coarse = iota((FE, ME), 0), iota((FE, ME), 1)
    away = fine - 2 * coarse
    weight = jnp.where((away == 0) | (away == 1), 0.75, 0.0)
    weight = weight + jnp.where((away == 2) | (away == -1), 0.25, 0.0)
    return dot(weight.astype(f32), v)


def inside_middle(px):
    row = iota((ME, MZ), 0) + MX * px - MH
    return (row >= 0) & (row < MX * N_PX)


def inside_fine(px):
    row = iota((FE, FZ), 0) + FX * px - FH
    return (row >= 0) & (row < FX * N_PX)


def to_slabs(plane, out, at):
    for m in range(8):
        out[m, at] = plane[:, 128 * m : 128 * (m + 1)]


def from_slabs(ref, at):
    return jnp.concatenate([ref[m, at] for m in range(8)], axis=1)


def pack_y(px, py, force, rho, cy, lower, upper):
    for at, out in ((0, lower), (1, upper)):
        out[0:32] = force[at]
        out[32:64] = rho[at]
        out[64:72] = cy[8 * at : 8 * at + 8]


def pack_x(px, py, force, rho, cx, below, above, low, high):
    for rows, out in ((slice(0, 8), low), (slice(24, 32), high)):
        shifted = slice(32 + rows.start, 32 + rows.stop)
        out[0:8] = below[rows]
        out[8:16] = force[0, rows]
        out[16:24] = force[1, rows]
        out[24:32] = above[rows]
        out[32:40] = below[shifted]
        out[40:48] = rho[0, rows]
        out[48:56] = rho[1, rows]
        out[56:64] = above[shifted]
        out[64:72] = jnp.concatenate([cx[rows]] * 8, axis=1)


def first_half(px, py, force, rho, cx, cy, cz, below, above, left, right, lines, f_ext, r_ext, cx_ext, cy_ext, u_own, slabs):
    columns = jnp.concatenate([left[64:72, 0:128], cx[...], right[64:72, 0:128]], axis=0)
    cx_ext[...] = columns
    cx_col = columns[:, 0:1]
    cy_rows = [below[64:65, :], None, None, above[64:65, :]]
    cy_rows[1] = jnp.concatenate([cy[0:1]] * 1, axis=1)
    cy_rows[2] = cy[8:9]
    cy_ext[...] = jnp.concatenate(cy_rows + [cy_rows[3]] * 4, axis=0)
    cz_row = cz[0:1]
    mids_f = [below[0:32], force[0], force[1], above[0:32]]
    mids_r = [below[32:64], rho[0], rho[1], above[32:64]]
    us = []
    fs = []
    rs = []
    for j in range(4):
        cut = slice(8 * j, 8 * j + 8)
        deep = slice(32 + 8 * j, 40 + 8 * j)
        f_full = jnp.concatenate([left[cut], mids_f[j], right[cut]], axis=0)
        r_full = jnp.concatenate([left[deep], mids_r[j], right[deep]], axis=0)
        f_ext[j] = f_full
        r_ext[j] = r_full
        fs.append(f_full)
        rs.append(r_full)
        us.append(solve_z(f_full / diagonal(r_full, cx_col, cy_rows[j], cz_row), lines))
    for j in (1, 2):
        own = us[j]
        applied = operate(own, near_x(own), us[j - 1] + us[j + 1], rs[j], cx_col, cy_rows[j], cz_row)
        scaled = (fs[j] - applied) / diagonal(rs[j], cx_col, cy_rows[j], cz_row)
        u_own[j - 1] = own[FH : FH + FX]
        to_slabs(scaled[FH : FH + FX], slabs, j - 1)


def solve_x_fine(px, py, slabs, lines, out):
    block = lines[0]
    for at in range(2):
        column = jnp.concatenate([slabs[m, at] for m in range(8)], axis=0)
        solved = dot(block, column)
        for m in range(8):
            out[m, at] = solved[32 * m : 32 * (m + 1)]


def add_slabs(px, py, u, slabs, out):
    for at in range(2):
        out[at] = u[at] + from_slabs(slabs, at)


def pack_u(px, py, u, below, above, low, high):
    for rows, out in ((slice(0, 8), low), (slice(24, 32), high)):
        for j, part in enumerate((below[0, rows], below[1, rows], u[0, rows], u[1, rows], above[0, rows], above[1, rows])):
            out[8 * j : 8 * j + 8] = part


def to_middle(px, py, u, below, above, left, right, f_ext, r_ext, cx_ext, cy_ext, cz, lines, u_ext, f_mid, v_out, r_mid, cx_mid, cyz_mid):
    mids = [below[0], below[1], u[0], u[1], above[0], above[1]]
    planes = []
    for j in range(6):
        cut = slice(8 * j, 8 * j + 8)
        planes.append(jnp.concatenate([left[cut], mids[j], right[cut]], axis=0))
    cx_col = cx_ext[:, 0:1]
    cz_row = cz[0:1]
    total = None
    for j in range(4):
        own = planes[j + 1]
        u_ext[j] = own
        applied = operate(own, near_x(own), planes[j] + planes[j + 2], r_ext[j], cx_col, cy_ext[j : j + 1], cz_row)
        left_over = f_ext[j] - applied
        if j in (1, 2):
            left_over = 3.0 * left_over
        total = left_over if total is None else total + left_over
    rhs = restrict_columns(restrict_rows(total * 0.125))
    rhs = jnp.where(inside_middle(px), rhs, 0.0)
    dense = pair_columns(pair_rows(r_ext[1] + r_ext[2]), 0.125)
    cxm = pair_rows(cx_ext[...]) * 0.125
    czm = pair_columns(cz[...], 0.125)
    cym = ((cy_ext[1:2] + cy_ext[2:3]) * 0.125)[:, 0:MZ]
    f_mid[...] = rhs
    r_mid[...] = dense
    cx_mid[...] = cxm
    cyz_mid[...] = jnp.concatenate([czm[0:1], cym, czm[2:8]], axis=0)
    diag = diagonal(dense, cxm[:, 0:1], cym, czm[0:1])
    v_out[...] = solve_z(rhs / diag, lines)


def middle_parts(r_mid, cx_mid, cyz_mid):
    return r_mid[...], cx_mid[:, 0:1], cyz_mid[1:2], cyz_mid[0:1]


def middle_scaled(px, py, v, below, above, f_mid, r_mid, cx_mid, cyz_mid, out):
    rho, cx, cy, cz = middle_parts(r_mid, cx_mid, cyz_mid)
    own = v[...]
    applied = operate(own, near_x(own), below[...] + above[...], rho, cx, cy, cz)
    scaled = (f_mid[...] - applied) / diagonal(rho, cx, cy, cz)
    part = roll(scaled, -MH, 0)[0:MX]
    for i in range(N_PX):
        out[i] = part


def solve_x_middle(px, py, gathered, lines, v, out):
    total = MX * N_PX
    pieces = []
    starts = (
        (jnp.maximum(MX * px - 8, 0), 8),
        (MX * px, MX),
        (jnp.minimum(MX * px + MX, total - 8), 8),
    )
    for start, size in starts:
        rows = dyn(lines, start, size)
        block = (start // 256) * 256
        pieces.append(dot(rows, dyn(gathered, block, 256)))
    full = jnp.concatenate(pieces, axis=0)
    part = roll(full, MH - 8, 0)[0:ME]
    out[...] = v[...] + jnp.where(inside_middle(px), part, 0.0)


def block_mean(px, py, v, below, above, f_mid, r_mid, cx_mid, cyz_mid, column, out):
    rho, cx, cy, cz = middle_parts(r_mid, cx_mid, cyz_mid)
    own = v[...]
    applied = operate(own, near_x(own), below[...] + above[...], rho, cx, cy, cz)
    row = iota((ME, MZ), 0)
    kept = jnp.where((row >= MH) & (row < MH + MX), f_mid[...] - applied, 0.0)
    mean = jnp.sum(jnp.sum(kept, axis=0, keepdims=True), axis=1, keepdims=True) * (1.0 / (MX * MZ))
    sent = column[...] * mean
    for i in range(N_PX):
        out[i] = jnp.broadcast_to(sent[i : i + 1], (8, 128))


def sum_x(px, py, parts, out):
    total = parts[0]
    for i in range(1, N_PX):
        total = total + parts[i]
    for j in range(N_PY):
        out[j] = total


def second_half(px, py, parts, v, below, above, f_mid, r_mid, cx_mid, cyz_mid, lines, out):
    total = parts[0]
    for j in range(1, N_PY):
        total = total + parts[j]
    lane = iota((8, 128), 1)
    row = iota((ME, MZ), 0)

    def raised(plane, dy):
        held = (py + dy >= 0) & (py + dy < N_PY)
        at = []
        for dx in range(3):
            wanted = (lane == dx * N_PY + py + dy) & held
            found = jnp.sum(jnp.where(wanted, total, 0.0), axis=1, keepdims=True)[0:1]
            at.append(found)
        return plane + jnp.where(row < MH, at[0], jnp.where(row < MH + MX, at[1], at[2]))

    own = raised(v[...], 0)
    beside = raised(below[...], -1) + raised(above[...], 1)
    rho, cx, cy, cz = middle_parts(r_mid, cx_mid, cyz_mid)
    applied = operate(own, near_x(own), beside, rho, cx, cy, cz)
    out[...] = own + solve_z((f_mid[...] - applied) / diagonal(rho, cx, cy, cz), lines)


def to_fine(px, py, v, below, above, u_ext, f_ext, r_ext, cx_ext, cy_ext, cz, lines, out, lower, upper):
    raised = [raise_columns(raise_rows(p[...])) * 0.25 for p in (below, v, above)]
    mids = [
        3.0 * raised[0] + raised[1],
        3.0 * raised[1] + raised[0],
        3.0 * raised[1] + raised[2],
        3.0 * raised[2] + raised[1],
    ]
    inside = inside_fine(px)
    us = []
    for j in range(4):
        held = inside
        if j == 0:
            held = inside & (py > 0)
        if j == 3:
            held = inside & (py < N_PY - 1)
        us.append(u_ext[j] + jnp.where(held, mids[j], 0.0))
    cx_col = cx_ext[:, 0:1]
    cz_row = cz[0:1]
    for j in (1, 2):
        own = us[j]
        cy_row = cy_ext[j : j + 1]
        rho = r_ext[j]
        applied = operate(own, near_x(own), us[j - 1] + us[j + 1], rho, cx_col, cy_row, cz_row)
        solved = own + solve_z((f_ext[j] - applied) / diagonal(rho, cx_col, cy_row, cz_row), lines)
        out[j - 1] = solved
        (lower if j == 1 else upper)[...] = solved[FH : FH + FX]


def last_scaled(px, py, u, below, above, f_ext, r_ext, cx_ext, cy_ext, cz, slabs):
    cx_col = cx_ext[FH : FH + FX, 0:1]
    cz_row = cz[0:1]
    inner = slice(FH, FH + FX)
    for at in range(2):
        full = u[at]
        beside_x = near_x(full)[inner]
        own = full[inner]
        beside_y = (below[...] if at == 0 else u[0, inner]) + (above[...] if at == 1 else u[1, inner])
        rho = r_ext[at + 1, inner]
        cy_row = cy_ext[at + 1 : at + 2]
        applied = operate(own, beside_x, beside_y, rho, cx_col, cy_row, cz_row)
        scaled = (f_ext[at + 1, inner] - applied) / diagonal(rho, cx_col, cy_row, cz_row)
        to_slabs(scaled, slabs, at)


def finish(px, py, u, slabs, out):
    for at in range(2):
        out[at] = u[at, FH : FH + FX] + from_slabs(slabs, at)


class Device:
    def run(self, stage, shapes, *args):
        def kernel(*refs):
            stage(lax.axis_index("px"), lax.axis_index("py"), *refs)

        whole = pl.BlockSpec(memory_space=pltpu.VMEM)
        outs = pl.pallas_call(
            kernel,
            out_shape=[jax.ShapeDtypeStruct(s, f32) for s in shapes],
            in_specs=[whole] * len(args),
            out_specs=[whole] * len(shapes),
            compiler_params=pltpu.CompilerParams(vmem_limit_bytes=56 * 1024 * 1024),
            name=stage.__name__,
        )(*args)
        return outs if len(shapes) > 1 else outs[0]

    def local(self, fn, *args):
        return fn(*args)

    def block_of(self, lines):
        at = lax.axis_index("px") // 8
        return lax.dynamic_slice_in_dim(lines, at, 1, axis=0)

    def beside(self, axis, low, high):
        n = lax.axis_size(axis)
        up = [(i, i + 1) for i in range(n - 1)]
        down = [(j, i) for i, j in up]
        return lax.ppermute(high, axis, up), lax.ppermute(low, axis, down)

    def swap(self, axis, array, group):
        n = lax.axis_size(axis)
        groups = None
        if group < n:
            groups = [list(range(k, k + group)) for k in range(0, n, group)]
        return lax.all_to_all(array, axis, 0, 0, axis_index_groups=groups, tiled=True)


def arrange_column(coarse):
    table = coarse.reshape(N_PY, N_PX).T
    none = jnp.zeros((1, N_PY), f32)
    before = jnp.concatenate([none, table[:-1]], axis=0)
    after = jnp.concatenate([table[1:], none], axis=0)
    return jnp.concatenate([before, table, after, jnp.zeros((N_PX, 128 - 3 * N_PY), f32)], axis=1)


def prepare(forcing, inv_density, stretch_x, stretch_y, stretch_z, coarse_inverse):
    force = forcing.transpose(1, 0, 2)
    rho = inv_density.transpose(1, 0, 2)
    cx = jnp.broadcast_to(stretch_x[:, None], (FX, 128))
    cy = jnp.repeat(jnp.broadcast_to(stretch_y[:, None], (2, FZ)), 8, axis=0)
    cz = jnp.broadcast_to(stretch_z[None], (8, FZ))
    return force, rho, cx, cy, cz, arrange_column(coarse_inverse)


def cycle(d, forcing, inv_density, stretch_x, stretch_y, stretch_z, lines_z0, lines_x0, lines_z1, lines_x1, coarse_inverse):
    force, rho, cx, cy, cz, column = d.local(
        prepare, forcing, inv_density, stretch_x, stretch_y, stretch_z, coarse_inverse
    )
    block = d.block_of(lines_x0)
    rows_x1 = d.local(lambda a: a.reshape(MX * N_PX, 256), lines_x1)
    plane, slab, wide = (72, FZ), (8, 2, FX, 128), (4, FE, FZ)

    lower, upper = d.run(pack_y, [plane] * 2, force, rho, cy)
    below, above = d.beside("py", lower, upper)
    low, high = d.run(pack_x, [plane] * 2, force, rho, cx, below, above)
    left, right = d.beside("px", low, high)
    f_ext, r_ext, cx_ext, cy_ext, u, slabs = d.run(
        first_half,
        [wide, wide, (FE, 128), (8, FZ), (2, FX, FZ), slab],
        force, rho, cx, cy, cz, below, above, left, right, lines_z0,
    )
    slabs = d.swap("px", slabs, 8)
    slabs = d.run(solve_x_fine, [slab], slabs, block)
    slabs = d.swap("px", slabs, 8)
    u = d.run(add_slabs, [(2, FX, FZ)], u, slabs)
    below, above = d.beside("py", u, u)
    low, high = d.run(pack_u, [(48, FZ)] * 2, u, below, above)
    left, right = d.beside("px", low, high)
    mid = (ME, MZ)
    u_ext, f_mid, v, r_mid, cx_mid, cyz_mid = d.run(
        to_middle,
        [wide, mid, mid, mid, (ME, 128), (8, MZ)],
        u, below, above, left, right, f_ext, r_ext, cx_ext, cy_ext, cz, lines_z1,
    )
    statics = (f_mid, r_mid, cx_mid, cyz_mid)

    below, above = d.beside("py", v, v)
    every = d.run(middle_scaled, [(N_PX, MX, MZ)], v, below, above, *statics)
    every = d.swap("px", every, N_PX)
    every = d.local(lambda a: a.reshape(MX * N_PX, MZ), every)
    v = d.run(solve_x_middle, [mid], every, rows_x1, v)
    below, above = d.beside("py", v, v)
    sent = d.run(block_mean, [(N_PX, 8, 128)], v, below, above, *statics, column)
    parts = d.swap("px", sent, N_PX)
    parts = d.run(sum_x, [(N_PY, 8, 128)], parts)
    parts = d.swap("py", parts, N_PY)
    v = d.run(second_half, [mid], parts, v, below, above, *statics, lines_z1)
    below, above = d.beside("py", v, v)
    every = d.run(middle_scaled, [(N_PX, MX, MZ)], v, below, above, *statics)
    every = d.swap("px", every, N_PX)
    every = d.local(lambda a: a.reshape(MX * N_PX, MZ), every)
    v = d.run(solve_x_middle, [mid], every, rows_x1, v)

    below, above = d.beside("py", v, v)
    u, lower, upper = d.run(
        to_fine,
        [(2, FE, FZ), (FX, FZ), (FX, FZ)],
        v, below, above, u_ext, f_ext, r_ext, cx_ext, cy_ext, cz, lines_z0,
    )
    below, above = d.beside("py", lower, upper)
    slabs = d.run(last_scaled, [slab], u, below, above, f_ext, r_ext, cx_ext, cy_ext, cz)
    slabs = d.swap("px", slabs, 8)
    slabs = d.run(solve_x_fine, [slab], slabs, block)
    slabs = d.swap("px", slabs, 8)
    u = d.run(finish, [(2, FX, FZ)], u, slabs)
    return d.local(lambda a: a.transpose(1, 0, 2), u)


def solution(mesh):
    placed = (
        P("px", "py", None),
        P("px", "py", None),
        P("px"),
        P("py"),
        P(),
        P(),
        P(),
        P(),
        P(),
        P(("py", "px"), None),
    )
    return jax.shard_map(
        functools.partial(cycle, Device()),
        mesh=mesh,
        in_specs=placed,
        out_specs=P("px", "py", None),
        check_vma=False,
    )
```

time: 562 us -> 344 us (0.61)
  the two profiles are of different devices: /device:TPU:72 before, /device:TPU:4 now
where the time goes in v1:
time: 344 us; the launch traced here: 342 us
  blocking collectives  110 us (32%)
  waiting for transfers between devices  92.6 us (27%)
  starting transfers between devices  72.7 us (21%)
  Pallas kernels  51 us (15%)
  local copies, waits for them, and re-layouts  14.6 us (4%)
    all_to_all x6, blocking collectives, swap(): lax.all_to_all(array, axis, 0, 0, axis_index_groups=groups, tiled=True)  110 us
    ppermute x18, starting transfers between devices, beside(): return (lax.ppermute(high, axis, up), lax.ppermute(low, axis, down))  57.7 us
    ppermute x18, waiting for transfers between devices, beside(): return (lax.ppermute(high, axis, up), lax.ppermute(low, axis, down))  55.6 us
    pallas_call x18, Pallas kernels, run(): pl.pallas_call(kernel, out_shape=[jax.ShapeDtypeStruct(s, f32) for s in s...  51 us
    all_to_all x2, waiting for transfers between devices, swap(): lax.all_to_all(array, axis, 0, 0, axis_index_groups=groups, tiled=True)  37 us
    all_to_all x2, starting transfers between devices, swap(): lax.all_to_all(array, axis, 0, 0, axis_index_groups=groups, tiled=True)  14.9 us
  transfers between devices with their start and end apart: 20, of which 16 were waited for; matrix products, arithmetic and copies ran while one was open for 1% of the time, Pallas kernels for 0%

profile of v1, /device:TPU:4, one launch (start us, length us, event | category | flops | bytes accessed | tf_op | source)
XLA Modules:
  0.0 342.2 jit_solution(767593731029997169)
XLA Ops:
  7.5 4.5 %collective-permute-start.1 = (f32[72,1024]{1,0:T(8,128)}, f32[72,1024]{1,0:T(8,128)S(1)}, u32[]{:S(2)}, u32[]{:S(2)}) collective-permute-start(f32[72,1024]{1,0:T(8,128)} %get-tuple-element.27), channel_id=1, source_target_pairs={{32,0},{64,32},{96,64},{128,96},{160,128},{192,160},{224,192},{256... | collective-permute-start | bytes 884744 | tf_op jit(solution)/shard_map/ppermute | solution.py:409
  12.1 2.7 collective-permute-done.refs_3_.refs_5_
  19.8 6.1 %collective-permute-start.2 = (f32[72,1024]{1,0:T(8,128)}, f32[72,1024]{1,0:T(8,128)S(1)}, u32[]{:S(2)}, u32[]{:S(2)}) collective-permute-start(f32[72,1024]{1,0:T(8,128)} %get-tuple-element.28), channel_id=1, source_target_pairs={{0,1},{1,2},{2,3},{3,4},{4,5},{5,6},{6,7},{7,8},{8,9},{9,10},{10,1... | collective-permute-start | bytes 884744 | tf_op jit(solution)/shard_map/ppermute | solution.py:409
  27.2 6.1 %collective-permute-done.2.refs_7_ = f32[72,1024]{1,0:T(8,128)S(1)} collective-permute-done((f32[72,1024]{1,0:T(8,128)}, f32[72,1024]{1,0:T(8,128)S(1)}, u32[]{:S(2)}, u32[]{:S(2)}) %collective-permute-start.2) | collective-permute-done | bytes 294944 | tf_op jit(solution)/shard_map/ppermute | solution.py:409
  33.4 15.2 %collective-permute-done.3.refs_8_ = f32[72,1024]{1,0:T(8,128)S(1)} collective-permute-done((f32[72,1024]{1,0:T(8,128)}, f32[72,1024]{1,0:T(8,128)S(1)}, u32[]{:S(2)}, u32[]{:S(2)}) %collective-permute-start.3) | collective-permute-done | bytes 294944 | tf_op jit(solution)/shard_map/ppermute | solution.py:409
  49.3 6.6 %first_half.1 = (f32[4,48,1024]{2,1,0:T(8,128)}, f32[4,48,1024]{2,1,0:T(8,128)}, f32[48,128]{1,0:T(8,128)}, f32[8,1024]{1,0:T(8,128)}, f32[2,32,1024]{2,1,0:T(8,128)}, /*index=5*/f32[8,2,32,128]{3,2,1,0:T(8,128)}) custom-call(f32[2,32,1024]{2,1,0:T(8,128)} %get-tuple-element.50.refs_0_, f32[2,32,1024]{2,1,0:T(8,128)} %get-tuple-element.49.refs_1_, ...), custom_call_target="tpu_custom_call" | custom-call | tf_op jit(solution)/shard_map/first_half/pallas_call | solution.py:388
  55.9 5.3 %all-to-all-start = ((f32[8,2,32,128]{3,2,1,0:T(8,128)}), f32[8,2,32,128]{3,2,1,0:T(8,128)S(1)}, u32[]{:S(2)}, u32[]{:S(2)}) async-start(f32[8,2,32,128]{3,2,1,0:T(8,128)} %get-tuple-element.31), calls=%async_computation | async-start | bytes 524288 | tf_op jit(solution)/shard_map/all_to_all | solution.py:416
  61.9 10.0 %all-to-all-done.refs_0_ = f32[8,2,32,128]{3,2,1,0:T(8,128)S(1)} async-done(((f32[8,2,32,128]{3,2,1,0:T(8,128)}), f32[8,2,32,128]{3,2,1,0:T(8,128)S(1)}, u32[]{:S(2)}, u32[]{:S(2)}) %all-to-all-start) | async-done | bytes 262176 | tf_op jit(solution)/shard_map/all_to_all | solution.py:416
  72.6 2.3 solve_x_fine.2
  74.9 13.6 %all_to_all.40.refs_1_ = f32[8,2,32,128]{3,2,1,0:T(8,128)} all-to-all(f32[8,2,32,128]{3,2,1,0:T(8,128)} %solve_x_fine.2), channel_id=1, replica_groups={{0,1,2,3,4,5,6,7},{8,9,10,11,12,13,14,15},{16,17,18,19,20,21,22,23},{24..., dimensions={0} | all-to-all | bytes 524288 | tf_op jit(solution)/shard_map/all_to_all | solution.py:416
  92.1 4.5 %collective-permute-start.5 = (f32[2,32,1024]{2,1,0:T(8,128)}, f32[2,32,1024]{2,1,0:T(8,128)S(1)}, u32[]{:S(2)}, u32[]{:S(2)}) collective-permute-start(f32[2,32,1024]{2,1,0:T(8,128)} %add_slabs.1.refs_0_), channel_id=1, source_target_pairs={{32,0},{64,32},{96,64},{128,96},{160,128},{192,160},{224,192},{256... | collective-permute-start | bytes 786440 | tf_op jit(solution)/shard_map/ppermute | solution.py:409
  103.5 3.8 %collective-permute-start.6 = (f32[48,1024]{1,0:T(8,128)}, f32[48,1024]{1,0:T(8,128)S(1)}, u32[]{:S(2)}, u32[]{:S(2)}) collective-permute-start(f32[48,1024]{1,0:T(8,128)} %get-tuple-element.32), channel_id=1, source_target_pairs={{0,1},{1,2},{2,3},{3,4},{4,5},{5,6},{6,7},{7,8},{8,9},{9,10},{10,1... | collective-permute-start | bytes 589832 | tf_op jit(solution)/shard_map/ppermute | solution.py:409
  108.6 3.6 %collective-permute-done.6.refs_3_ = f32[48,1024]{1,0:T(8,128)S(1)} collective-permute-done((f32[48,1024]{1,0:T(8,128)}, f32[48,1024]{1,0:T(8,128)S(1)}, u32[]{:S(2)}, u32[]{:S(2)}) %collective-permute-start.6) | collective-permute-done | bytes 196640 | tf_op jit(solution)/shard_map/ppermute | solution.py:409
  112.2 11.2 %collective-permute-done.7.refs_4_ = f32[48,1024]{1,0:T(8,128)S(1)} collective-permute-done((f32[48,1024]{1,0:T(8,128)}, f32[48,1024]{1,0:T(8,128)S(1)}, u32[]{:S(2)}, u32[]{:S(2)}) %collective-permute-start.7) | collective-permute-done | bytes 196640 | tf_op jit(solution)/shard_map/ppermute | solution.py:409
  124.0 4.9 %to_middle.1 = (f32[4,48,1024]{2,1,0:T(8,128)}, f32[24,512]{1,0:T(8,128)}, f32[24,512]{1,0:T(8,128)}, f32[24,512]{1,0:T(8,128)}, f32[24,128]{1,0:T(8,128)}, /*index=5*/f32[8,512]{1,0:T(8,128)}) custom-call(f32[2,32,1024]{2,1,0:T(8,128)} %add_slabs.1.refs_0_, f32[2,32,1024]{2,1,0:T(8,128)} %copy-done.4, f32[2,32,1024]{2,1,0:T(8,128)} %copy-done.5, ...), custom_call_target="tpu_custom_call" | custom-call | tf_op jit(solution)/shard_map/to_middle/pallas_call | solution.py:388
  130.9 4.5 %collective-permute-start.9 = (f32[24,512]{1,0:T(8,128)}, f32[24,512]{1,0:T(8,128)S(1)}, u32[]{:S(2)}, u32[]{:S(2)}) collective-permute-start(f32[24,512]{1,0:T(8,128)} %get-tuple-element.38.refs_0_.refs_2_), channel_id=1, source_target_pairs={{32,0},{64,32},{96,64},{128,96},{160,128},{192,160},{224,192},{256... | collective-permute-start | bytes 147464 | tf_op jit(solution)/shard_map/ppermute | solution.py:409
  140.2 9.7 %all-to-all-start.2 = ((f32[32,16,512]{2,1,0:T(8,128)}), f32[32,16,512]{2,1,0:T(8,128)S(1)}, u32[]{:S(2)}, u32[]{:S(2)}) async-start(f32[32,16,512]{2,1,0:T(8,128)} %middle_scaled.2), calls=%async_computation.2 | async-start | bytes 2097152 | tf_op jit(solution)/shard_map/all_to_all | solution.py:416
  151.3 27.0 %all-to-all-done.2 = f32[32,16,512]{2,1,0:T(8,128)S(1)} async-done(((f32[32,16,512]{2,1,0:T(8,128)}), f32[32,16,512]{2,1,0:T(8,128)S(1)}, u32[]{:S(2)}, u32[]{:S(2)}) %all-to-all-start.2) | async-done | bytes 1048608 | tf_op jit(solution)/shard_map/all_to_all | solution.py:416
  179.3 2.8 solve_x_middle.2.refs_0_.refs_1_
  184.0 4.5 %collective-permute-start.11 = (f32[24,512]{1,0:T(8,128)}, f32[24,512]{1,0:T(8,128)S(1)}, u32[]{:S(2)}, u32[]{:S(2)}) collective-permute-start(f32[24,512]{1,0:T(8,128)} %solve_x_middle.2.refs_0_.refs_1_), channel_id=1, source_target_pairs={{32,0},{64,32},{96,64},{128,96},{160,128},{192,160},{224,192},{256... | collective-permute-start | bytes 147464 | tf_op jit(solution)/shard_map/ppermute | solution.py:409
  193.0 19.1 %all_to_all.41.refs_0_ = f32[32,8,128]{2,1,0:T(8,128)} all-to-all(f32[32,8,128]{2,1,0:T(8,128)} %block_mean.1), channel_id=1, replica_groups=mesh['py'=16,'px'=32] {'px'}, dimensions={0} | all-to-all | bytes 262144 | tf_op jit(solution)/shard_map/all_to_all | solution.py:416
  213.7 9.7 %all_to_all.42.refs_0_ = f32[16,8,128]{2,1,0:T(8,128)} all-to-all(f32[16,8,128]{2,1,0:T(8,128)} %sum_x.1), channel_id=1, replica_groups=mesh['py'=16,'px'=32] {'py'}, dimensions={0} | all-to-all | bytes 131072 | tf_op jit(solution)/shard_map/all_to_all | solution.py:416
  223.5 2.5 second_half.1.refs_0_.refs_2_
  228.0 4.4 %collective-permute-start.13 = (f32[24,512]{1,0:T(8,128)}, f32[24,512]{1,0:T(8,128)S(1)}, u32[]{:S(2)}, u32[]{:S(2)}) collective-permute-start(f32[24,512]{1,0:T(8,128)} %second_half.1.refs_0_.refs_2_), channel_id=1, source_target_pairs={{32,0},{64,32},{96,64},{128,96},{160,128},{192,160},{224,192},{256... | collective-permute-start | bytes 147464 | tf_op jit(solution)/shard_map/ppermute | solution.py:409
  237.2 34.1 %all_to_all.43 = f32[32,16,512]{2,1,0:T(8,128)} all-to-all(f32[32,16,512]{2,1,0:T(8,128)} %middle_scaled.3), channel_id=1, replica_groups=mesh['py'=16,'px'=32] {'px'}, dimensions={0} | all-to-all | bytes 2097152 | tf_op jit(solution)/shard_map/all_to_all | solution.py:416
  271.4 2.8 solve_x_middle.3.refs_0_
  276.1 4.5 %collective-permute-start.15 = (f32[24,512]{1,0:T(8,128)}, f32[24,512]{1,0:T(8,128)S(1)}, u32[]{:S(2)}, u32[]{:S(2)}) collective-permute-start(f32[24,512]{1,0:T(8,128)} %solve_x_middle.3.refs_0_), channel_id=1, source_target_pairs={{32,0},{64,32},{96,64},{128,96},{160,128},{192,160},{224,192},{256... | collective-permute-start | bytes 147464 | tf_op jit(solution)/shard_map/ppermute | solution.py:409
  283.3 7.1 %to_fine.1 = (f32[2,48,1024]{2,1,0:T(8,128)}, f32[32,1024]{1,0:T(8,128)}, f32[32,1024]{1,0:T(8,128)}) custom-call(f32[24,512]{1,0:T(8,128)} %solve_x_middle.3.refs_0_, f32[24,512]{1,0:T(8,128)} %copy-done.15, f32[24,512]{1,0:T(8,128)} %copy-done.16, f32[4,48,1024]{2,1,0:T(8,128)} %get-tuple-element.43.refs_3_, ...), custom_call_target="tpu_custom_call" | custom-call | tf_op jit(solution)/shard_map/to_fine/pallas_call | solution.py:388
  292.3 4.5 %collective-permute-start.17 = (f32[32,1024]{1,0:T(8,128)}, f32[32,1024]{1,0:T(8,128)S(1)}, u32[]{:S(2)}, u32[]{:S(2)}) collective-permute-start(f32[32,1024]{1,0:T(8,128)} %get-tuple-element.46), channel_id=1, source_target_pairs={{32,0},{64,32},{96,64},{128,96},{160,128},{192,160},{224,192},{256... | collective-permute-start | bytes 393224 | tf_op jit(solution)/shard_map/ppermute | solution.py:409
  300.3 2.6 last_scaled.1
  303.0 18.0 %all_to_all.44.refs_0_ = f32[8,2,32,128]{3,2,1,0:T(8,128)} all-to-all(f32[8,2,32,128]{3,2,1,0:T(8,128)} %last_scaled.1), channel_id=1, replica_groups={{0,1,2,3,4,5,6,7},{8,9,10,11,12,13,14,15},{16,17,18,19,20,21,22,23},{24..., dimensions={0} | all-to-all | bytes 524288 | tf_op jit(solution)/shard_map/all_to_all | solution.py:416
  323.3 15.3 %all_to_all.45.refs_1_ = f32[8,2,32,128]{3,2,1,0:T(8,128)} all-to-all(f32[8,2,32,128]{3,2,1,0:T(8,128)} %solve_x_fine.3), channel_id=1, replica_groups={{0,1,2,3,4,5,6,7},{8,9,10,11,12,13,14,15},{16,17,18,19,20,21,22,23},{24..., dimensions={0} | all-to-all | bytes 524288 | tf_op jit(solution)/shard_map/all_to_all | solution.py:416
  (96 shorter events, 68.1 us)
Async XLA Ops:
  0.0 61.2 %copy-start = (f32[4,256,256]{2,1,0:T(8,128)S(1)}, f32[4,256,256]{2,1,0:T(8,128)}, u32[]{:S(2)}) copy-start(f32[4,256,256]{2,1,0:T(8,128)} %param.16) | copy-start | bytes 3145732
  5.5 11.5 %copy-start.23 = (f32[32]{0:T(128)S(1)}, f32[32]{0:T(128)}, u32[]{:S(2)}) copy-start(f32[32]{0:T(128)} %param.12) | copy-start | bytes 388
  5.5 9.3 %collective-permute-start = (f32[72,1024]{1,0:T(8,128)}, f32[72,1024]{1,0:T(8,128)S(1)}, u32[]{:S(2)}, u32[]{:S(2)}) collective-permute-start(f32[72,1024]{1,0:T(8,128)} %get-tuple-element.26), channel_id=1, source_target_pairs={{0,32},{32,64},{64,96},{96,128},{128,160},{160,192},{192,224},{224... | collective-permute-start | bytes 884744 | tf_op jit(solution)/shard_map/ppermute | solution.py:409
  7.5 9.5 %collective-permute-start.1 = (f32[72,1024]{1,0:T(8,128)}, f32[72,1024]{1,0:T(8,128)S(1)}, u32[]{:S(2)}, u32[]{:S(2)}) collective-permute-start(f32[72,1024]{1,0:T(8,128)} %get-tuple-element.27), channel_id=1, source_target_pairs={{32,0},{64,32},{96,64},{128,96},{160,128},{192,160},{224,192},{256... | collective-permute-start | bytes 884744 | tf_op jit(solution)/shard_map/ppermute | solution.py:409
  14.7 3.0 copy-start.2
  17.7 30.9 %copy-start.21 = (f32[1024]{0:T(1024)S(1)}, f32[1024]{0:T(1024)}, u32[]{:S(2)}) copy-start(f32[1024]{0:T(1024)} %param.14) | copy-start | bytes 12292
  19.8 13.5 %collective-permute-start.2 = (f32[72,1024]{1,0:T(8,128)}, f32[72,1024]{1,0:T(8,128)S(1)}, u32[]{:S(2)}, u32[]{:S(2)}) collective-permute-start(f32[72,1024]{1,0:T(8,128)} %get-tuple-element.28), channel_id=1, source_target_pairs={{0,1},{1,2},{2,3},{3,4},{4,5},{5,6},{6,7},{7,8},{8,9},{9,10},{10,1... | collective-permute-start | bytes 884744 | tf_op jit(solution)/shard_map/ppermute | solution.py:409
  25.9 22.7 %collective-permute-start.3 = (f32[72,1024]{1,0:T(8,128)}, f32[72,1024]{1,0:T(8,128)S(1)}, u32[]{:S(2)}, u32[]{:S(2)}) collective-permute-start(f32[72,1024]{1,0:T(8,128)} %get-tuple-element.29), channel_id=1, source_target_pairs={{1,0},{2,1},{3,2},{4,3},{5,4},{6,5},{7,6},{8,7},{9,8},{10,9},{11,1... | collective-permute-start | bytes 884744 | tf_op jit(solution)/shard_map/ppermute | solution.py:409
  33.4 15.9 %copy-start.7 = (f32[72,1024]{1,0:T(8,128)}, f32[72,1024]{1,0:T(8,128)S(1)}, u32[]{:S(2)}) copy-start(f32[72,1024]{1,0:T(8,128)S(1)} %collective-permute-done.2.refs_7_) | copy-start | bytes 884740
  55.9 16.0 %all-to-all-start = ((f32[8,2,32,128]{3,2,1,0:T(8,128)}), f32[8,2,32,128]{3,2,1,0:T(8,128)S(1)}, u32[]{:S(2)}, u32[]{:S(2)}) async-start(f32[8,2,32,128]{3,2,1,0:T(8,128)} %get-tuple-element.31), calls=%async_computation | async-start | bytes 524288 | tf_op jit(solution)/shard_map/all_to_all | solution.py:416
  90.2 8.8 %collective-permute-start.4 = (f32[2,32,1024]{2,1,0:T(8,128)}, f32[2,32,1024]{2,1,0:T(8,128)S(1)}, u32[]{:S(2)}, u32[]{:S(2)}) collective-permute-start(f32[2,32,1024]{2,1,0:T(8,128)} %add_slabs.1.refs_0_), channel_id=1, source_target_pairs={{0,32},{32,64},{64,96},{96,128},{128,160},{160,192},{192,224},{224... | collective-permute-start | bytes 786440 | tf_op jit(solution)/shard_map/ppermute | solution.py:409
  92.1 8.8 %collective-permute-start.5 = (f32[2,32,1024]{2,1,0:T(8,128)}, f32[2,32,1024]{2,1,0:T(8,128)S(1)}, u32[]{:S(2)}, u32[]{:S(2)}) collective-permute-start(f32[2,32,1024]{2,1,0:T(8,128)} %add_slabs.1.refs_0_), channel_id=1, source_target_pairs={{32,0},{64,32},{96,64},{128,96},{160,128},{192,160},{224,192},{256... | collective-permute-start | bytes 786440 | tf_op jit(solution)/shard_map/ppermute | solution.py:409
  99.0 1.9 copy-start.4
  103.5 8.7 %collective-permute-start.6 = (f32[48,1024]{1,0:T(8,128)}, f32[48,1024]{1,0:T(8,128)S(1)}, u32[]{:S(2)}, u32[]{:S(2)}) collective-permute-start(f32[48,1024]{1,0:T(8,128)} %get-tuple-element.32), channel_id=1, source_target_pairs={{0,1},{1,2},{2,3},{3,4},{4,5},{5,6},{6,7},{7,8},{8,9},{9,10},{10,1... | collective-permute-start | bytes 589832 | tf_op jit(solution)/shard_map/ppermute | solution.py:409
  107.3 16.1 %collective-permute-start.7 = (f32[48,1024]{1,0:T(8,128)}, f32[48,1024]{1,0:T(8,128)S(1)}, u32[]{:S(2)}, u32[]{:S(2)}) collective-permute-start(f32[48,1024]{1,0:T(8,128)} %get-tuple-element.33), channel_id=1, source_target_pairs={{1,0},{2,1},{3,2},{4,3},{5,4},{6,5},{7,6},{8,7},{9,8},{10,9},{11,1... | collective-permute-start | bytes 589832 | tf_op jit(solution)/shard_map/ppermute | solution.py:409
  112.2 11.2 %copy-start.11 = (f32[48,1024]{1,0:T(8,128)}, f32[48,1024]{1,0:T(8,128)S(1)}, u32[]{:S(2)}) copy-start(f32[48,1024]{1,0:T(8,128)S(1)} %collective-permute-done.6.refs_3_) | copy-start | bytes 589828
  129.0 6.5 %collective-permute-start.8 = (f32[24,512]{1,0:T(8,128)}, f32[24,512]{1,0:T(8,128)S(1)}, u32[]{:S(2)}, u32[]{:S(2)}) collective-permute-start(f32[24,512]{1,0:T(8,128)} %get-tuple-element.38.refs_0_.refs_2_), channel_id=1, source_target_pairs={{0,32},{32,64},{64,96},{96,128},{128,160},{160,192},{192,224},{224... | collective-permute-start | bytes 147464 | tf_op jit(solution)/shard_map/ppermute | solution.py:409
  130.9 6.6 %collective-permute-start.9 = (f32[24,512]{1,0:T(8,128)}, f32[24,512]{1,0:T(8,128)S(1)}, u32[]{:S(2)}, u32[]{:S(2)}) collective-permute-start(f32[24,512]{1,0:T(8,128)} %get-tuple-element.38.refs_0_.refs_2_), channel_id=1, source_target_pairs={{32,0},{64,32},{96,64},{128,96},{160,128},{192,160},{224,192},{256... | collective-permute-start | bytes 147464 | tf_op jit(solution)/shard_map/ppermute | solution.py:409
  135.5 2.0 copy-start.19
  140.2 10.2 %copy-start.22 = (f32[1,512]{1,0:T(1,128)S(1)}, f32[1,512]{1,0:T(1,128)}, u32[]{:S(2)}) copy-start(f32[1,512]{1,0:T(1,128)} %param.19) | copy-start | bytes 6148
  140.2 38.1 %all-to-all-start.2 = ((f32[32,16,512]{2,1,0:T(8,128)}), f32[32,16,512]{2,1,0:T(8,128)S(1)}, u32[]{:S(2)}, u32[]{:S(2)}) async-start(f32[32,16,512]{2,1,0:T(8,128)} %middle_scaled.2), calls=%async_computation.2 | async-start | bytes 2097152 | tf_op jit(solution)/shard_map/all_to_all | solution.py:416
  182.1 7.1 %collective-permute-start.10 = (f32[24,512]{1,0:T(8,128)}, f32[24,512]{1,0:T(8,128)S(1)}, u32[]{:S(2)}, u32[]{:S(2)}) collective-permute-start(f32[24,512]{1,0:T(8,128)} %solve_x_middle.2.refs_0_.refs_1_), channel_id=1, source_target_pairs={{0,32},{32,64},{64,96},{96,128},{128,160},{160,192},{192,224},{224... | collective-permute-start | bytes 147464 | tf_op jit(solution)/shard_map/ppermute | solution.py:409
  184.0 6.6 %collective-permute-start.11 = (f32[24,512]{1,0:T(8,128)}, f32[24,512]{1,0:T(8,128)S(1)}, u32[]{:S(2)}, u32[]{:S(2)}) collective-permute-start(f32[24,512]{1,0:T(8,128)} %solve_x_middle.2.refs_0_.refs_1_), channel_id=1, source_target_pairs={{32,0},{64,32},{96,64},{128,96},{160,128},{192,160},{224,192},{256... | collective-permute-start | bytes 147464 | tf_op jit(solution)/shard_map/ppermute | solution.py:409
  226.0 6.5 %collective-permute-start.12 = (f32[24,512]{1,0:T(8,128)}, f32[24,512]{1,0:T(8,128)S(1)}, u32[]{:S(2)}, u32[]{:S(2)}) collective-permute-start(f32[24,512]{1,0:T(8,128)} %second_half.1.refs_0_.refs_2_), channel_id=1, source_target_pairs={{0,32},{32,64},{64,96},{96,128},{128,160},{160,192},{192,224},{224... | collective-permute-start | bytes 147464 | tf_op jit(solution)/shard_map/ppermute | solution.py:409
  228.0 6.5 %collective-permute-start.13 = (f32[24,512]{1,0:T(8,128)}, f32[24,512]{1,0:T(8,128)S(1)}, u32[]{:S(2)}, u32[]{:S(2)}) collective-permute-start(f32[24,512]{1,0:T(8,128)} %second_half.1.refs_0_.refs_2_), channel_id=1, source_target_pairs={{32,0},{64,32},{96,64},{128,96},{160,128},{192,160},{224,192},{256... | collective-permute-start | bytes 147464 | tf_op jit(solution)/shard_map/ppermute | solution.py:409
  232.5 2.0 copy-start.17
  274.2 6.5 %collective-permute-start.14 = (f32[24,512]{1,0:T(8,128)}, f32[24,512]{1,0:T(8,128)S(1)}, u32[]{:S(2)}, u32[]{:S(2)}) collective-permute-start(f32[24,512]{1,0:T(8,128)} %solve_x_middle.3.refs_0_), channel_id=1, source_target_pairs={{0,32},{32,64},{64,96},{96,128},{128,160},{160,192},{192,224},{224... | collective-permute-start | bytes 147464 | tf_op jit(solution)/shard_map/ppermute | solution.py:409
  276.1 6.6 %collective-permute-start.15 = (f32[24,512]{1,0:T(8,128)}, f32[24,512]{1,0:T(8,128)S(1)}, u32[]{:S(2)}, u32[]{:S(2)}) collective-permute-start(f32[24,512]{1,0:T(8,128)} %solve_x_middle.3.refs_0_), channel_id=1, source_target_pairs={{32,0},{64,32},{96,64},{128,96},{160,128},{192,160},{224,192},{256... | collective-permute-start | bytes 147464 | tf_op jit(solution)/shard_map/ppermute | solution.py:409
  280.7 2.0 copy-start.15
  290.4 7.4 %collective-permute-start.16 = (f32[32,1024]{1,0:T(8,128)}, f32[32,1024]{1,0:T(8,128)S(1)}, u32[]{:S(2)}, u32[]{:S(2)}) collective-permute-start(f32[32,1024]{1,0:T(8,128)} %get-tuple-element.45), channel_id=1, source_target_pairs={{0,32},{32,64},{64,96},{96,128},{128,160},{160,192},{192,224},{224... | collective-permute-start | bytes 393224 | tf_op jit(solution)/shard_map/ppermute | solution.py:409
  292.3 7.4 %collective-permute-start.17 = (f32[32,1024]{1,0:T(8,128)}, f32[32,1024]{1,0:T(8,128)S(1)}, u32[]{:S(2)}, u32[]{:S(2)}) collective-permute-start(f32[32,1024]{1,0:T(8,128)} %get-tuple-element.46), channel_id=1, source_target_pairs={{32,0},{64,32},{96,64},{128,96},{160,128},{192,160},{224,192},{256... | collective-permute-start | bytes 393224 | tf_op jit(solution)/shard_map/ppermute | solution.py:409
  297.8 1.9 copy-start.13
  (12 other events, 9.0 us)

commit v2 on v1

v2 whole, which is shorter than its diff:
```python
import functools

import jax
import jax.numpy as jnp
from jax import lax
from jax.experimental import pallas as pl
from jax.experimental.pallas import tpu as pltpu
from jax.sharding import PartitionSpec as P

shift_term = 0.1
f32 = jnp.float32
bf16 = jnp.bfloat16

N_PY, N_PX = 16, 32
FX, FZ = 32, 1024
MX, MZ = 16, 512
FH, MH = 8, 4
FE, ME = FX + 2 * FH, MX + 2 * MH


def roll(v, shift, axis):
    return pltpu.roll(v, shift % v.shape[axis], axis)


def dyn(ref, start, size):
    return ref[pl.ds(pl.multiple_of(start, 8), size), :]


def halves(a):
    high = a.astype(bf16)
    return high, (a - high.astype(f32)).astype(bf16)


def thirds(a):
    high, rest = a.astype(bf16), None
    rest = a - high.astype(f32)
    middle = rest.astype(bf16)
    return high, middle, (rest - middle.astype(f32)).astype(bf16)


def product(a, b, dims):
    return lax.dot_general(a, b, (dims, ((), ())), preferred_element_type=f32)


def dot(a, b, dims=((1,), (0,))):
    a_high, a_low = halves(a)
    b_high, b_low = halves(b)
    return product(a_high, b_high, dims) + (product(a_high, b_low, dims) + product(a_low, b_high, dims))


def pick_right(a, weight):
    dims = ((1,), (0,))
    w = weight.astype(bf16)
    high, middle, low = thirds(a)
    return product(high, w, dims) + (product(middle, w, dims) + product(low, w, dims))


def pick_left(weight, a):
    dims = ((1,), (0,))
    w = weight.astype(bf16)
    high, middle, low = thirds(a)
    return product(w, high, dims) + (product(w, middle, dims) + product(w, low, dims))


def iota(shape, axis):
    return lax.broadcasted_iota(jnp.int32, shape, axis)


def near_z(v):
    lane = iota(v.shape, 1)
    last = v.shape[1] - 1
    below = jnp.where(lane == 0, 0.0, roll(v, 1, 1))
    above = jnp.where(lane == last, 0.0, roll(v, -1, 1))
    return below + above


def near_x(v):
    return roll(v, 1, 0) + roll(v, -1, 0)


def operate(v, v_near_x, v_near_y, rho, cx, cy, cz):
    twice = 2.0 * v
    stencil = cx * (twice - v_near_x) + cy * (twice - v_near_y) + cz * (twice - near_z(v))
    return shift_term * v + rho * stencil


def diagonal(rho, cx, cy, cz):
    return shift_term + 2.0 * rho * (cx + cy + cz)


def solve_z(w, lines):
    count, size = lines.shape[0], lines.shape[1]
    parts = []
    for k in range(count):
        parts.append(dot(w[:, k * size : (k + 1) * size], lines[k], ((1,), (1,))))
    return jnp.concatenate(parts, axis=1)


def columns_by(v, pick):
    cuts = [slice(256 * k, 256 * (k + 1)) for k in range(v.shape[1] // 256)]
    return jnp.concatenate([pick_right(v[:, cut], pick) for cut in cuts], axis=1)


def pair_columns(v, scale):
    fine, coarse = iota((256, 128), 0), iota((256, 128), 1)
    return columns_by(v, jnp.where(fine // 2 == coarse, scale, 0.0))


def even_columns(v, scale):
    fine, coarse = iota((256, 128), 0), iota((256, 128), 1)
    return columns_by(v, jnp.where(fine == 2 * coarse, scale, 0.0))


def restrict_columns(v):
    lane = iota(v.shape, 1)
    last = v.shape[1] - 1
    one = jnp.where(lane == last, 0.0, roll(v, -1, 1))
    two = jnp.where(lane >= last - 1, 0.0, roll(v, -2, 1))
    below = jnp.where(lane == 0, 0.0, roll(v, 1, 1))
    return even_columns(below + 3.0 * v + 3.0 * one + two, 0.125)


def raise_columns(v):
    lane = iota(v.shape, 1)
    last = v.shape[1] - 1
    below = jnp.where(lane == 0, 0.0, roll(v, 1, 1))
    above = jnp.where(lane == last, 0.0, roll(v, -1, 1))
    even = 3.0 * v + below
    odd = 3.0 * v + above
    coarse, fine = iota((128, 256), 0), iota((128, 256), 1)
    at_even = jnp.where(fine == 2 * coarse, 0.25, 0.0)
    at_odd = jnp.where(fine == 2 * coarse + 1, 0.25, 0.0)
    parts = []
    for k in range(v.shape[1] // 128):
        cut = slice(128 * k, 128 * (k + 1))
        parts.append(pick_right(even[:, cut], at_even) + pick_right(odd[:, cut], at_odd))
    return jnp.concatenate(parts, axis=1)


def restrict_rows(v):
    coarse, fine = iota((ME, FE), 0), iota((ME, FE), 1)
    away = fine - 2 * coarse
    weight = jnp.where((away == 0) | (away == 1), 0.375, 0.0)
    weight = weight + jnp.where((away == -1) | (away == 2), 0.125, 0.0)
    return pick_left(weight, v)


def pair_rows(v):
    coarse, fine = iota((ME, FE), 0), iota((ME, FE), 1)
    return pick_left(jnp.where(fine // 2 == coarse, 1.0, 0.0), v)


def raise_rows(v):
    fine, coarse = iota((FE, ME), 0), iota((FE, ME), 1)
    away = fine - 2 * coarse
    weight = jnp.where((away == 0) | (away == 1), 0.75, 0.0)
    weight = weight + jnp.where((away == 2) | (away == -1), 0.25, 0.0)
    return pick_left(weight, v)


def inside_middle(px):
    row = iota((ME, MZ), 0) + MX * px - MH
    return (row >= 0) & (row < MX * N_PX)


def inside_fine(px):
    row = iota((FE, FZ), 0) + FX * px - FH
    return (row >= 0) & (row < FX * N_PX)


def to_slabs(plane, out, at):
    for m in range(8):
        out[m, at] = plane[:, 128 * m : 128 * (m + 1)]


def from_slabs(ref, at):
    return jnp.concatenate([ref[m, at] for m in range(8)], axis=1)


def start(px, py, forcing, inv_density, sx, sy, force, rho, lower, upper, low, high, cx):
    square = iota((FX, FX), 0) == iota((FX, FX), 1)
    column = jnp.sum(jnp.where(square, sx[...], 0.0), axis=1, keepdims=True)
    cx[...] = jnp.broadcast_to(column, (FX, 128))
    wide = jnp.broadcast_to(column, (FX, FZ))
    for at, out in ((0, lower), (1, upper)):
        f_plane, r_plane = forcing[:, at, :], inv_density[:, at, :]
        force[at] = f_plane
        rho[at] = r_plane
        out[0:32] = f_plane
        out[32:64] = r_plane
        out[64:72] = jnp.broadcast_to(sy[0:1, at : at + 1], (8, FZ))
        for side, rows in ((low, slice(0, 8)), (high, slice(24, 32))):
            side[8 * at : 8 * at + 8] = f_plane[rows]
            side[16 + 8 * at : 24 + 8 * at] = r_plane[rows]
    low[32:40] = wide[0:8]
    high[32:40] = wide[24:32]


def own_lines(px, py, force, rho, cx, sy, cz, lines, u):
    parts = []
    for at in range(2):
        parts.append(force[at] / diagonal(rho[at], cx[:, 0:1], sy[0:1, at : at + 1], cz[...]))
    solved = solve_z(jnp.concatenate(parts, axis=0), lines)
    u[0] = solved[0:FX]
    u[1] = solved[FX : 2 * FX]


def first_half(px, py, force, rho, cx, sy, cz, u, below, above, left, right, lines, slabs):
    cx_col = cx[:, 0:1]
    cz_row = cz[...]
    parts = []
    for side in (below, above):
        parts.append(side[0:32] / diagonal(side[32:64], cx_col, side[64:65], cz_row))
    for side in (left, right):
        for at in range(2):
            cut, deep = slice(8 * at, 8 * at + 8), slice(16 + 8 * at, 24 + 8 * at)
            parts.append(side[cut] / diagonal(side[deep], side[32:40, 0:1], sy[0:1, at : at + 1], cz_row))
    solved = solve_z(jnp.concatenate(parts, axis=0), lines)
    planes = [solved[0:32], u[0], u[1], solved[32:64]]
    for at in range(2):
        own = u[at]
        before, after = solved[64 + 8 * at : 72 + 8 * at], solved[80 + 8 * at : 88 + 8 * at]
        beside_x = near_x(jnp.concatenate([before, own, after], axis=0))[FH : FH + FX]
        beside_y = planes[at] + planes[at + 2]
        cy = sy[0:1, at : at + 1]
        applied = operate(own, beside_x, beside_y, rho[at], cx_col, cy, cz_row)
        to_slabs((force[at] - applied) / diagonal(rho[at], cx_col, cy, cz_row), slabs, at)


def middle_statics(px, py, rho, cx, sy, cz, left, right, column, r_mid, cx_mid, cyz_mid, told):
    total = None
    for at in range(2):
        deep = slice(16 + 8 * at, 24 + 8 * at)
        plane = jnp.concatenate([left[deep], rho[at], right[deep]], axis=0)
        total = plane if total is None else total + plane
    dense = pair_columns(pair_rows(total), 0.125)
    columns = jnp.concatenate([left[32:40, 0:128], cx[...], right[32:40, 0:128]], axis=0)
    cym = jnp.broadcast_to((sy[0:1, 0:1] + sy[0:1, 1:2]) * 0.125, (8, MZ))
    czm = pair_columns(jnp.broadcast_to(cz[...], (16, FZ)), 0.125)
    r_mid[...] = dense
    cx_mid[...] = pair_rows(columns) * 0.125
    cyz_mid[...] = jnp.concatenate([czm[0:1], cym[0:7]], axis=0)
    own = roll(dense, -MH, 0)[0:MX]
    told[0:8, 0:MZ] = own[0:8]
    told[0:8, MZ:FZ] = own[8:16]
    for k in range(4):
        told[8:16, 128 * k : 128 * (k + 1)] = column[8 * k : 8 * (k + 1)]
    told[8:16, MZ:FZ] = cym


def solve_x_fine(px, py, slabs, lines, out):
    block = lines[0]
    for at in range(2):
        column = jnp.concatenate([slabs[m, at] for m in range(8)], axis=0)
        solved = dot(block, column)
        for m in range(8):
            out[m, at] = solved[32 * m : 32 * (m + 1)]


def add_slabs(px, py, u, slabs, told, out):
    for at in range(2):
        out[FX * at : FX * (at + 1)] = u[at] + from_slabs(slabs, at)
    out[64:80] = told[...]


def pack_u(px, py, u, below, above, y_below, y_above, low, high):
    for start_row, out in ((0, low), (24, high)):
        rows = slice(start_row, start_row + 8)
        next_rows = slice(32 + start_row, 40 + start_row)
        for j, side in enumerate((below, u, above)):
            out[16 * j : 16 * j + 8] = side[rows]
            out[16 * j + 8 : 16 * j + 16] = side[next_rows]
        for j, side in enumerate((y_below, y_above)):
            out[48 + 16 * j : 56 + 16 * j] = side[rows]
            out[56 + 16 * j : 64 + 16 * j] = side[next_rows]


def to_middle(px, py, u, below, above, left, right, force, rho, y_below, y_above, x_left, x_right, cx, sy, cz, r_mid, cx_mid, cyz_mid, lines, u_ext, f_ext, r_ext, cx_ext, f_mid, v_out, told):
    columns = jnp.concatenate([x_left[32:40, 0:128], cx[...], x_right[32:40, 0:128]], axis=0)
    cx_ext[...] = columns
    cx_col = columns[:, 0:1]
    cz_row = cz[...]
    told[0:16] = below[64:80]
    told[16:32] = above[64:80]
    planes = []
    for j in range(6):
        side = (below, u, above)[j // 2]
        own = side[FX * (j % 2) : FX * (j % 2) + FX]
        planes.append(jnp.concatenate([left[8 * j : 8 * j + 8], own, right[8 * j : 8 * j + 8]], axis=0))
    total = None
    for j in range(4):
        if j in (1, 2):
            at = j - 1
            cut, deep = slice(8 * at, 8 * at + 8), slice(16 + 8 * at, 24 + 8 * at)
            f_plane = jnp.concatenate([x_left[cut], force[at], x_right[cut]], axis=0)
            r_plane = jnp.concatenate([x_left[deep], rho[at], x_right[deep]], axis=0)
            f_ext[at] = f_plane
            r_ext[at] = r_plane
            cy = sy[0:1, at : at + 1]
        else:
            side, at = (y_below, 48) if j == 0 else (y_above, 64)
            cut, deep = slice(at, at + 8), slice(at + 8, at + 16)
            f_plane = jnp.concatenate([left[cut], side[0:32], right[cut]], axis=0)
            r_plane = jnp.concatenate([left[deep], side[32:64], right[deep]], axis=0)
            cy = side[64:65]
        own = planes[j + 1]
        u_ext[j] = own
        applied = operate(own, near_x(own), planes[j] + planes[j + 2], r_plane, cx_col, cy, cz_row)
        left_over = f_plane - applied
        if j in (1, 2):
            left_over = 3.0 * left_over
        total = left_over if total is None else total + left_over
    rhs = restrict_columns(restrict_rows(total * 0.125))
    rhs = jnp.where(inside_middle(px), rhs, 0.0)
    f_mid[...] = rhs
    diag = diagonal(*middle_parts(r_mid, cx_mid, cyz_mid))
    v_out[...] = solve_z(rhs / diag, lines)


def middle_parts(r_mid, cx_mid, cyz_mid):
    return r_mid[...], cx_mid[:, 0:1], cyz_mid[1:2], cyz_mid[0:1]


def middle_scaled(px, py, v, below, above, f_mid, r_mid, cx_mid, cyz_mid, out):
    rho, cx, cy, cz = middle_parts(r_mid, cx_mid, cyz_mid)
    own = v[...]
    applied = operate(own, near_x(own), below[...] + above[...], rho, cx, cy, cz)
    scaled = (f_mid[...] - applied) / diagonal(rho, cx, cy, cz)
    part = roll(scaled, -MH, 0)[0:MX]
    for i in range(N_PX):
        out[i] = part


def solve_x_middle(px, py, gathered, lines, v, out):
    total = MX * N_PX
    pieces = []
    starts = (
        (jnp.maximum(MX * px - 8, 0), 8),
        (MX * px, MX),
        (jnp.minimum(MX * px + MX, total - 8), 8),
    )
    for start, size in starts:
        rows = dyn(lines, start, size)
        block = (start // 256) * 256
        pieces.append(dot(rows, dyn(gathered, block, 256)))
    full = jnp.concatenate(pieces, axis=0)
    part = roll(full, MH - 8, 0)[0:ME]
    out[...] = v[...] + jnp.where(inside_middle(px), part, 0.0)


def block_mean(px, py, v, f_mid, r_mid, cx_mid, cyz_mid, told, column, out):
    rho, cx, cy, cz = middle_parts(r_mid, cx_mid, cyz_mid)
    own = v[...]
    applied = operate(own, near_x(own), 0.0, rho, cx, cy, cz)
    row = iota((ME, MZ), 0)
    kept = jnp.where((row >= MH) & (row < MH + MX), f_mid[...] - applied, 0.0)

    def mean(a):
        return jnp.sum(jnp.sum(a, axis=0, keepdims=True), axis=1, keepdims=True) * (1.0 / (MX * MZ))

    sent = column[...] * mean(kept)
    inner = roll(own, -MH, 0)[0:MX]
    for at in (0, 16):
        share = mean(told[at : at + 8, 0:MZ] * inner[0:8] + told[at : at + 8, MZ:FZ] * inner[8:16])
        share = share * told[at + 8 : at + 9, MZ : MZ + 1]
        theirs = [told[at + 8 : at + 16, 128 * k : 128 * (k + 1)] for k in range(4)]
        sent = sent + jnp.concatenate(theirs, axis=0) * share
    for i in range(N_PX):
        out[i] = jnp.broadcast_to(sent[i : i + 1], (8, 128))


def sum_x(px, py, parts, out):
    total = parts[0]
    for i in range(1, N_PX):
        total = total + parts[i]
    for j in range(N_PY):
        out[j] = total


def second_half(px, py, parts, v, below, above, f_mid, r_mid, cx_mid, cyz_mid, lines, out):
    total = parts[0]
    for j in range(1, N_PY):
        total = total + parts[j]
    lane = iota((8, 128), 1)
    row = iota((ME, MZ), 0)

    def raised(plane, dy):
        held = (py + dy >= 0) & (py + dy < N_PY)
        at = []
        for dx in range(3):
            wanted = (lane == dx * N_PY + py + dy) & held
            found = jnp.sum(jnp.where(wanted, total, 0.0), axis=1, keepdims=True)[0:1]
            at.append(found)
        return plane + jnp.where(row < MH, at[0], jnp.where(row < MH + MX, at[1], at[2]))

    own = raised(v[...], 0)
    beside = raised(below[...], -1) + raised(above[...], 1)
    rho, cx, cy, cz = middle_parts(r_mid, cx_mid, cyz_mid)
    applied = operate(own, near_x(own), beside, rho, cx, cy, cz)
    out[...] = own + solve_z((f_mid[...] - applied) / diagonal(rho, cx, cy, cz), lines)


def to_fine(px, py, v, below, above, u_ext, f_ext, r_ext, cx_ext, sy, cz, lines, out, lower, upper):
    rows = [raise_rows(p[...]) for p in (below, v, above)]
    columns = raise_columns(jnp.concatenate(rows, axis=0)) * 0.25
    raised = [columns[FE * i : FE * (i + 1)] for i in range(3)]
    mids = [
        3.0 * raised[0] + raised[1],
        3.0 * raised[1] + raised[0],
        3.0 * raised[1] + raised[2],
        3.0 * raised[2] + raised[1],
    ]
    inside = inside_fine(px)
    us = []
    for j in range(4):
        held = inside
        if j == 0:
            held = inside & (py > 0)
        if j == 3:
            held = inside & (py < N_PY - 1)
        us.append(u_ext[j] + jnp.where(held, mids[j], 0.0))
    cx_col = cx_ext[:, 0:1]
    cz_row = cz[...]
    parts = []
    for at in range(2):
        own = us[at + 1]
        cy = sy[0:1, at : at + 1]
        applied = operate(own, near_x(own), us[at] + us[at + 2], r_ext[at], cx_col, cy, cz_row)
        parts.append((f_ext[at] - applied) / diagonal(r_ext[at], cx_col, cy, cz_row))
    solved = solve_z(jnp.concatenate(parts, axis=0), lines)
    for at in range(2):
        new = us[at + 1] + solved[FE * at : FE * (at + 1)]
        out[at] = new
        (lower if at == 0 else upper)[...] = new[FH : FH + FX]


def last_scaled(px, py, u, below, above, f_ext, r_ext, cx_ext, sy, cz, slabs):
    cx_col = cx_ext[FH : FH + FX, 0:1]
    cz_row = cz[...]
    inner = slice(FH, FH + FX)
    for at in range(2):
        full = u[at]
        beside_x = near_x(full)[inner]
        own = full[inner]
        beside_y = (below[...] if at == 0 else u[0, inner]) + (above[...] if at == 1 else u[1, inner])
        rho = r_ext[at, inner]
        cy = sy[0:1, at : at + 1]
        applied = operate(own, beside_x, beside_y, rho, cx_col, cy, cz_row)
        scaled = (f_ext[at, inner] - applied) / diagonal(rho, cx_col, cy, cz_row)
        to_slabs(scaled, slabs, at)


def finish(px, py, u, slabs, out):
    for at in range(2):
        out[:, at, :] = u[at, FH : FH + FX] + from_slabs(slabs, at)


class Device:
    def run(self, stage, shapes, *args):
        def kernel(*refs):
            stage(lax.axis_index("px"), lax.axis_index("py"), *refs)

        whole = pl.BlockSpec(memory_space=pltpu.VMEM)
        outs = pl.pallas_call(
            kernel,
            out_shape=[jax.ShapeDtypeStruct(s, f32) for s in shapes],
            in_specs=[whole] * len(args),
            out_specs=[whole] * len(shapes),
            compiler_params=pltpu.CompilerParams(vmem_limit_bytes=24 * 1024 * 1024),
            name=stage.__name__,
        )(*args)
        return outs if len(shapes) > 1 else outs[0]

    def local(self, fn, *args):
        return fn(*args)

    def block_of(self, lines):
        at = lax.axis_index("px") // 8
        return lax.dynamic_slice_in_dim(lines, at, 1, axis=0)

    def beside(self, axis, low, high):
        n = lax.axis_size(axis)
        up = [(i, i + 1) for i in range(n - 1)]
        down = [(j, i) for i, j in up]
        return lax.ppermute(high, axis, up), lax.ppermute(low, axis, down)

    def swap(self, axis, array, group):
        n = lax.axis_size(axis)
        groups = None
        if group < n:
            groups = [list(range(k, k + group)) for k in range(0, n, group)]
        return lax.all_to_all(array, axis, 0, 0, axis_index_groups=groups, tiled=True)


def arrange_column(coarse):
    table = coarse.reshape(N_PY, N_PX).T
    none = jnp.zeros((1, N_PY), f32)
    before = jnp.concatenate([none, table[:-1]], axis=0)
    after = jnp.concatenate([table[1:], none], axis=0)
    return jnp.concatenate([before, table, after, jnp.zeros((N_PX, 128 - 3 * N_PY), f32)], axis=1)


def cycle(d, forcing, inv_density, stretch_x, stretch_y, stretch_z, lines_z0, lines_x0, lines_z1, lines_x1, coarse_inverse):
    sx = d.local(lambda a: a.reshape(1, FX), stretch_x)
    sy = d.local(lambda a: a.reshape(1, 2), stretch_y)
    cz = d.local(lambda a: a.reshape(1, FZ), stretch_z)
    rows_x1 = d.local(lambda a: a.reshape(MX * N_PX, 256), lines_x1)
    slab, own, mid = (8, 2, FX, 128), (2, FX, FZ), (ME, MZ)

    force, rho, lower, upper, low, high, cx = d.run(
        start,
        [own, own, (72, FZ), (72, FZ), (40, FZ), (40, FZ), (FX, 128)],
        forcing, inv_density, sx, sy,
    )
    y_below, y_above = d.beside("py", lower, upper)
    x_left, x_right = d.beside("px", low, high)
    column = d.local(arrange_column, coarse_inverse)
    block = d.block_of(lines_x0)
    u = d.run(own_lines, [own], force, rho, cx, sy, cz, lines_z0)
    slabs = d.run(
        first_half, [slab],
        force, rho, cx, sy, cz, u, y_below, y_above, x_left, x_right, lines_z0,
    )
    slabs = d.swap("px", slabs, 8)
    r_mid, cx_mid, cyz_mid, told = d.run(
        middle_statics,
        [mid, (ME, 128), (8, MZ), (16, FZ)],
        rho, cx, sy, cz, x_left, x_right, column,
    )
    slabs = d.run(solve_x_fine, [slab], slabs, block)
    slabs = d.swap("px", slabs, 8)
    u = d.run(add_slabs, [(80, FZ)], u, slabs, told)
    below, above = d.beside("py", u, u)
    low, high = d.run(pack_u, [(80, FZ)] * 2, u, below, above, y_below, y_above)
    left, right = d.beside("px", low, high)
    u_ext, f_ext, r_ext, cx_ext, f_mid, v, told = d.run(
        to_middle,
        [(4, FE, FZ), (2, FE, FZ), (2, FE, FZ), (FE, 128), mid, mid, (32, FZ)],
        u, below, above, left, right, force, rho, y_below, y_above, x_left, x_right,
        cx, sy, cz, r_mid, cx_mid, cyz_mid, lines_z1,
    )
    statics = (f_mid, r_mid, cx_mid, cyz_mid)

    below, above = d.beside("py", v, v)
    every = d.run(middle_scaled, [(N_PX, MX, MZ)], v, below, above, *statics)
    every = d.swap("px", every, N_PX)
    every = d.local(lambda a: a.reshape(MX * N_PX, MZ), every)
    v = d.run(solve_x_middle, [mid], every, rows_x1, v)
    below, above = d.beside("py", v, v)
    sent = d.run(block_mean, [(N_PX, 8, 128)], v, *statics, told, column)
    parts = d.swap("px", sent, N_PX)
    parts = d.run(sum_x, [(N_PY, 8, 128)], parts)
    parts = d.swap("py", parts, N_PY)
    v = d.run(second_half, [mid], parts, v, below, above, *statics, lines_z1)
    below, above = d.beside("py", v, v)
    every = d.run(middle_scaled, [(N_PX, MX, MZ)], v, below, above, *statics)
    every = d.swap("px", every, N_PX)
    every = d.local(lambda a: a.reshape(MX * N_PX, MZ), every)
    v = d.run(solve_x_middle, [mid], every, rows_x1, v)

    below, above = d.beside("py", v, v)
    u, lower, upper = d.run(
        to_fine,
        [(2, FE, FZ), (FX, FZ), (FX, FZ)],
        v, below, above, u_ext, f_ext, r_ext, cx_ext, sy, cz, lines_z0,
    )
    below, above = d.beside("py", lower, upper)
    slabs = d.run(last_scaled, [slab], u, below, above, f_ext, r_ext, cx_ext, sy, cz)
    slabs = d.swap("px", slabs, 8)
    slabs = d.run(solve_x_fine, [slab], slabs, block)
    slabs = d.swap("px", slabs, 8)
    return d.run(finish, [(FX, 2, FZ)], u, slabs)


def solution(mesh):
    placed = (
        P("px", "py", None),
        P("px", "py", None),
        P("px"),
        P("py"),
        P(),
        P(),
        P(),
        P(),
        P(),
        P(("py", "px"), None),
    )
    return jax.shard_map(
        functools.partial(cycle, Device()),
        mesh=mesh,
        in_specs=placed,
        out_specs=P("px", "py", None),
        check_vma=False,
    )
```

time: 344 us -> 277 us (0.81)
  the two profiles are of different devices: /device:TPU:4 before, /device:TPU:2 now
where the time goes in v2:
time: 277 us; the launch traced here: 276 us
  blocking collectives  118 us (43%)
  waiting for transfers between devices  74.2 us (27%)
  starting transfers between devices  60.4 us (22%)
  local copies, waits for them, and re-layouts  11.1 us (4%)
  Pallas kernels  10.7 us (4%)
    all_to_all x5, blocking collectives, swap(): lax.all_to_all(array, axis, 0, 0, axis_index_groups=groups, tiled=True)  118 us
    ppermute x18, waiting for transfers between devices, beside(): return (lax.ppermute(high, axis, up), lax.ppermute(low, axis, down))  58.8 us
    ppermute x18, starting transfers between devices, beside(): return (lax.ppermute(high, axis, up), lax.ppermute(low, axis, down))  45.5 us
    all_to_all x3, waiting for transfers between devices, swap(): lax.all_to_all(array, axis, 0, 0, axis_index_groups=groups, tiled=True)  15.5 us
    all_to_all x3, starting transfers between devices, swap(): lax.all_to_all(array, axis, 0, 0, axis_index_groups=groups, tiled=True)  15 us
    unnamed x73, local copies, waits for them, and re-layouts  10.8 us
    pallas_call x19, Pallas kernels, run(): pl.pallas_call(kernel, out_shape=[jax.ShapeDtypeStruct(s, f32) for s in s...  10.7 us
  transfers between devices with their start and end apart: 21, of which 14 were waited for; matrix products, arithmetic and copies ran while one was open for 1% of the time, Pallas kernels for 0%

profile of v2, /device:TPU:2, one launch (start us, length us, event | category | flops | bytes accessed | tf_op | source)
XLA Modules:
  0.0 276.1 jit_solution(3445035675455031626)
XLA Ops:
  2.8 1.9 collective-permute-start
  4.7 4.5 %collective-permute-start.1 = (f32[72,1024]{1,0:T(8,128)S(1)}, f32[72,1024]{1,0:T(8,128)S(1)}, u32[]{:S(2)}, u32[]{:S(2)}) collective-permute-start(f32[72,1024]{1,0:T(8,128)S(1)} %get-tuple-element.32), channel_id=1, source_target_pairs={{32,0},{64,32},{96,64},{128,96},{160,128},{192,160},{224,192},{256... | collective-permute-start | bytes 884744 | tf_op jit(solution)/shard_map/ppermute | solution.py:485
  9.3 6.1 %collective-permute-start.2 = (f32[40,1024]{1,0:T(8,128)S(1)}, f32[40,1024]{1,0:T(8,128)S(1)}, u32[]{:S(2)}, u32[]{:S(2)}) collective-permute-start(f32[40,1024]{1,0:T(8,128)S(1)} %get-tuple-element.33), channel_id=1, source_target_pairs={{0,1},{1,2},{2,3},{3,4},{4,5},{5,6},{6,7},{7,8},{8,9},{9,10},{10,1... | collective-permute-start | bytes 491528 | tf_op jit(solution)/shard_map/ppermute | solution.py:485
  18.9 11.5 %collective-permute-done.3.refs_9_.refs_5_.refs_10_ = f32[40,1024]{1,0:T(8,128)S(1)} collective-permute-done((f32[40,1024]{1,0:T(8,128)S(1)}, f32[40,1024]{1,0:T(8,128)S(1)}, u32[]{:S(2)}, u32[]{:S(2)}) %collective-permute-start.3) | collective-permute-done | bytes 163872 | tf_op jit(solution)/shard_map/ppermute | solution.py:485
  31.8 5.2 %all-to-all-start = ((f32[8,2,32,128]{3,2,1,0:T(8,128)}), f32[8,2,32,128]{3,2,1,0:T(8,128)S(1)}, u32[]{:S(2)}, u32[]{:S(2)}) async-start(f32[8,2,32,128]{3,2,1,0:T(8,128)} %first_half.1), calls=%async_computation | async-start | bytes 524288 | tf_op jit(solution)/shard_map/all_to_all | solution.py:492
  37.1 9.6 %all-to-all-done.refs_0_ = f32[8,2,32,128]{3,2,1,0:T(8,128)S(1)} async-done(((f32[8,2,32,128]{3,2,1,0:T(8,128)}), f32[8,2,32,128]{3,2,1,0:T(8,128)S(1)}, u32[]{:S(2)}, u32[]{:S(2)}) %all-to-all-start) | async-done | bytes 262176 | tf_op jit(solution)/shard_map/all_to_all | solution.py:492
  47.8 4.5 %all-to-all-start.1 = ((f32[8,2,32,128]{3,2,1,0:T(8,128)}), f32[8,2,32,128]{3,2,1,0:T(8,128)S(1)}, u32[]{:S(2)}, u32[]{:S(2)}) async-start(f32[8,2,32,128]{3,2,1,0:T(8,128)} %copy-done.9), calls=%async_computation.1 | async-start | bytes 524288 | tf_op jit(solution)/shard_map/all_to_all | solution.py:492
  56.1 5.9 %all-to-all-done.1.refs_1_ = f32[8,2,32,128]{3,2,1,0:T(8,128)S(1)} async-done(((f32[8,2,32,128]{3,2,1,0:T(8,128)}), f32[8,2,32,128]{3,2,1,0:T(8,128)S(1)}, u32[]{:S(2)}, u32[]{:S(2)}) %all-to-all-start.1) | async-done | bytes 262176 | tf_op jit(solution)/shard_map/all_to_all | solution.py:492
  62.1 2.1 collective-permute-start.5
  64.1 2.4 collective-permute-start.4
  66.6 2.2 collective-permute-done.5.refs_2_
  68.7 8.8 %collective-permute-done.4.refs_1_ = f32[80,1024]{1,0:T(8,128)S(1)} collective-permute-done((f32[80,1024]{1,0:T(8,128)S(1)}, f32[80,1024]{1,0:T(8,128)S(1)}, u32[]{:S(2)}, u32[]{:S(2)}) %collective-permute-start.4) | collective-permute-done | bytes 327712 | tf_op jit(solution)/shard_map/ppermute | solution.py:485
  80.2 3.3 %collective-permute-done.6.refs_3_ = f32[80,1024]{1,0:T(8,128)S(1)} collective-permute-done((f32[80,1024]{1,0:T(8,128)S(1)}, f32[80,1024]{1,0:T(8,128)S(1)}, u32[]{:S(2)}, u32[]{:S(2)}) %collective-permute-start.6) | collective-permute-done | bytes 327712 | tf_op jit(solution)/shard_map/ppermute | solution.py:485
  83.5 14.2 %collective-permute-done.7.refs_4_ = f32[80,1024]{1,0:T(8,128)S(1)} collective-permute-done((f32[80,1024]{1,0:T(8,128)S(1)}, f32[80,1024]{1,0:T(8,128)S(1)}, u32[]{:S(2)}, u32[]{:S(2)}) %collective-permute-start.7) | collective-permute-done | bytes 327712 | tf_op jit(solution)/shard_map/ppermute | solution.py:485
  104.2 2.4 collective-permute-start.8
  106.6 3.9 %collective-permute-done.8.refs_1_ = f32[24,512]{1,0:T(8,128)S(1)} collective-permute-done((f32[24,512]{1,0:T(8,128)S(1)}, f32[24,512]{1,0:T(8,128)S(1)}, u32[]{:S(2)}, u32[]{:S(2)}) %collective-permute-start.8) | collective-permute-done | bytes 49184 | tf_op jit(solution)/shard_map/ppermute | solution.py:485
  110.8 36.5 %all_to_all.40 = f32[32,16,512]{2,1,0:T(8,128)S(1)} all-to-all(f32[32,16,512]{2,1,0:T(8,128)S(1)} %middle_scaled.2), channel_id=1, replica_groups=mesh['py'=16,'px'=32] {'px'}, dimensions={0} | all-to-all | bytes 2097152 | tf_op jit(solution)/shard_map/all_to_all | solution.py:492
  148.2 19.5 %all_to_all.41.refs_0_ = f32[32,8,128]{2,1,0:T(8,128)S(1)} all-to-all(f32[32,8,128]{2,1,0:T(8,128)S(1)} %block_mean.1), channel_id=1, replica_groups=mesh['py'=16,'px'=32] {'px'}, dimensions={0} | all-to-all | bytes 262144 | tf_op jit(solution)/shard_map/all_to_all | solution.py:492
  168.3 5.2 %all-to-all-start.4 = ((f32[16,8,128]{2,1,0:T(8,128)}), f32[16,8,128]{2,1,0:T(8,128)S(1)}, u32[]{:S(2)}, u32[]{:S(2)}) async-start(f32[16,8,128]{2,1,0:T(8,128)} %sum_x.1), calls=%async_computation.4 | async-start | bytes 131072 | tf_op jit(solution)/shard_map/all_to_all | solution.py:492
  173.5 3.1 %collective-permute-start.11 = (f32[24,512]{1,0:T(8,128)S(1)}, f32[24,512]{1,0:T(8,128)S(1)}, u32[]{:S(2)}, u32[]{:S(2)}) collective-permute-start(f32[24,512]{1,0:T(8,128)S(1)} %solve_x_middle.2.refs_0_.refs_1_), channel_id=1, source_target_pairs={{32,0},{64,32},{96,64},{128,96},{160,128},{192,160},{224,192},{256... | collective-permute-start | bytes 147464 | tf_op jit(solution)/shard_map/ppermute | solution.py:485
  176.6 1.9 collective-permute-start.10
  178.6 4.4 %collective-permute-done.10.refs_2_ = f32[24,512]{1,0:T(8,128)S(1)} collective-permute-done((f32[24,512]{1,0:T(8,128)S(1)}, f32[24,512]{1,0:T(8,128)S(1)}, u32[]{:S(2)}, u32[]{:S(2)}) %collective-permute-start.10) | collective-permute-done | bytes 49184 | tf_op jit(solution)/shard_map/ppermute | solution.py:485
  183.4 1.9 collective-permute-start.13
  185.4 2.4 collective-permute-start.12
  187.8 3.9 %collective-permute-done.12.refs_1_ = f32[24,512]{1,0:T(8,128)S(1)} collective-permute-done((f32[24,512]{1,0:T(8,128)S(1)}, f32[24,512]{1,0:T(8,128)S(1)}, u32[]{:S(2)}, u32[]{:S(2)}) %collective-permute-start.12) | collective-permute-done | bytes 49184 | tf_op jit(solution)/shard_map/ppermute | solution.py:485
  191.9 30.7 %all_to_all.42 = f32[32,16,512]{2,1,0:T(8,128)S(1)} all-to-all(f32[32,16,512]{2,1,0:T(8,128)S(1)} %middle_scaled.3), channel_id=1, replica_groups=mesh['py'=16,'px'=32] {'px'}, dimensions={0} | all-to-all | bytes 2097152 | tf_op jit(solution)/shard_map/all_to_all | solution.py:492
  223.1 2.0 collective-permute-start.15
  225.1 2.4 collective-permute-start.14
  227.6 3.9 %collective-permute-done.14.refs_1_ = f32[24,512]{1,0:T(8,128)S(1)} collective-permute-done((f32[24,512]{1,0:T(8,128)S(1)}, f32[24,512]{1,0:T(8,128)S(1)}, u32[]{:S(2)}, u32[]{:S(2)}) %collective-permute-start.14) | collective-permute-done | bytes 49184 | tf_op jit(solution)/shard_map/ppermute | solution.py:485
  235.8 4.5 %collective-permute-start.17 = (f32[32,1024]{1,0:T(8,128)S(1)}, f32[32,1024]{1,0:T(8,128)S(1)}, u32[]{:S(2)}, u32[]{:S(2)}) collective-permute-start(f32[32,1024]{1,0:T(8,128)S(1)} %get-tuple-element.50), channel_id=1, source_target_pairs={{32,0},{64,32},{96,64},{128,96},{160,128},{192,160},{224,192},{256... | collective-permute-start | bytes 393224 | tf_op jit(solution)/shard_map/ppermute | solution.py:485
  243.2 16.6 %all_to_all.43.refs_0_ = f32[8,2,32,128]{3,2,1,0:T(8,128)S(1)} all-to-all(f32[8,2,32,128]{3,2,1,0:T(8,128)S(1)} %last_scaled.1), channel_id=1, replica_groups={{0,1,2,3,4,5,6,7},{8,9,10,11,12,13,14,15},{16,17,18,19,20,21,22,23},{24..., dimensions={0} | all-to-all | bytes 524288 | tf_op jit(solution)/shard_map/all_to_all | solution.py:492
  260.2 15.1 %all_to_all.44.refs_1_ = f32[8,2,32,128]{3,2,1,0:T(8,128)S(1)} all-to-all(f32[8,2,32,128]{3,2,1,0:T(8,128)S(1)} %solve_x_fine.3), channel_id=1, replica_groups={{0,1,2,3,4,5,6,7},{8,9,10,11,12,13,14,15},{16,17,18,19,20,21,22,23},{24..., dimensions={0} | all-to-all | bytes 524288 | tf_op jit(solution)/shard_map/all_to_all | solution.py:492
  (115 shorter events, 33.0 us)
Async XLA Ops:
  0.0 37.1 %copy-start = (f32[4,256,256]{2,1,0:T(8,128)S(1)}, f32[4,256,256]{2,1,0:T(8,128)}, u32[]{:S(2)}) copy-start(f32[4,256,256]{2,1,0:T(8,128)} %param.16) | copy-start | bytes 3145732
  2.8 51.0 %copy-start.20 = (f32[32,128]{1,0:T(8,128)}, f32[32,128]{1,0:T(8,128)S(1)}, u32[]{:S(2)}) copy-start(f32[32,128]{1,0:T(8,128)S(1)} %get-tuple-element.30.refs_2_.refs_1_.refs_11_) | copy-start | bytes 49156
  2.8 27.5 %collective-permute-start = (f32[72,1024]{1,0:T(8,128)S(1)}, f32[72,1024]{1,0:T(8,128)S(1)}, u32[]{:S(2)}, u32[]{:S(2)}) collective-permute-start(f32[72,1024]{1,0:T(8,128)S(1)} %get-tuple-element.31), channel_id=1, source_target_pairs={{0,32},{32,64},{64,96},{96,128},{128,160},{160,192},{192,224},{224... | collective-permute-start | bytes 884744 | tf_op jit(solution)/shard_map/ppermute | solution.py:485
  4.7 25.6 %collective-permute-start.1 = (f32[72,1024]{1,0:T(8,128)S(1)}, f32[72,1024]{1,0:T(8,128)S(1)}, u32[]{:S(2)}, u32[]{:S(2)}) collective-permute-start(f32[72,1024]{1,0:T(8,128)S(1)} %get-tuple-element.32), channel_id=1, source_target_pairs={{32,0},{64,32},{96,64},{128,96},{160,128},{192,160},{224,192},{256... | collective-permute-start | bytes 884744 | tf_op jit(solution)/shard_map/ppermute | solution.py:485
  9.3 9.6 %collective-permute-start.2 = (f32[40,1024]{1,0:T(8,128)S(1)}, f32[40,1024]{1,0:T(8,128)S(1)}, u32[]{:S(2)}, u32[]{:S(2)}) collective-permute-start(f32[40,1024]{1,0:T(8,128)S(1)} %get-tuple-element.33), channel_id=1, source_target_pairs={{0,1},{1,2},{2,3},{3,4},{4,5},{5,6},{6,7},{7,8},{8,9},{9,10},{10,1... | collective-permute-start | bytes 491528 | tf_op jit(solution)/shard_map/ppermute | solution.py:485
  15.4 14.9 %collective-permute-start.3 = (f32[40,1024]{1,0:T(8,128)S(1)}, f32[40,1024]{1,0:T(8,128)S(1)}, u32[]{:S(2)}, u32[]{:S(2)}) collective-permute-start(f32[40,1024]{1,0:T(8,128)S(1)} %get-tuple-element.34), channel_id=1, source_target_pairs={{1,0},{2,1},{3,2},{4,3},{5,4},{6,5},{7,6},{8,7},{9,8},{10,9},{11,1... | collective-permute-start | bytes 491528 | tf_op jit(solution)/shard_map/ppermute | solution.py:485
  30.4 23.4 %copy-start.7 = (f32[40,1024]{1,0:T(8,128)}, f32[40,1024]{1,0:T(8,128)S(1)}, u32[]{:S(2)}) copy-start(f32[40,1024]{1,0:T(8,128)S(1)} %collective-permute-done.3.refs_9_.refs_5_.refs_10_) | copy-start | bytes 491524
  31.8 14.9 %all-to-all-start = ((f32[8,2,32,128]{3,2,1,0:T(8,128)}), f32[8,2,32,128]{3,2,1,0:T(8,128)S(1)}, u32[]{:S(2)}, u32[]{:S(2)}) async-start(f32[8,2,32,128]{3,2,1,0:T(8,128)} %first_half.1), calls=%async_computation | async-start | bytes 524288 | tf_op jit(solution)/shard_map/all_to_all | solution.py:492
  47.8 14.3 %all-to-all-start.1 = ((f32[8,2,32,128]{3,2,1,0:T(8,128)}), f32[8,2,32,128]{3,2,1,0:T(8,128)S(1)}, u32[]{:S(2)}, u32[]{:S(2)}) async-start(f32[8,2,32,128]{3,2,1,0:T(8,128)} %copy-done.9), calls=%async_computation.1 | async-start | bytes 524288 | tf_op jit(solution)/shard_map/all_to_all | solution.py:492
  62.1 35.7 %copy-start.4 = (f32[2,256,256]{2,1,0:T(8,128)S(1)}, f32[2,256,256]{2,1,0:T(8,128)}, u32[]{:S(2)}) copy-start(f32[2,256,256]{2,1,0:T(8,128)} %refs_8_.1) | copy-start | bytes 1572868
  62.1 35.6 %copy-start.8 = (f32[40,1024]{1,0:T(8,128)S(1)}, f32[40,1024]{1,0:T(8,128)}, u32[]{:S(2)}) copy-start(f32[40,1024]{1,0:T(8,128)} %copy-done.7) | copy-start | bytes 491524
  62.1 6.6 %collective-permute-start.5 = (f32[80,1024]{1,0:T(8,128)S(1)}, f32[80,1024]{1,0:T(8,128)S(1)}, u32[]{:S(2)}, u32[]{:S(2)}) collective-permute-start(f32[80,1024]{1,0:T(8,128)S(1)} %add_slabs.1.refs_0_), channel_id=1, source_target_pairs={{32,0},{64,32},{96,64},{128,96},{160,128},{192,160},{224,192},{256... | collective-permute-start | bytes 983048 | tf_op jit(solution)/shard_map/ppermute | solution.py:485
  64.1 13.4 %collective-permute-start.4 = (f32[80,1024]{1,0:T(8,128)S(1)}, f32[80,1024]{1,0:T(8,128)S(1)}, u32[]{:S(2)}, u32[]{:S(2)}) collective-permute-start(f32[80,1024]{1,0:T(8,128)S(1)} %add_slabs.1.refs_0_), channel_id=1, source_target_pairs={{0,32},{32,64},{64,96},{96,128},{128,160},{160,192},{192,224},{224... | collective-permute-start | bytes 983048 | tf_op jit(solution)/shard_map/ppermute | solution.py:485
  77.5 20.2 %copy-start.15 = (f32[8,512]{1,0:T(8,128)S(1)}, f32[8,512]{1,0:T(8,128)}, u32[]{:S(2)}) copy-start(f32[8,512]{1,0:T(8,128)} %copy-done.14) | copy-start | bytes 49156
  77.5 20.2 %copy-start.18 = (f32[24,128]{1,0:T(8,128)S(1)}, f32[24,128]{1,0:T(8,128)}, u32[]{:S(2)}) copy-start(f32[24,128]{1,0:T(8,128)} %copy-done.17) | copy-start | bytes 36868
  77.5 20.2 %copy-start.21 = (f32[32,128]{1,0:T(8,128)S(1)}, f32[32,128]{1,0:T(8,128)}, u32[]{:S(2)}) copy-start(f32[32,128]{1,0:T(8,128)} %copy-done.20) | copy-start | bytes 49156
  77.6 5.9 %collective-permute-start.6 = (f32[80,1024]{1,0:T(8,128)S(1)}, f32[80,1024]{1,0:T(8,128)S(1)}, u32[]{:S(2)}, u32[]{:S(2)}) collective-permute-start(f32[80,1024]{1,0:T(8,128)S(1)} %get-tuple-element.36), channel_id=1, source_target_pairs={{0,1},{1,2},{2,3},{3,4},{4,5},{5,6},{6,7},{7,8},{8,9},{9,10},{10,1... | collective-permute-start | bytes 983048 | tf_op jit(solution)/shard_map/ppermute | solution.py:485
  78.9 18.8 %collective-permute-start.7 = (f32[80,1024]{1,0:T(8,128)S(1)}, f32[80,1024]{1,0:T(8,128)S(1)}, u32[]{:S(2)}, u32[]{:S(2)}) collective-permute-start(f32[80,1024]{1,0:T(8,128)S(1)} %get-tuple-element.37), channel_id=1, source_target_pairs={{1,0},{2,1},{3,2},{4,3},{5,4},{6,5},{7,6},{8,7},{9,8},{10,9},{11,1... | collective-permute-start | bytes 983048 | tf_op jit(solution)/shard_map/ppermute | solution.py:485
  102.3 45.4 %copy-start.10 = (f32[24,512]{1,0:T(8,128)}, f32[24,512]{1,0:T(8,128)S(1)}, u32[]{:S(2)}) copy-start(f32[24,512]{1,0:T(8,128)S(1)} %get-tuple-element.42.refs_3_.refs_1_.refs_4_) | copy-start | bytes 147460
  102.3 4.3 %collective-permute-start.9 = (f32[24,512]{1,0:T(8,128)S(1)}, f32[24,512]{1,0:T(8,128)S(1)}, u32[]{:S(2)}, u32[]{:S(2)}) collective-permute-start(f32[24,512]{1,0:T(8,128)S(1)} %get-tuple-element.41.refs_0_.refs_2_), channel_id=1, source_target_pairs={{32,0},{64,32},{96,64},{128,96},{160,128},{192,160},{224,192},{256... | collective-permute-start | bytes 147464 | tf_op jit(solution)/shard_map/ppermute | solution.py:485
  104.2 6.3 %collective-permute-start.8 = (f32[24,512]{1,0:T(8,128)S(1)}, f32[24,512]{1,0:T(8,128)S(1)}, u32[]{:S(2)}, u32[]{:S(2)}) collective-permute-start(f32[24,512]{1,0:T(8,128)S(1)} %get-tuple-element.41.refs_0_.refs_2_), channel_id=1, source_target_pairs={{0,32},{32,64},{64,96},{96,128},{128,160},{160,192},{192,224},{224... | collective-permute-start | bytes 147464 | tf_op jit(solution)/shard_map/ppermute | solution.py:485
  110.7 36.5 %copy-start.3 = (f32[2,256,256]{2,1,0:T(8,128)S(1)}, f32[2,256,256]{2,1,0:T(8,128)}, u32[]{:S(2)}) copy-start(f32[2,256,256]{2,1,0:T(8,128)} %param.18) | copy-start | bytes 1572868
  168.3 14.6 %all-to-all-start.4 = ((f32[16,8,128]{2,1,0:T(8,128)}), f32[16,8,128]{2,1,0:T(8,128)S(1)}, u32[]{:S(2)}, u32[]{:S(2)}) async-start(f32[16,8,128]{2,1,0:T(8,128)} %sum_x.1), calls=%async_computation.4 | async-start | bytes 131072 | tf_op jit(solution)/shard_map/all_to_all | solution.py:492
  173.5 5.0 %collective-permute-start.11 = (f32[24,512]{1,0:T(8,128)S(1)}, f32[24,512]{1,0:T(8,128)S(1)}, u32[]{:S(2)}, u32[]{:S(2)}) collective-permute-start(f32[24,512]{1,0:T(8,128)S(1)} %solve_x_middle.2.refs_0_.refs_1_), channel_id=1, source_target_pairs={{32,0},{64,32},{96,64},{128,96},{160,128},{192,160},{224,192},{256... | collective-permute-start | bytes 147464 | tf_op jit(solution)/shard_map/ppermute | solution.py:485
  176.6 6.3 %collective-permute-start.10 = (f32[24,512]{1,0:T(8,128)S(1)}, f32[24,512]{1,0:T(8,128)S(1)}, u32[]{:S(2)}, u32[]{:S(2)}) collective-permute-start(f32[24,512]{1,0:T(8,128)S(1)} %solve_x_middle.2.refs_0_.refs_1_), channel_id=1, source_target_pairs={{0,32},{32,64},{64,96},{96,128},{128,160},{160,192},{192,224},{224... | collective-permute-start | bytes 147464 | tf_op jit(solution)/shard_map/ppermute | solution.py:485
  183.4 4.3 %collective-permute-start.13 = (f32[24,512]{1,0:T(8,128)S(1)}, f32[24,512]{1,0:T(8,128)S(1)}, u32[]{:S(2)}, u32[]{:S(2)}) collective-permute-start(f32[24,512]{1,0:T(8,128)S(1)} %second_half.1.refs_0_.refs_2_), channel_id=1, source_target_pairs={{32,0},{64,32},{96,64},{128,96},{160,128},{192,160},{224,192},{256... | collective-permute-start | bytes 147464 | tf_op jit(solution)/shard_map/ppermute | solution.py:485
  185.4 6.3 %collective-permute-start.12 = (f32[24,512]{1,0:T(8,128)S(1)}, f32[24,512]{1,0:T(8,128)S(1)}, u32[]{:S(2)}, u32[]{:S(2)}) collective-permute-start(f32[24,512]{1,0:T(8,128)S(1)} %second_half.1.refs_0_.refs_2_), channel_id=1, source_target_pairs={{0,32},{32,64},{64,96},{96,128},{128,160},{160,192},{192,224},{224... | collective-permute-start | bytes 147464 | tf_op jit(solution)/shard_map/ppermute | solution.py:485
  191.9 39.6 %copy-start.13 = (f32[4,48,1024]{2,1,0:T(8,128)S(1)}, f32[4,48,1024]{2,1,0:T(8,128)}, u32[]{:S(2)}) copy-start(f32[4,48,1024]{2,1,0:T(8,128)} %copy-done.12) | copy-start | bytes 2359300
  223.1 4.5 %collective-permute-start.15 = (f32[24,512]{1,0:T(8,128)S(1)}, f32[24,512]{1,0:T(8,128)S(1)}, u32[]{:S(2)}, u32[]{:S(2)}) collective-permute-start(f32[24,512]{1,0:T(8,128)S(1)} %solve_x_middle.3.refs_0_), channel_id=1, source_target_pairs={{32,0},{64,32},{96,64},{128,96},{160,128},{192,160},{224,192},{256... | collective-permute-start | bytes 147464 | tf_op jit(solution)/shard_map/ppermute | solution.py:485
  225.1 6.3 %collective-permute-start.14 = (f32[24,512]{1,0:T(8,128)S(1)}, f32[24,512]{1,0:T(8,128)S(1)}, u32[]{:S(2)}, u32[]{:S(2)}) collective-permute-start(f32[24,512]{1,0:T(8,128)S(1)} %solve_x_middle.3.refs_0_), channel_id=1, source_target_pairs={{0,32},{32,64},{64,96},{96,128},{128,160},{160,192},{192,224},{224... | collective-permute-start | bytes 147464 | tf_op jit(solution)/shard_map/ppermute | solution.py:485
  233.9 7.6 %collective-permute-start.16 = (f32[32,1024]{1,0:T(8,128)S(1)}, f32[32,1024]{1,0:T(8,128)S(1)}, u32[]{:S(2)}, u32[]{:S(2)}) collective-permute-start(f32[32,1024]{1,0:T(8,128)S(1)} %get-tuple-element.49), channel_id=1, source_target_pairs={{0,32},{32,64},{64,96},{96,128},{128,160},{160,192},{192,224},{224... | collective-permute-start | bytes 393224 | tf_op jit(solution)/shard_map/ppermute | solution.py:485
  235.8 7.0 %collective-permute-start.17 = (f32[32,1024]{1,0:T(8,128)S(1)}, f32[32,1024]{1,0:T(8,128)S(1)}, u32[]{:S(2)}, u32[]{:S(2)}) collective-permute-start(f32[32,1024]{1,0:T(8,128)S(1)} %get-tuple-element.50), channel_id=1, source_target_pairs={{32,0},{64,32},{96,64},{128,96},{160,128},{192,160},{224,192},{256... | collective-permute-start | bytes 393224 | tf_op jit(solution)/shard_map/ppermute | solution.py:485
  (25 other events, 116.8 us)

commit v3 on v2

--- a/solution.py
+++ b/solution.py
@@ -1,11 +1,10 @@
-import functools
-
 import jax
 import jax.numpy as jnp
 from jax import lax
 from jax.experimental import pallas as pl
 from jax.experimental.pallas import tpu as pltpu
 from jax.sharding import PartitionSpec as P
+
 
 shift_term = 0.1
 f32 = jnp.float32
@@ -273,6 +272,7 @@
         for j, side in enumerate((y_below, y_above)):
             out[48 + 16 * j : 56 + 16 * j] = side[rows]
             out[56 + 16 * j : 64 + 16 * j] = side[next_rows]
+        out[80:88] = u[72:80]
 
 
 def to_middle(px, py, u, below, above, left, right, force, rho, y_below, y_above, x_left, x_right, cx, sy, cz, r_mid, cx_mid, cyz_mid, lines, u_ext, f_ext, r_ext, cx_ext, f_mid, v_out, told):
@@ -282,6 +282,8 @@
     cz_row = cz[...]
     told[0:16] = below[64:80]
     told[16:32] = above[64:80]
+    told[32:40] = right[80:88]
+    told[40:48] = left[80:88]
     planes = []
     for j in range(6):
         side = (below, u, above)[j // 2]
@@ -327,7 +329,7 @@
     applied = operate(own, near_x(own), below[...] + above[...], rho, cx, cy, cz)
     scaled = (f_mid[...] - applied) / diagonal(rho, cx, cy, cz)
     part = roll(scaled, -MH, 0)[0:MX]
-    for i in range(N_PX):
+    for i in range(out.shape[0]):
         out[i] = part
 
 
@@ -348,6 +350,32 @@
     out[...] = v[...] + jnp.where(inside_middle(px), part, 0.0)
 
 
+def solve_x_block(px, py, gathered, lines, v, out):
+    total = MX * N_PX
+    pieces = []
+    starts = (
+        (jnp.maximum(MX * px - 8, 0), 8),
+        (MX * px, MX),
+        (jnp.minimum(MX * px + MX, total - 8), 8),
+    )
+    for start, size in starts:
+        pieces.append(dyn(lines, start, size))
+    full = dot(jnp.concatenate(pieces, axis=0), gathered[...])
+    part = roll(full, MH - 8, 0)[0:ME]
+    row = iota((ME, MZ), 0) + MX * px - MH
+    first = 256 * (px // 16)
+    held = (row >= first) & (row < first + 256)
+    out[...] = jnp.where(held, v[...] + part, 0.0)
+
+
+def mend(px, py, v, other, out):
+    row = iota((ME, MZ), 0)
+    theirs = other[...]
+    up = jnp.where((row >= MH + MX) & (px == 15), roll(theirs, MX, 0), 0.0)
+    down = jnp.where((row < MH) & (px == 16), roll(theirs, -MX, 0), 0.0)
+    out[...] = v[...] + (up + down)
+
+
 def block_mean(px, py, v, f_mid, r_mid, cx_mid, cyz_mid, told, column, out):
     rho, cx, cy, cz = middle_parts(r_mid, cx_mid, cyz_mid)
     own = v[...]
@@ -364,6 +392,11 @@
         share = mean(told[at : at + 8, 0:MZ] * inner[0:8] + told[at : at + 8, MZ:FZ] * inner[8:16])
         share = share * told[at + 8 : at + 9, MZ : MZ + 1]
         theirs = [told[at + 8 : at + 16, 128 * k : 128 * (k + 1)] for k in range(4)]
+        sent = sent + jnp.concatenate(theirs, axis=0) * share
+    for at, edge, inner_row, mine in ((32, MH + MX, MH + MX - 1, px == 15), (40, MH - 1, MH, px == 16)):
+        line = r_mid[edge : edge + 1] * cx_mid[edge : edge + 1, 0:1] * v[inner_row : inner_row + 1]
+        share = jnp.where(mine, mean(line), 0.0)
+        theirs = [told[at : at + 8, 128 * k : 128 * (k + 1)] for k in range(4)]
         sent = sent + jnp.concatenate(theirs, axis=0) * share
     for i in range(N_PX):
         out[i] = jnp.broadcast_to(sent[i : i + 1], (8, 128))
@@ -467,7 +500,6 @@
             in_specs=[whole] * len(args),
             out_specs=[whole] * len(shapes),
             compiler_params=pltpu.CompilerParams(vmem_limit_bytes=24 * 1024 * 1024),
-            name=stage.__name__,
         )(*args)
         return outs if len(shapes) > 1 else outs[0]
 
@@ -483,6 +515,9 @@
         up = [(i, i + 1) for i in range(n - 1)]
         down = [(j, i) for i, j in up]
         return lax.ppermute(high, axis, up), lax.ppermute(low, axis, down)
+
+    def across(self, array):
+        return lax.ppermute(array, "px", [(15, 16), (16, 15)])
 
     def swap(self, axis, array, group):
         n = lax.axis_size(axis)
@@ -531,24 +566,26 @@
     slabs = d.swap("px", slabs, 8)
     u = d.run(add_slabs, [(80, FZ)], u, slabs, told)
     below, above = d.beside("py", u, u)
-    low, high = d.run(pack_u, [(80, FZ)] * 2, u, below, above, y_below, y_above)
+    low, high = d.run(pack_u, [(88, FZ)] * 2, u, below, above, y_below, y_above)
     left, right = d.beside("px", low, high)
     u_ext, f_ext, r_ext, cx_ext, f_mid, v, told = d.run(
         to_middle,
-        [(4, FE, FZ), (2, FE, FZ), (2, FE, FZ), (FE, 128), mid, mid, (32, FZ)],
+        [(4, FE, FZ), (2, FE, FZ), (2, FE, FZ), (FE, 128), mid, mid, (48, FZ)],
         u, below, above, left, right, force, rho, y_below, y_above, x_left, x_right,
         cx, sy, cz, r_mid, cx_mid, cyz_mid, lines_z1,
     )
     statics = (f_mid, r_mid, cx_mid, cyz_mid)
 
     below, above = d.beside("py", v, v)
-    every = d.run(middle_scaled, [(N_PX, MX, MZ)], v, below, above, *statics)
-    every = d.swap("px", every, N_PX)
-    every = d.local(lambda a: a.reshape(MX * N_PX, MZ), every)
-    v = d.run(solve_x_middle, [mid], every, rows_x1, v)
-    below, above = d.beside("py", v, v)
+    every = d.run(middle_scaled, [(16, MX, MZ)], v, below, above, *statics)
+    every = d.swap("px", every, 16)
+    every = d.local(lambda a: a.reshape(256, MZ), every)
+    v = d.run(solve_x_block, [mid], every, rows_x1, v)
+    other = d.across(v)
     sent = d.run(block_mean, [(N_PX, 8, 128)], v, *statics, told, column)
     parts = d.swap("px", sent, N_PX)
+    v = d.run(mend, [mid], v, other)
+    below, above = d.beside("py", v, v)
     parts = d.run(sum_x, [(N_PY, 8, 128)], parts)
     parts = d.swap("py", parts, N_PY)
     v = d.run(second_half, [mid], parts, v, below, above, *statics, lines_z1)
@@ -585,10 +622,10 @@
         P(),
         P(("py", "px"), None),
     )
+
+    def step(*args):
+        return cycle(Device(), *args)
+
     return jax.shard_map(
-        functools.partial(cycle, Device()),
-        mesh=mesh,
-        in_specs=placed,
-        out_specs=P("px", "py", None),
-        check_vma=False,
-    )
+        step, mesh=mesh, in_specs=placed, out_specs=P("px", "py", None), check_vma=False
+    )

time: 277 us -> 273 us (0.986)
  blocking collectives: 118 us -> 113 us
    all_to_all x5, blocking collectives: 118 us -> 113 us  [swap(): lax.all_to_all(array, axis, 0, 0, axis_index_groups=groups, tiled=True)]
    pallas_call x19 -> x20, Pallas kernels: 10.7 us -> 10.5 us  [run(): pl.pallas_call(kernel, out_shape=[jax.ShapeDtypeStruct(s, f32) for s in s...]
  transfers between devices with their start and end apart: 21 -> 22, of which waited for: 14 -> 14; matrix products, arithmetic and copies ran while one was open for 1% -> 1% of each run, Pallas kernels for 0% -> 0%
where the time goes in v3:
time: 273 us; the launch traced here: 272 us
  blocking collectives  113 us (41%)
  waiting for transfers between devices  75.8 us (28%)
  starting transfers between devices  60.5 us (22%)
  local copies, waits for them, and re-layouts  10.6 us (4%)
  Pallas kernels  10.5 us (4%)
    all_to_all x5, blocking collectives, swap(): lax.all_to_all(array, axis, 0, 0, axis_index_groups=groups, tiled=True)  113 us
    ppermute x18, waiting for transfers between devices, beside(): return (lax.ppermute(high, axis, up), lax.ppermute(low, axis, down))  60.2 us
    ppermute x18, starting transfers between devices, beside(): return (lax.ppermute(high, axis, up), lax.ppermute(low, axis, down))  45.5 us
    all_to_all x3, waiting for transfers between devices, swap(): lax.all_to_all(array, axis, 0, 0, axis_index_groups=groups, tiled=True)  15.6 us
    all_to_all x3, starting transfers between devices, swap(): lax.all_to_all(array, axis, 0, 0, axis_index_groups=groups, tiled=True)  14.3 us
    pallas_call x20, Pallas kernels, run(): pl.pallas_call(kernel, out_shape=[jax.ShapeDtypeStruct(s, f32) for s in s...  10.5 us
    unnamed x73, local copies, waits for them, and re-layouts  10.4 us
  transfers between devices with their start and end apart: 22, of which 14 were waited for; matrix products, arithmetic and copies ran while one was open for 1% of the time, Pallas kernels for 0%

profile of v3, /device:TPU:2, one launch (start us, length us, event | category | flops | bytes accessed | tf_op | source)
XLA Modules:
  0.0 271.8 jit_solution(17145367852743053670)
XLA Ops:
  2.8 1.9 collective-permute-start
  4.7 4.5 %collective-permute-start.1 = (f32[72,1024]{1,0:T(8,128)S(1)}, f32[72,1024]{1,0:T(8,128)S(1)}, u32[]{:S(2)}, u32[]{:S(2)}) collective-permute-start(f32[72,1024]{1,0:T(8,128)S(1)} %get-tuple-element.32), channel_id=1, source_target_pairs={{32,0},{64,32},{96,64},{128,96},{160,128},{192,160},{224,192},{256... | collective-permute-start | bytes 884744 | tf_op jit(solution)/shard_map/ppermute | solution.py:517
  9.3 6.1 %collective-permute-start.2 = (f32[40,1024]{1,0:T(8,128)S(1)}, f32[40,1024]{1,0:T(8,128)S(1)}, u32[]{:S(2)}, u32[]{:S(2)}) collective-permute-start(f32[40,1024]{1,0:T(8,128)S(1)} %get-tuple-element.33), channel_id=1, source_target_pairs={{0,1},{1,2},{2,3},{3,4},{4,5},{5,6},{6,7},{7,8},{8,9},{9,10},{10,1... | collective-permute-start | bytes 491528 | tf_op jit(solution)/shard_map/ppermute | solution.py:517
  18.9 11.5 %collective-permute-done.3.refs_9_.refs_5_.refs_10_ = f32[40,1024]{1,0:T(8,128)S(1)} collective-permute-done((f32[40,1024]{1,0:T(8,128)S(1)}, f32[40,1024]{1,0:T(8,128)S(1)}, u32[]{:S(2)}, u32[]{:S(2)}) %collective-permute-start.3) | collective-permute-done | bytes 163872 | tf_op jit(solution)/shard_map/ppermute | solution.py:517
  31.8 5.2 %all-to-all-start = ((f32[8,2,32,128]{3,2,1,0:T(8,128)}), f32[8,2,32,128]{3,2,1,0:T(8,128)S(1)}, u32[]{:S(2)}, u32[]{:S(2)}) async-start(f32[8,2,32,128]{3,2,1,0:T(8,128)} %shard_map.102), calls=%async_computation | async-start | bytes 524288 | tf_op jit(solution)/shard_map/all_to_all | solution.py:527
  37.1 9.6 %all-to-all-done.refs_0_ = f32[8,2,32,128]{3,2,1,0:T(8,128)S(1)} async-done(((f32[8,2,32,128]{3,2,1,0:T(8,128)}), f32[8,2,32,128]{3,2,1,0:T(8,128)S(1)}, u32[]{:S(2)}, u32[]{:S(2)}) %all-to-all-start) | async-done | bytes 262176 | tf_op jit(solution)/shard_map/all_to_all | solution.py:527
  47.8 4.5 %all-to-all-start.1 = ((f32[8,2,32,128]{3,2,1,0:T(8,128)}), f32[8,2,32,128]{3,2,1,0:T(8,128)S(1)}, u32[]{:S(2)}, u32[]{:S(2)}) async-start(f32[8,2,32,128]{3,2,1,0:T(8,128)} %copy-done.9), calls=%async_computation.1 | async-start | bytes 524288 | tf_op jit(solution)/shard_map/all_to_all | solution.py:527
  56.0 6.0 %all-to-all-done.1.refs_1_ = f32[8,2,32,128]{3,2,1,0:T(8,128)S(1)} async-done(((f32[8,2,32,128]{3,2,1,0:T(8,128)}), f32[8,2,32,128]{3,2,1,0:T(8,128)S(1)}, u32[]{:S(2)}, u32[]{:S(2)}) %all-to-all-start.1) | async-done | bytes 262176 | tf_op jit(solution)/shard_map/all_to_all | solution.py:527
  62.1 2.1 collective-permute-start.5
  64.1 2.4 collective-permute-start.4
  66.6 2.2 collective-permute-done.5.refs_2_
  68.7 9.2 %collective-permute-done.4.refs_1_ = f32[80,1024]{1,0:T(8,128)S(1)} collective-permute-done((f32[80,1024]{1,0:T(8,128)S(1)}, f32[80,1024]{1,0:T(8,128)S(1)}, u32[]{:S(2)}, u32[]{:S(2)}) %collective-permute-start.4) | collective-permute-done | bytes 327712 | tf_op jit(solution)/shard_map/ppermute | solution.py:517
  80.6 3.6 %collective-permute-done.6.refs_3_ = f32[88,1024]{1,0:T(8,128)S(1)} collective-permute-done((f32[88,1024]{1,0:T(8,128)S(1)}, f32[88,1024]{1,0:T(8,128)S(1)}, u32[]{:S(2)}, u32[]{:S(2)}) %collective-permute-start.6) | collective-permute-done | bytes 360480 | tf_op jit(solution)/shard_map/ppermute | solution.py:517
  84.2 14.9 %collective-permute-done.7.refs_4_ = f32[88,1024]{1,0:T(8,128)S(1)} collective-permute-done((f32[88,1024]{1,0:T(8,128)S(1)}, f32[88,1024]{1,0:T(8,128)S(1)}, u32[]{:S(2)}, u32[]{:S(2)}) %collective-permute-start.7) | collective-permute-done | bytes 360480 | tf_op jit(solution)/shard_map/ppermute | solution.py:517
  105.0 2.4 collective-permute-start.8
  107.5 3.9 %collective-permute-done.8.refs_1_ = f32[24,512]{1,0:T(8,128)S(1)} collective-permute-done((f32[24,512]{1,0:T(8,128)S(1)}, f32[24,512]{1,0:T(8,128)S(1)}, u32[]{:S(2)}, u32[]{:S(2)}) %collective-permute-start.8) | collective-permute-done | bytes 49184 | tf_op jit(solution)/shard_map/ppermute | solution.py:517
  111.5 24.0 %all_to_all.40 = f32[16,16,512]{2,1,0:T(8,128)S(1)} all-to-all(f32[16,16,512]{2,1,0:T(8,128)S(1)} %shard_map.108), channel_id=1, replica_groups={{0,1,2,3,4,5,6,7,8,9,10,11,12,13,14,15},{16,17,18,19,20,21,22,23,24,25,..., dimensions={0} | all-to-all | bytes 1048576 | tf_op jit(solution)/shard_map/all_to_all | solution.py:527
  136.5 18.0 %all_to_all.41.refs_0_ = f32[32,8,128]{2,1,0:T(8,128)S(1)} all-to-all(f32[32,8,128]{2,1,0:T(8,128)S(1)} %shard_map.110), channel_id=1, replica_groups=mesh['py'=16,'px'=32] {'px'}, dimensions={0} | all-to-all | bytes 262144 | tf_op jit(solution)/shard_map/all_to_all | solution.py:527
  155.2 4.5 %all-to-all-start.4 = ((f32[16,8,128]{2,1,0:T(8,128)}), f32[16,8,128]{2,1,0:T(8,128)S(1)}, u32[]{:S(2)}, u32[]{:S(2)}) async-start(f32[16,8,128]{2,1,0:T(8,128)} %shard_map.111), calls=%async_computation.4 | async-start | bytes 131072 | tf_op jit(solution)/shard_map/all_to_all | solution.py:527
  160.6 3.1 %collective-permute-start.12 = (f32[24,512]{1,0:T(8,128)S(1)}, f32[24,512]{1,0:T(8,128)S(1)}, u32[]{:S(2)}, u32[]{:S(2)}) collective-permute-start(f32[24,512]{1,0:T(8,128)S(1)} %shard_map.112.refs_1_), channel_id=1, source_target_pairs={{32,0},{64,32},{96,64},{128,96},{160,128},{192,160},{224,192},{256... | collective-permute-start | bytes 147464 | tf_op jit(solution)/shard_map/ppermute | solution.py:517
  163.7 1.9 collective-permute-start.11
  165.6 4.4 %collective-permute-done.11.refs_2_ = f32[24,512]{1,0:T(8,128)S(1)} collective-permute-done((f32[24,512]{1,0:T(8,128)S(1)}, f32[24,512]{1,0:T(8,128)S(1)}, u32[]{:S(2)}, u32[]{:S(2)}) %collective-permute-start.11) | collective-permute-done | bytes 49184 | tf_op jit(solution)/shard_map/ppermute | solution.py:517
  170.4 1.9 collective-permute-start.14
  172.4 2.4 collective-permute-start.13
  174.8 3.9 %collective-permute-done.13.refs_1_ = f32[24,512]{1,0:T(8,128)S(1)} collective-permute-done((f32[24,512]{1,0:T(8,128)S(1)}, f32[24,512]{1,0:T(8,128)S(1)}, u32[]{:S(2)}, u32[]{:S(2)}) %collective-permute-start.13) | collective-permute-done | bytes 49184 | tf_op jit(solution)/shard_map/ppermute | solution.py:517
  178.9 39.6 %all_to_all.42 = f32[32,16,512]{2,1,0:T(8,128)S(1)} all-to-all(f32[32,16,512]{2,1,0:T(8,128)S(1)} %shard_map.114), channel_id=1, replica_groups=mesh['py'=16,'px'=32] {'px'}, dimensions={0} | all-to-all | bytes 2097152 | tf_op jit(solution)/shard_map/all_to_all | solution.py:527
  219.0 2.0 collective-permute-start.16
  221.0 2.4 collective-permute-start.15
  223.4 3.9 %collective-permute-done.15.refs_1_ = f32[24,512]{1,0:T(8,128)S(1)} collective-permute-done((f32[24,512]{1,0:T(8,128)S(1)}, f32[24,512]{1,0:T(8,128)S(1)}, u32[]{:S(2)}, u32[]{:S(2)}) %collective-permute-start.15) | collective-permute-done | bytes 49184 | tf_op jit(solution)/shard_map/ppermute | solution.py:517
  231.7 4.5 %collective-permute-start.18 = (f32[32,1024]{1,0:T(8,128)S(1)}, f32[32,1024]{1,0:T(8,128)S(1)}, u32[]{:S(2)}, u32[]{:S(2)}) collective-permute-start(f32[32,1024]{1,0:T(8,128)S(1)} %get-tuple-element.50), channel_id=1, source_target_pairs={{32,0},{64,32},{96,64},{128,96},{160,128},{192,160},{224,192},{256... | collective-permute-start | bytes 393224 | tf_op jit(solution)/shard_map/ppermute | solution.py:517
  239.1 17.3 %all_to_all.43.refs_0_ = f32[8,2,32,128]{3,2,1,0:T(8,128)S(1)} all-to-all(f32[8,2,32,128]{3,2,1,0:T(8,128)S(1)} %shard_map.117), channel_id=1, replica_groups={{0,1,2,3,4,5,6,7},{8,9,10,11,12,13,14,15},{16,17,18,19,20,21,22,23},{24..., dimensions={0} | all-to-all | bytes 524288 | tf_op jit(solution)/shard_map/all_to_all | solution.py:527
  256.8 14.2 %all_to_all.44.refs_1_ = f32[8,2,32,128]{3,2,1,0:T(8,128)S(1)} all-to-all(f32[8,2,32,128]{3,2,1,0:T(8,128)S(1)} %shard_map.118), channel_id=1, replica_groups={{0,1,2,3,4,5,6,7},{8,9,10,11,12,13,14,15},{16,17,18,19,20,21,22,23},{24..., dimensions={0} | all-to-all | bytes 524288 | tf_op jit(solution)/shard_map/all_to_all | solution.py:527
  (118 shorter events, 33.1 us)
Async XLA Ops:
  0.0 37.1 %copy-start = (f32[4,256,256]{2,1,0:T(8,128)S(1)}, f32[4,256,256]{2,1,0:T(8,128)}, u32[]{:S(2)}) copy-start(f32[4,256,256]{2,1,0:T(8,128)} %param.16) | copy-start | bytes 3145732
  2.8 50.9 %copy-start.20 = (f32[32,128]{1,0:T(8,128)}, f32[32,128]{1,0:T(8,128)S(1)}, u32[]{:S(2)}) copy-start(f32[32,128]{1,0:T(8,128)S(1)} %get-tuple-element.30.refs_2_.refs_1_.refs_11_) | copy-start | bytes 49156
  2.8 27.5 %collective-permute-start = (f32[72,1024]{1,0:T(8,128)S(1)}, f32[72,1024]{1,0:T(8,128)S(1)}, u32[]{:S(2)}, u32[]{:S(2)}) collective-permute-start(f32[72,1024]{1,0:T(8,128)S(1)} %get-tuple-element.31), channel_id=1, source_target_pairs={{0,32},{32,64},{64,96},{96,128},{128,160},{160,192},{192,224},{224... | collective-permute-start | bytes 884744 | tf_op jit(solution)/shard_map/ppermute | solution.py:517
  4.7 25.6 %collective-permute-start.1 = (f32[72,1024]{1,0:T(8,128)S(1)}, f32[72,1024]{1,0:T(8,128)S(1)}, u32[]{:S(2)}, u32[]{:S(2)}) collective-permute-start(f32[72,1024]{1,0:T(8,128)S(1)} %get-tuple-element.32), channel_id=1, source_target_pairs={{32,0},{64,32},{96,64},{128,96},{160,128},{192,160},{224,192},{256... | collective-permute-start | bytes 884744 | tf_op jit(solution)/shard_map/ppermute | solution.py:517
  9.3 9.6 %collective-permute-start.2 = (f32[40,1024]{1,0:T(8,128)S(1)}, f32[40,1024]{1,0:T(8,128)S(1)}, u32[]{:S(2)}, u32[]{:S(2)}) collective-permute-start(f32[40,1024]{1,0:T(8,128)S(1)} %get-tuple-element.33), channel_id=1, source_target_pairs={{0,1},{1,2},{2,3},{3,4},{4,5},{5,6},{6,7},{7,8},{8,9},{9,10},{10,1... | collective-permute-start | bytes 491528 | tf_op jit(solution)/shard_map/ppermute | solution.py:517
  15.4 14.9 %collective-permute-start.3 = (f32[40,1024]{1,0:T(8,128)S(1)}, f32[40,1024]{1,0:T(8,128)S(1)}, u32[]{:S(2)}, u32[]{:S(2)}) collective-permute-start(f32[40,1024]{1,0:T(8,128)S(1)} %get-tuple-element.34), channel_id=1, source_target_pairs={{1,0},{2,1},{3,2},{4,3},{5,4},{6,5},{7,6},{8,7},{9,8},{10,9},{11,1... | collective-permute-start | bytes 491528 | tf_op jit(solution)/shard_map/ppermute | solution.py:517
  30.4 23.3 %copy-start.7 = (f32[40,1024]{1,0:T(8,128)}, f32[40,1024]{1,0:T(8,128)S(1)}, u32[]{:S(2)}) copy-start(f32[40,1024]{1,0:T(8,128)S(1)} %collective-permute-done.3.refs_9_.refs_5_.refs_10_) | copy-start | bytes 491524
  31.8 14.9 %all-to-all-start = ((f32[8,2,32,128]{3,2,1,0:T(8,128)}), f32[8,2,32,128]{3,2,1,0:T(8,128)S(1)}, u32[]{:S(2)}, u32[]{:S(2)}) async-start(f32[8,2,32,128]{3,2,1,0:T(8,128)} %shard_map.102), calls=%async_computation | async-start | bytes 524288 | tf_op jit(solution)/shard_map/all_to_all | solution.py:527
  47.8 14.3 %all-to-all-start.1 = ((f32[8,2,32,128]{3,2,1,0:T(8,128)}), f32[8,2,32,128]{3,2,1,0:T(8,128)S(1)}, u32[]{:S(2)}, u32[]{:S(2)}) async-start(f32[8,2,32,128]{3,2,1,0:T(8,128)} %copy-done.9), calls=%async_computation.1 | async-start | bytes 524288 | tf_op jit(solution)/shard_map/all_to_all | solution.py:527
  62.1 37.1 %copy-start.4 = (f32[2,256,256]{2,1,0:T(8,128)S(1)}, f32[2,256,256]{2,1,0:T(8,128)}, u32[]{:S(2)}) copy-start(f32[2,256,256]{2,1,0:T(8,128)} %refs_8_.1) | copy-start | bytes 1572868
  62.1 37.1 %copy-start.8 = (f32[40,1024]{1,0:T(8,128)S(1)}, f32[40,1024]{1,0:T(8,128)}, u32[]{:S(2)}) copy-start(f32[40,1024]{1,0:T(8,128)} %copy-done.7) | copy-start | bytes 491524
  62.1 6.6 %collective-permute-start.5 = (f32[80,1024]{1,0:T(8,128)S(1)}, f32[80,1024]{1,0:T(8,128)S(1)}, u32[]{:S(2)}, u32[]{:S(2)}) collective-permute-start(f32[80,1024]{1,0:T(8,128)S(1)} %shard_map.105.refs_0_), channel_id=1, source_target_pairs={{32,0},{64,32},{96,64},{128,96},{160,128},{192,160},{224,192},{256... | collective-permute-start | bytes 983048 | tf_op jit(solution)/shard_map/ppermute | solution.py:517
  64.1 13.7 %collective-permute-start.4 = (f32[80,1024]{1,0:T(8,128)S(1)}, f32[80,1024]{1,0:T(8,128)S(1)}, u32[]{:S(2)}, u32[]{:S(2)}) collective-permute-start(f32[80,1024]{1,0:T(8,128)S(1)} %shard_map.105.refs_0_), channel_id=1, source_target_pairs={{0,32},{32,64},{64,96},{96,128},{128,160},{160,192},{192,224},{224... | collective-permute-start | bytes 983048 | tf_op jit(solution)/shard_map/ppermute | solution.py:517
  77.9 21.3 %copy-start.18 = (f32[24,128]{1,0:T(8,128)S(1)}, f32[24,128]{1,0:T(8,128)}, u32[]{:S(2)}) copy-start(f32[24,128]{1,0:T(8,128)} %copy-done.17) | copy-start | bytes 36868
  77.9 21.3 %copy-start.21 = (f32[32,128]{1,0:T(8,128)S(1)}, f32[32,128]{1,0:T(8,128)}, u32[]{:S(2)}) copy-start(f32[32,128]{1,0:T(8,128)} %copy-done.20) | copy-start | bytes 49156
  77.9 6.3 %collective-permute-start.6 = (f32[88,1024]{1,0:T(8,128)S(1)}, f32[88,1024]{1,0:T(8,128)S(1)}, u32[]{:S(2)}, u32[]{:S(2)}) collective-permute-start(f32[88,1024]{1,0:T(8,128)S(1)} %get-tuple-element.36), channel_id=1, source_target_pairs={{0,1},{1,2},{2,3},{3,4},{4,5},{5,6},{6,7},{7,8},{8,9},{9,10},{10,1... | collective-permute-start | bytes 1081352 | tf_op jit(solution)/shard_map/ppermute | solution.py:517
  79.3 19.9 %collective-permute-start.7 = (f32[88,1024]{1,0:T(8,128)S(1)}, f32[88,1024]{1,0:T(8,128)S(1)}, u32[]{:S(2)}, u32[]{:S(2)}) collective-permute-start(f32[88,1024]{1,0:T(8,128)S(1)} %get-tuple-element.37), channel_id=1, source_target_pairs={{1,0},{2,1},{3,2},{4,3},{5,4},{6,5},{7,6},{8,7},{9,8},{10,9},{11,1... | collective-permute-start | bytes 1081352 | tf_op jit(solution)/shard_map/ppermute | solution.py:517
  103.1 32.7 %copy-start.10 = (f32[24,512]{1,0:T(8,128)}, f32[24,512]{1,0:T(8,128)S(1)}, u32[]{:S(2)}) copy-start(f32[24,512]{1,0:T(8,128)S(1)} %get-tuple-element.42.refs_3_.refs_1_.refs_4_) | copy-start | bytes 147460
  103.1 4.3 %collective-permute-start.9 = (f32[24,512]{1,0:T(8,128)S(1)}, f32[24,512]{1,0:T(8,128)S(1)}, u32[]{:S(2)}, u32[]{:S(2)}) collective-permute-start(f32[24,512]{1,0:T(8,128)S(1)} %get-tuple-element.41.refs_0_.refs_2_), channel_id=1, source_target_pairs={{32,0},{64,32},{96,64},{128,96},{160,128},{192,160},{224,192},{256... | collective-permute-start | bytes 147464 | tf_op jit(solution)/shard_map/ppermute | solution.py:517
  105.0 6.3 %collective-permute-start.8 = (f32[24,512]{1,0:T(8,128)S(1)}, f32[24,512]{1,0:T(8,128)S(1)}, u32[]{:S(2)}, u32[]{:S(2)}) collective-permute-start(f32[24,512]{1,0:T(8,128)S(1)} %get-tuple-element.41.refs_0_.refs_2_), channel_id=1, source_target_pairs={{0,32},{32,64},{64,96},{96,128},{128,160},{160,192},{192,224},{224... | collective-permute-start | bytes 147464 | tf_op jit(solution)/shard_map/ppermute | solution.py:517
  111.5 24.1 %copy-start.3 = (f32[2,256,256]{2,1,0:T(8,128)S(1)}, f32[2,256,256]{2,1,0:T(8,128)}, u32[]{:S(2)}) copy-start(f32[2,256,256]{2,1,0:T(8,128)} %param.18) | copy-start | bytes 1572868
  155.2 14.8 %all-to-all-start.4 = ((f32[16,8,128]{2,1,0:T(8,128)}), f32[16,8,128]{2,1,0:T(8,128)S(1)}, u32[]{:S(2)}, u32[]{:S(2)}) async-start(f32[16,8,128]{2,1,0:T(8,128)} %shard_map.111), calls=%async_computation.4 | async-start | bytes 131072 | tf_op jit(solution)/shard_map/all_to_all | solution.py:527
  159.7 0.8 collective-permute-start.10
  160.6 5.0 %collective-permute-start.12 = (f32[24,512]{1,0:T(8,128)S(1)}, f32[24,512]{1,0:T(8,128)S(1)}, u32[]{:S(2)}, u32[]{:S(2)}) collective-permute-start(f32[24,512]{1,0:T(8,128)S(1)} %shard_map.112.refs_1_), channel_id=1, source_target_pairs={{32,0},{64,32},{96,64},{128,96},{160,128},{192,160},{224,192},{256... | collective-permute-start | bytes 147464 | tf_op jit(solution)/shard_map/ppermute | solution.py:517
  163.7 6.3 %collective-permute-start.11 = (f32[24,512]{1,0:T(8,128)S(1)}, f32[24,512]{1,0:T(8,128)S(1)}, u32[]{:S(2)}, u32[]{:S(2)}) collective-permute-start(f32[24,512]{1,0:T(8,128)S(1)} %shard_map.112.refs_1_), channel_id=1, source_target_pairs={{0,32},{32,64},{64,96},{96,128},{128,160},{160,192},{192,224},{224... | collective-permute-start | bytes 147464 | tf_op jit(solution)/shard_map/ppermute | solution.py:517
  170.4 4.3 %collective-permute-start.14 = (f32[24,512]{1,0:T(8,128)S(1)}, f32[24,512]{1,0:T(8,128)S(1)}, u32[]{:S(2)}, u32[]{:S(2)}) collective-permute-start(f32[24,512]{1,0:T(8,128)S(1)} %shard_map.113.refs_0_.refs_2_), channel_id=1, source_target_pairs={{32,0},{64,32},{96,64},{128,96},{160,128},{192,160},{224,192},{256... | collective-permute-start | bytes 147464 | tf_op jit(solution)/shard_map/ppermute | solution.py:517
  172.4 6.3 %collective-permute-start.13 = (f32[24,512]{1,0:T(8,128)S(1)}, f32[24,512]{1,0:T(8,128)S(1)}, u32[]{:S(2)}, u32[]{:S(2)}) collective-permute-start(f32[24,512]{1,0:T(8,128)S(1)} %shard_map.113.refs_0_.refs_2_), channel_id=1, source_target_pairs={{0,32},{32,64},{64,96},{96,128},{128,160},{160,192},{192,224},{224... | collective-permute-start | bytes 147464 | tf_op jit(solution)/shard_map/ppermute | solution.py:517
  178.9 48.4 %copy-start.13 = (f32[4,48,1024]{2,1,0:T(8,128)S(1)}, f32[4,48,1024]{2,1,0:T(8,128)}, u32[]{:S(2)}) copy-start(f32[4,48,1024]{2,1,0:T(8,128)} %copy-done.12) | copy-start | bytes 2359300
  219.0 4.5 %collective-permute-start.16 = (f32[24,512]{1,0:T(8,128)S(1)}, f32[24,512]{1,0:T(8,128)S(1)}, u32[]{:S(2)}, u32[]{:S(2)}) collective-permute-start(f32[24,512]{1,0:T(8,128)S(1)} %shard_map.115.refs_0_), channel_id=1, source_target_pairs={{32,0},{64,32},{96,64},{128,96},{160,128},{192,160},{224,192},{256... | collective-permute-start | bytes 147464 | tf_op jit(solution)/shard_map/ppermute | solution.py:517
  221.0 6.3 %collective-permute-start.15 = (f32[24,512]{1,0:T(8,128)S(1)}, f32[24,512]{1,0:T(8,128)S(1)}, u32[]{:S(2)}, u32[]{:S(2)}) collective-permute-start(f32[24,512]{1,0:T(8,128)S(1)} %shard_map.115.refs_0_), channel_id=1, source_target_pairs={{0,32},{32,64},{64,96},{96,128},{128,160},{160,192},{192,224},{224... | collective-permute-start | bytes 147464 | tf_op jit(solution)/shard_map/ppermute | solution.py:517
  229.7 7.2 %collective-permute-start.17 = (f32[32,1024]{1,0:T(8,128)S(1)}, f32[32,1024]{1,0:T(8,128)S(1)}, u32[]{:S(2)}, u32[]{:S(2)}) collective-permute-start(f32[32,1024]{1,0:T(8,128)S(1)} %get-tuple-element.49), channel_id=1, source_target_pairs={{0,32},{32,64},{64,96},{96,128},{128,160},{160,192},{192,224},{224... | collective-permute-start | bytes 393224 | tf_op jit(solution)/shard_map/ppermute | solution.py:517
  231.7 7.0 %collective-permute-start.18 = (f32[32,1024]{1,0:T(8,128)S(1)}, f32[32,1024]{1,0:T(8,128)S(1)}, u32[]{:S(2)}, u32[]{:S(2)}) collective-permute-start(f32[32,1024]{1,0:T(8,128)S(1)} %get-tuple-element.50), channel_id=1, source_target_pairs={{32,0},{64,32},{96,64},{128,96},{160,128},{192,160},{224,192},{256... | collective-permute-start | bytes 393224 | tf_op jit(solution)/shard_map/ppermute | solution.py:517
  (26 other events, 133.8 us)

commit v4 on v3

--- a/solution.py
+++ b/solution.py
@@ -63,6 +63,22 @@
 
 def iota(shape, axis):
     return lax.broadcasted_iota(jnp.int32, shape, axis)
+
+
+def rows_of(rows):
+    at = iota((8, rows[0].shape[1]), 0)
+    total = jnp.zeros((8, rows[0].shape[1]), f32)
+    for i, row in enumerate(rows):
+        total = jnp.where(at == i, row, total)
+    return total
+
+
+def rows_at(pairs):
+    at = iota((8, pairs[0][1].shape[1]), 0)
+    total = jnp.zeros((8, pairs[0][1].shape[1]), f32)
+    for i, row in pairs:
+        total = jnp.where(at == i, row, total)
+    return total
 
 
 def near_z(v):
@@ -181,6 +197,7 @@
     column = jnp.sum(jnp.where(square, sx[...], 0.0), axis=1, keepdims=True)
     cx[...] = jnp.broadcast_to(column, (FX, 128))
     wide = jnp.broadcast_to(column, (FX, FZ))
+    edges = {}
     for at, out in ((0, lower), (1, upper)):
         f_plane, r_plane = forcing[:, at, :], inv_density[:, at, :]
         force[at] = f_plane
@@ -188,11 +205,12 @@
         out[0:32] = f_plane
         out[32:64] = r_plane
         out[64:72] = jnp.broadcast_to(sy[0:1, at : at + 1], (8, FZ))
-        for side, rows in ((low, slice(0, 8)), (high, slice(24, 32))):
-            side[8 * at : 8 * at + 8] = f_plane[rows]
-            side[16 + 8 * at : 24 + 8 * at] = r_plane[rows]
-    low[32:40] = wide[0:8]
-    high[32:40] = wide[24:32]
+        for row in (0, FX - 1):
+            edges[at, row] = (f_plane[row : row + 1], r_plane[row : row + 1])
+    for side, row, cut in ((low, 0, slice(0, 8)), (high, FX - 1, slice(24, 32))):
+        for k in range(2):
+            side[8 * k : 8 * k + 8] = rows_of([edges[0, row][k], edges[1, row][k]])
+        side[16:24] = wide[cut]
 
 
 def own_lines(px, py, force, rho, cx, sy, cz, lines, u):
@@ -210,15 +228,15 @@
     parts = []
     for side in (below, above):
         parts.append(side[0:32] / diagonal(side[32:64], cx_col, side[64:65], cz_row))
-    for side in (left, right):
-        for at in range(2):
-            cut, deep = slice(8 * at, 8 * at + 8), slice(16 + 8 * at, 24 + 8 * at)
-            parts.append(side[cut] / diagonal(side[deep], side[32:40, 0:1], sy[0:1, at : at + 1], cz_row))
+    cy_edge = jnp.where(iota((8, 1), 0) == 0, sy[0:1, 0:1], sy[0:1, 1:2])
+    for side, row in ((left, 23), (right, 16)):
+        parts.append(side[0:8] / diagonal(side[8:16], side[row : row + 1, 0:1], cy_edge, cz_row))
     solved = solve_z(jnp.concatenate(parts, axis=0), lines)
     planes = [solved[0:32], u[0], u[1], solved[32:64]]
     for at in range(2):
         own = u[at]
-        before, after = solved[64 + 8 * at : 72 + 8 * at], solved[80 + 8 * at : 88 + 8 * at]
+        before = rows_at([(7, solved[64 + at : 65 + at])])
+        after = rows_at([(0, solved[72 + at : 73 + at])])
         beside_x = near_x(jnp.concatenate([before, own, after], axis=0))[FH : FH + FX]
         beside_y = planes[at] + planes[at + 2]
         cy = sy[0:1, at : at + 1]
@@ -226,20 +244,15 @@
         to_slabs((force[at] - applied) / diagonal(rho[at], cx_col, cy, cz_row), slabs, at)
 
 
-def middle_statics(px, py, rho, cx, sy, cz, left, right, column, r_mid, cx_mid, cyz_mid, told):
-    total = None
-    for at in range(2):
-        deep = slice(16 + 8 * at, 24 + 8 * at)
-        plane = jnp.concatenate([left[deep], rho[at], right[deep]], axis=0)
-        total = plane if total is None else total + plane
-    dense = pair_columns(pair_rows(total), 0.125)
-    columns = jnp.concatenate([left[32:40, 0:128], cx[...], right[32:40, 0:128]], axis=0)
+def middle_statics(px, py, rho, cx, sy, cz, left, right, column, cx_mid, cyz_mid, told):
+    coarse, fine = iota((MX, FX), 0), iota((MX, FX), 1)
+    pairs = pick_left(jnp.where(fine // 2 == coarse, 1.0, 0.0), rho[0] + rho[1])
+    own = pair_columns(pairs, 0.125)
+    columns = jnp.concatenate([left[16:24, 0:128], cx[...], right[16:24, 0:128]], axis=0)
     cym = jnp.broadcast_to((sy[0:1, 0:1] + sy[0:1, 1:2]) * 0.125, (8, MZ))
     czm = pair_columns(jnp.broadcast_to(cz[...], (16, FZ)), 0.125)
-    r_mid[...] = dense
     cx_mid[...] = pair_rows(columns) * 0.125
     cyz_mid[...] = jnp.concatenate([czm[0:1], cym[0:7]], axis=0)
-    own = roll(dense, -MH, 0)[0:MX]
     told[0:8, 0:MZ] = own[0:8]
     told[0:8, MZ:FZ] = own[8:16]
     for k in range(4):
@@ -262,57 +275,72 @@
     out[64:80] = told[...]
 
 
-def pack_u(px, py, u, below, above, y_below, y_above, low, high):
-    for start_row, out in ((0, low), (24, high)):
-        rows = slice(start_row, start_row + 8)
-        next_rows = slice(32 + start_row, 40 + start_row)
-        for j, side in enumerate((below, u, above)):
-            out[16 * j : 16 * j + 8] = side[rows]
-            out[16 * j + 8 : 16 * j + 16] = side[next_rows]
-        for j, side in enumerate((y_below, y_above)):
-            out[48 + 16 * j : 56 + 16 * j] = side[rows]
-            out[56 + 16 * j : 64 + 16 * j] = side[next_rows]
-        out[80:88] = u[72:80]
-
-
-def to_middle(px, py, u, below, above, left, right, force, rho, y_below, y_above, x_left, x_right, cx, sy, cz, r_mid, cx_mid, cyz_mid, lines, u_ext, f_ext, r_ext, cx_ext, f_mid, v_out, told):
-    columns = jnp.concatenate([x_left[32:40, 0:128], cx[...], x_right[32:40, 0:128]], axis=0)
-    cx_ext[...] = columns
-    cx_col = columns[:, 0:1]
+def half_residual(px, py, u, below, above, force, rho, y_below, y_above, cx, sy, cz, q, low, high):
+    cx_col = cx[...][:, 0:1]
     cz_row = cz[...]
-    told[0:16] = below[64:80]
-    told[16:32] = above[64:80]
-    told[32:40] = right[80:88]
-    told[40:48] = left[80:88]
-    planes = []
-    for j in range(6):
-        side = (below, u, above)[j // 2]
-        own = side[FX * (j % 2) : FX * (j % 2) + FX]
-        planes.append(jnp.concatenate([left[8 * j : 8 * j + 8], own, right[8 * j : 8 * j + 8]], axis=0))
+    us = [below[0:32], below[32:64], u[0:32], u[32:64], above[0:32], above[32:64]]
+    fs = [y_below[0:32], force[0], force[1], y_above[0:32]]
+    rs = [y_below[32:64], rho[0], rho[1], y_above[32:64]]
+    cys = [y_below[64:65], sy[0:1, 0:1], sy[0:1, 1:2], y_above[64:65]]
+    row = iota((FX, FZ), 0)
     total = None
     for j in range(4):
-        if j in (1, 2):
-            at = j - 1
-            cut, deep = slice(8 * at, 8 * at + 8), slice(16 + 8 * at, 24 + 8 * at)
-            f_plane = jnp.concatenate([x_left[cut], force[at], x_right[cut]], axis=0)
-            r_plane = jnp.concatenate([x_left[deep], rho[at], x_right[deep]], axis=0)
-            f_ext[at] = f_plane
-            r_ext[at] = r_plane
-            cy = sy[0:1, at : at + 1]
-        else:
-            side, at = (y_below, 48) if j == 0 else (y_above, 64)
-            cut, deep = slice(at, at + 8), slice(at + 8, at + 16)
-            f_plane = jnp.concatenate([left[cut], side[0:32], right[cut]], axis=0)
-            r_plane = jnp.concatenate([left[deep], side[32:64], right[deep]], axis=0)
-            cy = side[64:65]
-        own = planes[j + 1]
-        u_ext[j] = own
-        applied = operate(own, near_x(own), planes[j] + planes[j + 2], r_plane, cx_col, cy, cz_row)
-        left_over = f_plane - applied
+        own = us[j + 1]
+        beside_x = jnp.where(row == 0, 0.0, roll(own, 1, 0)) + jnp.where(row == FX - 1, 0.0, roll(own, -1, 0))
+        left_over = fs[j] - operate(own, beside_x, us[j] + us[j + 2], rs[j], cx_col, cys[j], cz_row)
         if j in (1, 2):
             left_over = 3.0 * left_over
         total = left_over if total is None else total + left_over
-    rhs = restrict_columns(restrict_rows(total * 0.125))
+    total = total * 0.125
+    q[...] = total
+    for out, edge, step, cut in ((low, 0, 1, slice(0, 8)), (high, FX - 1, -1, slice(24, 32))):
+        out[0:8] = total[cut]
+        next_row = edge + step
+        picked = [us[j + 1][edge : edge + 1] for j in range(4)]
+        out[8:16] = rows_of(picked + [us[j + 1][next_row : next_row + 1] for j in range(4)])
+        out[16:24] = rows_of([rs[j][edge : edge + 1] for j in range(4)])
+        out[24:32, 0:MZ] = u[72:80, 0:MZ]
+        out[24:32, MZ:FZ] = u[64:72, 0:MZ] if edge == 0 else u[64:72, MZ:FZ]
+
+
+def to_middle(px, py, q, u, below, above, left, right, force, rho, y_below, y_above, x_left, x_right, cx, cx_mid, cyz_mid, lines, u_ext, f_ext, r_ext, cx_ext, r_mid, f_mid, v_out, told):
+    columns = jnp.concatenate([x_left[16:24, 0:128], cx[...], x_right[16:24, 0:128]], axis=0)
+    cx_ext[...] = columns
+    told[0:16] = below[64:80]
+    told[16:32] = above[64:80]
+    told[32:40] = right[24:32]
+    told[40:48] = left[24:32]
+    us = [below[32:64], u[0:32], u[32:64], above[0:32]]
+    rs = [y_below[32:64], rho[0], rho[1], y_above[32:64]]
+    cross = []
+    for side, row in ((left, 0), (right, FX - 1)):
+        inward = outward = None
+        for j in range(4):
+            weight = 0.375 if j in (1, 2) else 0.125
+            here = weight * rs[j][row : row + 1] * side[8 + j : 9 + j]
+            there = weight * side[16 + j : 17 + j] * us[j][row : row + 1]
+            inward = here if inward is None else inward + here
+            outward = there if outward is None else outward + there
+        at = FH + row
+        beyond = at - 1 if row == 0 else at + 1
+        cross.append((at, inward * columns[at : at + 1, 0:1]))
+        cross.append((beyond, outward * columns[beyond : beyond + 1, 0:1]))
+    total = jnp.concatenate([left[0:8], q[...], right[0:8]], axis=0)
+    line = iota((FE, FZ), 0)
+    for at, term in cross:
+        total = total + jnp.where(line == at, term, 0.0)
+    for j in range(4):
+        before = rows_at([(7, left[8 + j : 9 + j]), (6, left[12 + j : 13 + j])])
+        after = rows_at([(0, right[8 + j : 9 + j]), (1, right[12 + j : 13 + j])])
+        u_ext[j] = jnp.concatenate([before, us[j], after], axis=0)
+    for at in range(2):
+        for k, own, out in ((0, force, f_ext), (8, rho, r_ext)):
+            before = rows_at([(7, x_left[k + at : k + at + 1])])
+            after = rows_at([(0, x_right[k + at : k + at + 1])])
+            out[at] = jnp.concatenate([before, own[at], after], axis=0)
+    dense = [left[24:32, MZ:FZ], u[64:72, 0:MZ], u[64:72, MZ:FZ], right[24:32, MZ:FZ]]
+    r_mid[...] = roll(jnp.concatenate(dense, axis=0), MH - 8, 0)[0:ME]
+    rhs = restrict_columns(restrict_rows(total))
     rhs = jnp.where(inside_middle(px), rhs, 0.0)
     f_mid[...] = rhs
     diag = diagonal(*middle_parts(r_mid, cx_mid, cyz_mid))
@@ -544,7 +572,7 @@
 
     force, rho, lower, upper, low, high, cx = d.run(
         start,
-        [own, own, (72, FZ), (72, FZ), (40, FZ), (40, FZ), (FX, 128)],
+        [own, own, (72, FZ), (72, FZ), (24, FZ), (24, FZ), (FX, 128)],
         forcing, inv_density, sx, sy,
     )
     y_below, y_above = d.beside("py", lower, upper)
@@ -557,22 +585,25 @@
         force, rho, cx, sy, cz, u, y_below, y_above, x_left, x_right, lines_z0,
     )
     slabs = d.swap("px", slabs, 8)
-    r_mid, cx_mid, cyz_mid, told = d.run(
+    cx_mid, cyz_mid, told = d.run(
         middle_statics,
-        [mid, (ME, 128), (8, MZ), (16, FZ)],
+        [(ME, 128), (8, MZ), (16, FZ)],
         rho, cx, sy, cz, x_left, x_right, column,
     )
     slabs = d.run(solve_x_fine, [slab], slabs, block)
     slabs = d.swap("px", slabs, 8)
     u = d.run(add_slabs, [(80, FZ)], u, slabs, told)
     below, above = d.beside("py", u, u)
-    low, high = d.run(pack_u, [(88, FZ)] * 2, u, below, above, y_below, y_above)
+    q, low, high = d.run(
+        half_residual, [(FX, FZ)] * 3,
+        u, below, above, force, rho, y_below, y_above, cx, sy, cz,
+    )
     left, right = d.beside("px", low, high)
-    u_ext, f_ext, r_ext, cx_ext, f_mid, v, told = d.run(
+    u_ext, f_ext, r_ext, cx_ext, r_mid, f_mid, v, told = d.run(
         to_middle,
-        [(4, FE, FZ), (2, FE, FZ), (2, FE, FZ), (FE, 128), mid, mid, (48, FZ)],
-        u, below, above, left, right, force, rho, y_below, y_above, x_left, x_right,
-        cx, sy, cz, r_mid, cx_mid, cyz_mid, lines_z1,
+        [(4, FE, FZ), (2, FE, FZ), (2, FE, FZ), (FE, 128), mid, mid, mid, (48, FZ)],
+        q, u, below, above, left, right, force, rho, y_below, y_above, x_left, x_right,
+        cx, cx_mid, cyz_mid, lines_z1,
     )
     statics = (f_mid, r_mid, cx_mid, cyz_mid)
 

time: 273 us -> 260 us (0.952)
  waiting for transfers between devices: 75.8 us -> 59.5 us
  blocking collectives: 113 us -> 116 us
    ppermute x18, waiting for transfers between devices: 60.2 us -> 43.7 us  [beside(): return (lax.ppermute(high, axis, up), lax.ppermute(low, axis, down))]
    unnamed x73 -> x63, local copies, waits for them, and re-layouts: 10.4 us -> 8.29 us
  transfers between devices with their start and end apart: 22 -> 22, of which waited for: 14 -> 13; matrix products, arithmetic and copies ran while one was open for 1% -> 1% of each run, Pallas kernels for 0% -> 0%
where the time goes in v4:
time: 260 us; the launch traced here: 259 us
  blocking collectives  116 us (45%)
  starting transfers between devices  62.3 us (24%)
  waiting for transfers between devices  59.5 us (23%)
  Pallas kernels  11 us (4%)
  local copies, waits for them, and re-layouts  8.56 us (3%)
    all_to_all x5, blocking collectives, swap(): lax.all_to_all(array, axis, 0, 0, axis_index_groups=groups, tiled=True)  116 us
    ppermute x18, starting transfers between devices, beside(): return (lax.ppermute(high, axis, up), lax.ppermute(low, axis, down))  46.3 us
    ppermute x18, waiting for transfers between devices, beside(): return (lax.ppermute(high, axis, up), lax.ppermute(low, axis, down))  43.7 us
    all_to_all x3, waiting for transfers between devices, swap(): lax.all_to_all(array, axis, 0, 0, axis_index_groups=groups, tiled=True)  15.8 us
    all_to_all x3, starting transfers between devices, swap(): lax.all_to_all(array, axis, 0, 0, axis_index_groups=groups, tiled=True)  15.2 us
    pallas_call x20, Pallas kernels, run(): pl.pallas_call(kernel, out_shape=[jax.ShapeDtypeStruct(s, f32) for s in s...  11 us
    unnamed x63, local copies, waits for them, and re-layouts  8.29 us
  transfers between devices with their start and end apart: 22, of which 13 were waited for; matrix products, arithmetic and copies ran while one was open for 1% of the time, Pallas kernels for 0%

profile of v4, /device:TPU:2, one launch (start us, length us, event | category | flops | bytes accessed | tf_op | source)
XLA Modules:
  0.0 258.5 jit_solution(3560520318641494806)
XLA Ops:
  2.8 1.9 collective-permute-start
  4.7 4.5 %collective-permute-start.1 = (f32[72,1024]{1,0:T(8,128)S(1)}, f32[72,1024]{1,0:T(8,128)S(1)}, u32[]{:S(2)}, u32[]{:S(2)}) collective-permute-start(f32[72,1024]{1,0:T(8,128)S(1)} %get-tuple-element.33), channel_id=1, source_target_pairs={{32,0},{64,32},{96,64},{128,96},{160,128},{192,160},{224,192},{256... | collective-permute-start | bytes 884744 | tf_op jit(solution)/shard_map/ppermute | solution.py:545
  9.3 6.1 %collective-permute-start.2 = (f32[24,1024]{1,0:T(8,128)S(1)}, f32[24,1024]{1,0:T(8,128)S(1)}, u32[]{:S(2)}, u32[]{:S(2)}) collective-permute-start(f32[24,1024]{1,0:T(8,128)S(1)} %get-tuple-element.34), channel_id=1, source_target_pairs={{0,1},{1,2},{2,3},{3,4},{4,5},{5,6},{6,7},{7,8},{8,9},{9,10},{10,1... | collective-permute-start | bytes 294920 | tf_op jit(solution)/shard_map/ppermute | solution.py:545
  18.6 8.7 %collective-permute-done.3.refs_9_.refs_5_.refs_11_ = f32[24,1024]{1,0:T(8,128)S(1)} collective-permute-done((f32[24,1024]{1,0:T(8,128)S(1)}, f32[24,1024]{1,0:T(8,128)S(1)}, u32[]{:S(2)}, u32[]{:S(2)}) %collective-permute-start.3) | collective-permute-done | bytes 98336 | tf_op jit(solution)/shard_map/ppermute | solution.py:545
  28.8 6.1 %all-to-all-start = ((f32[8,2,32,128]{3,2,1,0:T(8,128)}), f32[8,2,32,128]{3,2,1,0:T(8,128)S(1)}, u32[]{:S(2)}, u32[]{:S(2)}) async-start(f32[8,2,32,128]{3,2,1,0:T(8,128)} %shard_map.102), calls=%async_computation | async-start | bytes 524288 | tf_op jit(solution)/shard_map/all_to_all | solution.py:555
  34.9 9.5 %all-to-all-done.refs_0_ = f32[8,2,32,128]{3,2,1,0:T(8,128)S(1)} async-done(((f32[8,2,32,128]{3,2,1,0:T(8,128)}), f32[8,2,32,128]{3,2,1,0:T(8,128)S(1)}, u32[]{:S(2)}, u32[]{:S(2)}) %all-to-all-start) | async-done | bytes 262176 | tf_op jit(solution)/shard_map/all_to_all | solution.py:555
  45.5 3.5 %all-to-all-start.1 = ((f32[8,2,32,128]{3,2,1,0:T(8,128)}), f32[8,2,32,128]{3,2,1,0:T(8,128)S(1)}, u32[]{:S(2)}, u32[]{:S(2)}) async-start(f32[8,2,32,128]{3,2,1,0:T(8,128)} %shard_map.103), calls=%async_computation.1 | async-start | bytes 524288 | tf_op jit(solution)/shard_map/all_to_all | solution.py:555
  52.4 6.3 %all-to-all-done.1.refs_1_ = f32[8,2,32,128]{3,2,1,0:T(8,128)S(1)} async-done(((f32[8,2,32,128]{3,2,1,0:T(8,128)}), f32[8,2,32,128]{3,2,1,0:T(8,128)S(1)}, u32[]{:S(2)}, u32[]{:S(2)}) %all-to-all-start.1) | async-done | bytes 262176 | tf_op jit(solution)/shard_map/all_to_all | solution.py:555
  58.8 2.1 collective-permute-start.5
  60.9 2.4 collective-permute-start.4
  63.3 3.2 %collective-permute-done.5.refs_2_.refs_3_ = f32[80,1024]{1,0:T(8,128)S(1)} collective-permute-done((f32[80,1024]{1,0:T(8,128)S(1)}, f32[80,1024]{1,0:T(8,128)S(1)}, u32[]{:S(2)}, u32[]{:S(2)}) %collective-permute-start.5) | collective-permute-done | bytes 327712 | tf_op jit(solution)/shard_map/ppermute | solution.py:545
  66.5 5.1 %collective-permute-done.4.refs_1_.refs_2_ = f32[80,1024]{1,0:T(8,128)S(1)} collective-permute-done((f32[80,1024]{1,0:T(8,128)S(1)}, f32[80,1024]{1,0:T(8,128)S(1)}, u32[]{:S(2)}, u32[]{:S(2)}) %collective-permute-start.4) | collective-permute-done | bytes 327712 | tf_op jit(solution)/shard_map/ppermute | solution.py:545
  72.2 2.1 collective-permute-start.6
  76.8 6.9 %collective-permute-done.7.refs_5_ = f32[32,1024]{1,0:T(8,128)S(1)} collective-permute-done((f32[32,1024]{1,0:T(8,128)S(1)}, f32[32,1024]{1,0:T(8,128)S(1)}, u32[]{:S(2)}, u32[]{:S(2)}) %collective-permute-start.7) | collective-permute-done | bytes 131104 | tf_op jit(solution)/shard_map/ppermute | solution.py:545
  88.0 2.4 collective-permute-start.8
  90.4 3.9 %collective-permute-done.8.refs_1_ = f32[24,512]{1,0:T(8,128)S(1)} collective-permute-done((f32[24,512]{1,0:T(8,128)S(1)}, f32[24,512]{1,0:T(8,128)S(1)}, u32[]{:S(2)}, u32[]{:S(2)}) %collective-permute-start.8) | collective-permute-done | bytes 49184 | tf_op jit(solution)/shard_map/ppermute | solution.py:545
  94.4 27.1 %all_to_all.40 = f32[16,16,512]{2,1,0:T(8,128)S(1)} all-to-all(f32[16,16,512]{2,1,0:T(8,128)S(1)} %shard_map.108), channel_id=1, replica_groups={{0,1,2,3,4,5,6,7,8,9,10,11,12,13,14,15},{16,17,18,19,20,21,22,23,24,25,..., dimensions={0} | all-to-all | bytes 1048576 | tf_op jit(solution)/shard_map/all_to_all | solution.py:555
  122.5 17.4 %all_to_all.41.refs_0_ = f32[32,8,128]{2,1,0:T(8,128)S(1)} all-to-all(f32[32,8,128]{2,1,0:T(8,128)S(1)} %shard_map.110), channel_id=1, replica_groups=mesh['py'=16,'px'=32] {'px'}, dimensions={0} | all-to-all | bytes 262144 | tf_op jit(solution)/shard_map/all_to_all | solution.py:555
  140.6 5.6 %all-to-all-start.4 = ((f32[16,8,128]{2,1,0:T(8,128)}), f32[16,8,128]{2,1,0:T(8,128)S(1)}, u32[]{:S(2)}, u32[]{:S(2)}) async-start(f32[16,8,128]{2,1,0:T(8,128)} %shard_map.111), calls=%async_computation.4 | async-start | bytes 131072 | tf_op jit(solution)/shard_map/all_to_all | solution.py:555
  147.1 3.1 %collective-permute-start.12 = (f32[24,512]{1,0:T(8,128)S(1)}, f32[24,512]{1,0:T(8,128)S(1)}, u32[]{:S(2)}, u32[]{:S(2)}) collective-permute-start(f32[24,512]{1,0:T(8,128)S(1)} %shard_map.112.refs_1_), channel_id=1, source_target_pairs={{32,0},{64,32},{96,64},{128,96},{160,128},{192,160},{224,192},{256... | collective-permute-start | bytes 147464 | tf_op jit(solution)/shard_map/ppermute | solution.py:545
  150.2 1.9 collective-permute-start.11
  152.1 4.4 %collective-permute-done.11.refs_2_ = f32[24,512]{1,0:T(8,128)S(1)} collective-permute-done((f32[24,512]{1,0:T(8,128)S(1)}, f32[24,512]{1,0:T(8,128)S(1)}, u32[]{:S(2)}, u32[]{:S(2)}) %collective-permute-start.11) | collective-permute-done | bytes 49184 | tf_op jit(solution)/shard_map/ppermute | solution.py:545
  157.0 1.9 collective-permute-start.14
  158.9 2.4 collective-permute-start.13
  161.3 3.9 %collective-permute-done.13.refs_1_ = f32[24,512]{1,0:T(8,128)S(1)} collective-permute-done((f32[24,512]{1,0:T(8,128)S(1)}, f32[24,512]{1,0:T(8,128)S(1)}, u32[]{:S(2)}, u32[]{:S(2)}) %collective-permute-start.13) | collective-permute-done | bytes 49184 | tf_op jit(solution)/shard_map/ppermute | solution.py:545
  165.5 39.8 %all_to_all.42 = f32[32,16,512]{2,1,0:T(8,128)S(1)} all-to-all(f32[32,16,512]{2,1,0:T(8,128)S(1)} %shard_map.114), channel_id=1, replica_groups=mesh['py'=16,'px'=32] {'px'}, dimensions={0} | all-to-all | bytes 2097152 | tf_op jit(solution)/shard_map/all_to_all | solution.py:555
  205.7 2.0 collective-permute-start.16
  207.8 2.4 collective-permute-start.15
  210.2 3.9 %collective-permute-done.15.refs_1_ = f32[24,512]{1,0:T(8,128)S(1)} collective-permute-done((f32[24,512]{1,0:T(8,128)S(1)}, f32[24,512]{1,0:T(8,128)S(1)}, u32[]{:S(2)}, u32[]{:S(2)}) %collective-permute-start.15) | collective-permute-done | bytes 49184 | tf_op jit(solution)/shard_map/ppermute | solution.py:545
  218.4 4.5 %collective-permute-start.18 = (f32[32,1024]{1,0:T(8,128)S(1)}, f32[32,1024]{1,0:T(8,128)S(1)}, u32[]{:S(2)}, u32[]{:S(2)}) collective-permute-start(f32[32,1024]{1,0:T(8,128)S(1)} %get-tuple-element.52), channel_id=1, source_target_pairs={{32,0},{64,32},{96,64},{128,96},{160,128},{192,160},{224,192},{256... | collective-permute-start | bytes 393224 | tf_op jit(solution)/shard_map/ppermute | solution.py:545
  225.8 17.3 %all_to_all.43.refs_0_ = f32[8,2,32,128]{3,2,1,0:T(8,128)S(1)} all-to-all(f32[8,2,32,128]{3,2,1,0:T(8,128)S(1)} %shard_map.117), channel_id=1, replica_groups={{0,1,2,3,4,5,6,7},{8,9,10,11,12,13,14,15},{16,17,18,19,20,21,22,23},{24..., dimensions={0} | all-to-all | bytes 524288 | tf_op jit(solution)/shard_map/all_to_all | solution.py:555
  243.5 14.2 %all_to_all.44.refs_1_ = f32[8,2,32,128]{3,2,1,0:T(8,128)S(1)} all-to-all(f32[8,2,32,128]{3,2,1,0:T(8,128)S(1)} %shard_map.118), channel_id=1, replica_groups={{0,1,2,3,4,5,6,7},{8,9,10,11,12,13,14,15},{16,17,18,19,20,21,22,23},{24..., dimensions={0} | all-to-all | bytes 524288 | tf_op jit(solution)/shard_map/all_to_all | solution.py:555
  (108 shorter events, 31.3 us)
Async XLA Ops:
  0.0 34.9 %copy-start = (f32[4,256,256]{2,1,0:T(8,128)S(1)}, f32[4,256,256]{2,1,0:T(8,128)}, u32[]{:S(2)}) copy-start(f32[4,256,256]{2,1,0:T(8,128)} %param.16) | copy-start | bytes 3145732
  2.8 24.5 %collective-permute-start = (f32[72,1024]{1,0:T(8,128)S(1)}, f32[72,1024]{1,0:T(8,128)S(1)}, u32[]{:S(2)}, u32[]{:S(2)}) collective-permute-start(f32[72,1024]{1,0:T(8,128)S(1)} %get-tuple-element.32), channel_id=1, source_target_pairs={{0,32},{32,64},{64,96},{96,128},{128,160},{160,192},{192,224},{224... | collective-permute-start | bytes 884744 | tf_op jit(solution)/shard_map/ppermute | solution.py:545
  4.7 22.6 %collective-permute-start.1 = (f32[72,1024]{1,0:T(8,128)S(1)}, f32[72,1024]{1,0:T(8,128)S(1)}, u32[]{:S(2)}, u32[]{:S(2)}) collective-permute-start(f32[72,1024]{1,0:T(8,128)S(1)} %get-tuple-element.33), channel_id=1, source_target_pairs={{32,0},{64,32},{96,64},{128,96},{160,128},{192,160},{224,192},{256... | collective-permute-start | bytes 884744 | tf_op jit(solution)/shard_map/ppermute | solution.py:545
  9.3 9.3 %collective-permute-start.2 = (f32[24,1024]{1,0:T(8,128)S(1)}, f32[24,1024]{1,0:T(8,128)S(1)}, u32[]{:S(2)}, u32[]{:S(2)}) collective-permute-start(f32[24,1024]{1,0:T(8,128)S(1)} %get-tuple-element.34), channel_id=1, source_target_pairs={{0,1},{1,2},{2,3},{3,4},{4,5},{5,6},{6,7},{7,8},{8,9},{9,10},{10,1... | collective-permute-start | bytes 294920 | tf_op jit(solution)/shard_map/ppermute | solution.py:545
  15.4 11.9 %collective-permute-start.3 = (f32[24,1024]{1,0:T(8,128)S(1)}, f32[24,1024]{1,0:T(8,128)S(1)}, u32[]{:S(2)}, u32[]{:S(2)}) collective-permute-start(f32[24,1024]{1,0:T(8,128)S(1)} %get-tuple-element.35), channel_id=1, source_target_pairs={{1,0},{2,1},{3,2},{4,3},{5,4},{6,5},{7,6},{8,7},{9,8},{10,9},{11,1... | collective-permute-start | bytes 294920 | tf_op jit(solution)/shard_map/ppermute | solution.py:545
  28.8 15.6 %all-to-all-start = ((f32[8,2,32,128]{3,2,1,0:T(8,128)}), f32[8,2,32,128]{3,2,1,0:T(8,128)S(1)}, u32[]{:S(2)}, u32[]{:S(2)}) async-start(f32[8,2,32,128]{3,2,1,0:T(8,128)} %shard_map.102), calls=%async_computation | async-start | bytes 524288 | tf_op jit(solution)/shard_map/all_to_all | solution.py:555
  45.5 13.3 %all-to-all-start.1 = ((f32[8,2,32,128]{3,2,1,0:T(8,128)}), f32[8,2,32,128]{3,2,1,0:T(8,128)S(1)}, u32[]{:S(2)}, u32[]{:S(2)}) async-start(f32[8,2,32,128]{3,2,1,0:T(8,128)} %shard_map.103), calls=%async_computation.1 | async-start | bytes 524288 | tf_op jit(solution)/shard_map/all_to_all | solution.py:555
  58.8 24.9 %copy-start.3 = (f32[2,256,256]{2,1,0:T(8,128)S(1)}, f32[2,256,256]{2,1,0:T(8,128)}, u32[]{:S(2)}) copy-start(f32[2,256,256]{2,1,0:T(8,128)} %refs_8_.1) | copy-start | bytes 1572868
  58.8 7.7 %collective-permute-start.5 = (f32[80,1024]{1,0:T(8,128)S(1)}, f32[80,1024]{1,0:T(8,128)S(1)}, u32[]{:S(2)}, u32[]{:S(2)}) collective-permute-start(f32[80,1024]{1,0:T(8,128)S(1)} %shard_map.105.refs_0_.refs_1_), channel_id=1, source_target_pairs={{32,0},{64,32},{96,64},{128,96},{160,128},{192,160},{224,192},{256... | collective-permute-start | bytes 983048 | tf_op jit(solution)/shard_map/ppermute | solution.py:545
  60.9 10.7 %collective-permute-start.4 = (f32[80,1024]{1,0:T(8,128)S(1)}, f32[80,1024]{1,0:T(8,128)S(1)}, u32[]{:S(2)}, u32[]{:S(2)}) collective-permute-start(f32[80,1024]{1,0:T(8,128)S(1)} %shard_map.105.refs_0_.refs_1_), channel_id=1, source_target_pairs={{0,32},{32,64},{64,96},{96,128},{128,160},{160,192},{192,224},{224... | collective-permute-start | bytes 983048 | tf_op jit(solution)/shard_map/ppermute | solution.py:545
  71.6 12.1 %copy-start.14 = (f32[8,512]{1,0:T(8,128)S(1)}, f32[8,512]{1,0:T(8,128)}, u32[]{:S(2)}) copy-start(f32[8,512]{1,0:T(8,128)} %copy-done.13) | copy-start | bytes 49156
  71.6 12.1 %copy-start.17 = (f32[24,128]{1,0:T(8,128)S(1)}, f32[24,128]{1,0:T(8,128)}, u32[]{:S(2)}) copy-start(f32[24,128]{1,0:T(8,128)} %copy-done.16) | copy-start | bytes 36868
  72.2 4.6 %collective-permute-start.6 = (f32[32,1024]{1,0:T(8,128)S(1)}, f32[32,1024]{1,0:T(8,128)S(1)}, u32[]{:S(2)}, u32[]{:S(2)}) collective-permute-start(f32[32,1024]{1,0:T(8,128)S(1)} %get-tuple-element.38), channel_id=1, source_target_pairs={{0,1},{1,2},{2,3},{3,4},{4,5},{5,6},{6,7},{7,8},{8,9},{9,10},{10,1... | collective-permute-start | bytes 393224 | tf_op jit(solution)/shard_map/ppermute | solution.py:545
  74.3 9.4 %collective-permute-start.7 = (f32[32,1024]{1,0:T(8,128)S(1)}, f32[32,1024]{1,0:T(8,128)S(1)}, u32[]{:S(2)}, u32[]{:S(2)}) collective-permute-start(f32[32,1024]{1,0:T(8,128)S(1)} %get-tuple-element.39), channel_id=1, source_target_pairs={{1,0},{2,1},{3,2},{4,3},{5,4},{6,5},{7,6},{8,7},{9,8},{10,9},{11,1... | collective-permute-start | bytes 393224 | tf_op jit(solution)/shard_map/ppermute | solution.py:545
  86.0 35.5 %copy-start.11 = (f32[4,48,1024]{2,1,0:T(8,128)}, f32[4,48,1024]{2,1,0:T(8,128)S(1)}, u32[]{:S(2)}) copy-start(f32[4,48,1024]{2,1,0:T(8,128)S(1)} %get-tuple-element.46.refs_3_) | copy-start | bytes 2359300
  86.0 35.8 %copy-start.7 = (f32[24,512]{1,0:T(8,128)}, f32[24,512]{1,0:T(8,128)S(1)}, u32[]{:S(2)}) copy-start(f32[24,512]{1,0:T(8,128)S(1)} %get-tuple-element.44.refs_4_.refs_2_.refs_5_) | copy-start | bytes 147460
  86.0 35.8 %copy-start.9 = (f32[24,512]{1,0:T(8,128)}, f32[24,512]{1,0:T(8,128)S(1)}, u32[]{:S(2)}) copy-start(f32[24,512]{1,0:T(8,128)S(1)} %get-tuple-element.43.refs_3_.refs_1_.refs_4_) | copy-start | bytes 147460
  86.1 4.3 %collective-permute-start.9 = (f32[24,512]{1,0:T(8,128)S(1)}, f32[24,512]{1,0:T(8,128)S(1)}, u32[]{:S(2)}, u32[]{:S(2)}) collective-permute-start(f32[24,512]{1,0:T(8,128)S(1)} %get-tuple-element.42.refs_0_.refs_2_), channel_id=1, source_target_pairs={{32,0},{64,32},{96,64},{128,96},{160,128},{192,160},{224,192},{256... | collective-permute-start | bytes 147464 | tf_op jit(solution)/shard_map/ppermute | solution.py:545
  88.0 6.3 %collective-permute-start.8 = (f32[24,512]{1,0:T(8,128)S(1)}, f32[24,512]{1,0:T(8,128)S(1)}, u32[]{:S(2)}, u32[]{:S(2)}) collective-permute-start(f32[24,512]{1,0:T(8,128)S(1)} %get-tuple-element.42.refs_0_.refs_2_), channel_id=1, source_target_pairs={{0,32},{32,64},{64,96},{96,128},{128,160},{160,192},{192,224},{224... | collective-permute-start | bytes 147464 | tf_op jit(solution)/shard_map/ppermute | solution.py:545
  94.4 27.1 %copy-start.4 = (f32[2,256,256]{2,1,0:T(8,128)S(1)}, f32[2,256,256]{2,1,0:T(8,128)}, u32[]{:S(2)}) copy-start(f32[2,256,256]{2,1,0:T(8,128)} %param.18) | copy-start | bytes 1572868
  140.6 15.9 %all-to-all-start.4 = ((f32[16,8,128]{2,1,0:T(8,128)}), f32[16,8,128]{2,1,0:T(8,128)S(1)}, u32[]{:S(2)}, u32[]{:S(2)}) async-start(f32[16,8,128]{2,1,0:T(8,128)} %shard_map.111), calls=%async_computation.4 | async-start | bytes 131072 | tf_op jit(solution)/shard_map/all_to_all | solution.py:555
  146.2 10.3 %copy-start.8 = (f32[24,512]{1,0:T(8,128)S(1)}, f32[24,512]{1,0:T(8,128)}, u32[]{:S(2)}) copy-start(f32[24,512]{1,0:T(8,128)} %copy-done.7) | copy-start | bytes 147460
  146.3 0.8 collective-permute-start.10
  147.1 5.0 %collective-permute-start.12 = (f32[24,512]{1,0:T(8,128)S(1)}, f32[24,512]{1,0:T(8,128)S(1)}, u32[]{:S(2)}, u32[]{:S(2)}) collective-permute-start(f32[24,512]{1,0:T(8,128)S(1)} %shard_map.112.refs_1_), channel_id=1, source_target_pairs={{32,0},{64,32},{96,64},{128,96},{160,128},{192,160},{224,192},{256... | collective-permute-start | bytes 147464 | tf_op jit(solution)/shard_map/ppermute | solution.py:545
  150.2 6.3 %collective-permute-start.11 = (f32[24,512]{1,0:T(8,128)S(1)}, f32[24,512]{1,0:T(8,128)S(1)}, u32[]{:S(2)}, u32[]{:S(2)}) collective-permute-start(f32[24,512]{1,0:T(8,128)S(1)} %shard_map.112.refs_1_), channel_id=1, source_target_pairs={{0,32},{32,64},{64,96},{96,128},{128,160},{160,192},{192,224},{224... | collective-permute-start | bytes 147464 | tf_op jit(solution)/shard_map/ppermute | solution.py:545
  157.0 4.3 %collective-permute-start.14 = (f32[24,512]{1,0:T(8,128)S(1)}, f32[24,512]{1,0:T(8,128)S(1)}, u32[]{:S(2)}, u32[]{:S(2)}) collective-permute-start(f32[24,512]{1,0:T(8,128)S(1)} %shard_map.113.refs_0_.refs_2_), channel_id=1, source_target_pairs={{32,0},{64,32},{96,64},{128,96},{160,128},{192,160},{224,192},{256... | collective-permute-start | bytes 147464 | tf_op jit(solution)/shard_map/ppermute | solution.py:545
  158.9 6.3 %collective-permute-start.13 = (f32[24,512]{1,0:T(8,128)S(1)}, f32[24,512]{1,0:T(8,128)S(1)}, u32[]{:S(2)}, u32[]{:S(2)}) collective-permute-start(f32[24,512]{1,0:T(8,128)S(1)} %shard_map.113.refs_0_.refs_2_), channel_id=1, source_target_pairs={{0,32},{32,64},{64,96},{96,128},{128,160},{160,192},{192,224},{224... | collective-permute-start | bytes 147464 | tf_op jit(solution)/shard_map/ppermute | solution.py:545
  165.5 48.6 %copy-start.12 = (f32[4,48,1024]{2,1,0:T(8,128)S(1)}, f32[4,48,1024]{2,1,0:T(8,128)}, u32[]{:S(2)}) copy-start(f32[4,48,1024]{2,1,0:T(8,128)} %copy-done.11) | copy-start | bytes 2359300
  205.7 4.5 %collective-permute-start.16 = (f32[24,512]{1,0:T(8,128)S(1)}, f32[24,512]{1,0:T(8,128)S(1)}, u32[]{:S(2)}, u32[]{:S(2)}) collective-permute-start(f32[24,512]{1,0:T(8,128)S(1)} %shard_map.115.refs_0_), channel_id=1, source_target_pairs={{32,0},{64,32},{96,64},{128,96},{160,128},{192,160},{224,192},{256... | collective-permute-start | bytes 147464 | tf_op jit(solution)/shard_map/ppermute | solution.py:545
  207.8 6.3 %collective-permute-start.15 = (f32[24,512]{1,0:T(8,128)S(1)}, f32[24,512]{1,0:T(8,128)S(1)}, u32[]{:S(2)}, u32[]{:S(2)}) collective-permute-start(f32[24,512]{1,0:T(8,128)S(1)} %shard_map.115.refs_0_), channel_id=1, source_target_pairs={{0,32},{32,64},{64,96},{96,128},{128,160},{160,192},{192,224},{224... | collective-permute-start | bytes 147464 | tf_op jit(solution)/shard_map/ppermute | solution.py:545
  216.5 7.2 %collective-permute-start.17 = (f32[32,1024]{1,0:T(8,128)S(1)}, f32[32,1024]{1,0:T(8,128)S(1)}, u32[]{:S(2)}, u32[]{:S(2)}) collective-permute-start(f32[32,1024]{1,0:T(8,128)S(1)} %get-tuple-element.51), channel_id=1, source_target_pairs={{0,32},{32,64},{64,96},{96,128},{128,160},{160,192},{192,224},{224... | collective-permute-start | bytes 393224 | tf_op jit(solution)/shard_map/ppermute | solution.py:545
  218.4 7.0 %collective-permute-start.18 = (f32[32,1024]{1,0:T(8,128)S(1)}, f32[32,1024]{1,0:T(8,128)S(1)}, u32[]{:S(2)}, u32[]{:S(2)}) collective-permute-start(f32[32,1024]{1,0:T(8,128)S(1)} %get-tuple-element.52), channel_id=1, source_target_pairs={{32,0},{64,32},{96,64},{128,96},{160,128},{192,160},{224,192},{256... | collective-permute-start | bytes 393224 | tf_op jit(solution)/shard_map/ppermute | solution.py:545
  (21 other events, 80.3 us)

commit v5 on v4

--- a/solution.py
+++ b/solution.py
@@ -255,8 +255,7 @@
     cyz_mid[...] = jnp.concatenate([czm[0:1], cym[0:7]], axis=0)
     told[0:8, 0:MZ] = own[0:8]
     told[0:8, MZ:FZ] = own[8:16]
-    for k in range(4):
-        told[8:16, 128 * k : 128 * (k + 1)] = column[8 * k : 8 * (k + 1)]
+    told[8:16, 0:MZ] = jnp.broadcast_to(column[...], (8, MZ))
     told[8:16, MZ:FZ] = cym
 
 
@@ -418,40 +417,31 @@
     inner = roll(own, -MH, 0)[0:MX]
     for at in (0, 16):
         share = mean(told[at : at + 8, 0:MZ] * inner[0:8] + told[at : at + 8, MZ:FZ] * inner[8:16])
-        share = share * told[at + 8 : at + 9, MZ : MZ + 1]
-        theirs = [told[at + 8 : at + 16, 128 * k : 128 * (k + 1)] for k in range(4)]
-        sent = sent + jnp.concatenate(theirs, axis=0) * share
+        sent = sent + told[at + 8 : at + 9, 0:MZ] * (share * told[at + 8 : at + 9, MZ : MZ + 1])
     for at, edge, inner_row, mine in ((32, MH + MX, MH + MX - 1, px == 15), (40, MH - 1, MH, px == 16)):
         line = r_mid[edge : edge + 1] * cx_mid[edge : edge + 1, 0:1] * v[inner_row : inner_row + 1]
-        share = jnp.where(mine, mean(line), 0.0)
-        theirs = [told[at : at + 8, 128 * k : 128 * (k + 1)] for k in range(4)]
-        sent = sent + jnp.concatenate(theirs, axis=0) * share
-    for i in range(N_PX):
-        out[i] = jnp.broadcast_to(sent[i : i + 1], (8, 128))
-
-
-def sum_x(px, py, parts, out):
-    total = parts[0]
-    for i in range(1, N_PX):
-        total = total + parts[i]
-    for j in range(N_PY):
-        out[j] = total
+        sent = sent + told[at : at + 1, 0:MZ] * jnp.where(mine, mean(line), 0.0)
+    lane = iota((8, MZ), 1)
+    at_x, at_y = lane % N_PX, lane // N_PX
+    wide = jnp.broadcast_to(sent, (8, MZ))
+    rows = []
+    for dy in (-1, 0, 1):
+        for dx in (-1, 0, 1):
+            held = (at_x + dx >= 0) & (at_x + dx < N_PX) & (at_y + dy >= 0) & (at_y + dy < N_PY)
+            rows.append(jnp.where(held, roll(wide, -(dy * N_PX + dx), 1), 0.0)[0:1])
+    stacked = jnp.concatenate([rows_of(rows[0:8]), rows_of(rows[8:9])], axis=0)
+    unit = jnp.where(iota((16, 128), 0) == iota((16, 128), 1), 1.0, 0.0).astype(bf16)
+    high, middle, low = thirds(stacked)
+    dims = ((0,), (0,))
+    out[...] = product(high, unit, dims) + (product(middle, unit, dims) + product(low, unit, dims))
 
 
 def second_half(px, py, parts, v, below, above, f_mid, r_mid, cx_mid, cyz_mid, lines, out):
-    total = parts[0]
-    for j in range(1, N_PY):
-        total = total + parts[j]
-    lane = iota((8, 128), 1)
+    total = jnp.sum(parts[...], axis=0, keepdims=True)
     row = iota((ME, MZ), 0)
 
     def raised(plane, dy):
-        held = (py + dy >= 0) & (py + dy < N_PY)
-        at = []
-        for dx in range(3):
-            wanted = (lane == dx * N_PY + py + dy) & held
-            found = jnp.sum(jnp.where(wanted, total, 0.0), axis=1, keepdims=True)[0:1]
-            at.append(found)
+        at = [total[0:1, 3 * (dy + 1) + dx : 3 * (dy + 1) + dx + 1] for dx in range(3)]
         return plane + jnp.where(row < MH, at[0], jnp.where(row < MH + MX, at[1], at[2]))
 
     own = raised(v[...], 0)
@@ -547,6 +537,11 @@
     def across(self, array):
         return lax.ppermute(array, "px", [(15, 16), (16, 15)])
 
+    def everyone(self, rows):
+        sent = rows.reshape(N_PX * N_PY, 1, 128)
+        got = lax.all_to_all(sent, ("py", "px"), 0, 0, tiled=True)
+        return got.reshape(N_PX * N_PY, 128)
+
     def swap(self, axis, array, group):
         n = lax.axis_size(axis)
         groups = None
@@ -555,15 +550,7 @@
         return lax.all_to_all(array, axis, 0, 0, axis_index_groups=groups, tiled=True)
 
 
-def arrange_column(coarse):
-    table = coarse.reshape(N_PY, N_PX).T
-    none = jnp.zeros((1, N_PY), f32)
-    before = jnp.concatenate([none, table[:-1]], axis=0)
-    after = jnp.concatenate([table[1:], none], axis=0)
-    return jnp.concatenate([before, table, after, jnp.zeros((N_PX, 128 - 3 * N_PY), f32)], axis=1)
-
-
-def cycle(d, forcing, inv_density, stretch_x, stretch_y, stretch_z, lines_z0, lines_x0, lines_z1, lines_x1, coarse_inverse):
+def cycle(d, forcing, inv_density, stretch_x, stretch_y, stretch_z, lines_z0, lines_x0, lines_z1, lines_x1, column):
     sx = d.local(lambda a: a.reshape(1, FX), stretch_x)
     sy = d.local(lambda a: a.reshape(1, 2), stretch_y)
     cz = d.local(lambda a: a.reshape(1, FZ), stretch_z)
@@ -577,7 +564,6 @@
     )
     y_below, y_above = d.beside("py", lower, upper)
     x_left, x_right = d.beside("px", low, high)
-    column = d.local(arrange_column, coarse_inverse)
     block = d.block_of(lines_x0)
     u = d.run(own_lines, [own], force, rho, cx, sy, cz, lines_z0)
     slabs = d.run(
@@ -613,12 +599,10 @@
     every = d.local(lambda a: a.reshape(256, MZ), every)
     v = d.run(solve_x_block, [mid], every, rows_x1, v)
     other = d.across(v)
-    sent = d.run(block_mean, [(N_PX, 8, 128)], v, *statics, told, column)
-    parts = d.swap("px", sent, N_PX)
+    sent = d.run(block_mean, [(N_PX * N_PY, 128)], v, *statics, told, column)
+    parts = d.everyone(sent)
     v = d.run(mend, [mid], v, other)
     below, above = d.beside("py", v, v)
-    parts = d.run(sum_x, [(N_PY, 8, 128)], parts)
-    parts = d.swap("py", parts, N_PY)
     v = d.run(second_half, [mid], parts, v, below, above, *statics, lines_z1)
     below, above = d.beside("py", v, v)
     every = d.run(middle_scaled, [(N_PX, MX, MZ)], v, below, above, *statics)

time: 260 us -> 255 us (0.981)
  blocking collectives: 116 us -> 98.8 us
  waiting for transfers between devices: 59.5 us -> 67.5 us
  starting transfers between devices: 62.3 us -> 68.3 us
    all_to_all x5 -> x4, blocking collectives: 116 us -> 98.8 us  [swap(): lax.all_to_all(array, axis, 0, 0, axis_index_groups=groups, tiled=True)]
    all_to_all x0 -> x1, starting transfers between devices: none -> 10.7 us  [everyone(): got = lax.all_to_all(sent, ('py', 'px'), 0, 0, tiled=True)]
    all_to_all x3 -> x2, starting transfers between devices: 15.2 us -> 9.6 us  [swap(): lax.all_to_all(array, axis, 0, 0, axis_index_groups=groups, tiled=True)]
    all_to_all x0 -> x1, waiting for transfers between devices: none -> 5.62 us  [everyone(): got = lax.all_to_all(sent, ('py', 'px'), 0, 0, tiled=True)]
    all_to_all x3 -> x2, waiting for transfers between devices: 15.8 us -> 17.5 us  [swap(): lax.all_to_all(array, axis, 0, 0, axis_index_groups=groups, tiled=True)]
    unnamed x63 -> x60, local copies, waits for them, and re-layouts: 8.29 us -> 7.57 us
    pallas_call x20 -> x19, Pallas kernels: 11 us -> 11.5 us  [run(): pl.pallas_call(kernel, out_shape=[jax.ShapeDtypeStruct(s, f32) for s in s...]
  transfers between devices with their start and end apart: 22 -> 22, of which waited for: 13 -> 14; matrix products, arithmetic and copies ran while one was open for 1% -> 0% of each run, Pallas kernels for 0% -> 0%
where the time goes in v5:
time: 255 us; the launch traced here: 254 us
  blocking collectives  98.8 us (39%)
  starting transfers between devices  68.3 us (27%)
  waiting for transfers between devices  67.5 us (26%)
  Pallas kernels  11.5 us (5%)
  local copies, waits for them, and re-layouts  7.59 us (3%)
    all_to_all x4, blocking collectives, swap(): lax.all_to_all(array, axis, 0, 0, axis_index_groups=groups, tiled=True)  98.8 us
    ppermute x18, starting transfers between devices, beside(): return (lax.ppermute(high, axis, up), lax.ppermute(low, axis, down))  47.2 us
    ppermute x18, waiting for transfers between devices, beside(): return (lax.ppermute(high, axis, up), lax.ppermute(low, axis, down))  44.3 us
    all_to_all x2, waiting for transfers between devices, swap(): lax.all_to_all(array, axis, 0, 0, axis_index_groups=groups, tiled=True)  17.5 us
    pallas_call x19, Pallas kernels, run(): pl.pallas_call(kernel, out_shape=[jax.ShapeDtypeStruct(s, f32) for s in s...  11.5 us
    all_to_all x1, starting transfers between devices, everyone(): got = lax.all_to_all(sent, ('py', 'px'), 0, 0, tiled=True)  10.7 us
    all_to_all x2, starting transfers between devices, swap(): lax.all_to_all(array, axis, 0, 0, axis_index_groups=groups, tiled=True)  9.6 us
    unnamed x60, local copies, waits for them, and re-layouts  7.57 us
  transfers between devices with their start and end apart: 22, of which 14 were waited for; matrix products, arithmetic and copies ran while one was open for 0% of the time, Pallas kernels for 0%

profile of v5, /device:TPU:2, one launch (start us, length us, event | category | flops | bytes accessed | tf_op | source)
XLA Modules:
  0.0 254.1 jit_solution(6845442391865643323)
XLA Ops:
  2.8 1.9 collective-permute-start
  4.7 4.5 %collective-permute-start.1 = (f32[72,1024]{1,0:T(8,128)S(1)}, f32[72,1024]{1,0:T(8,128)S(1)}, u32[]{:S(2)}, u32[]{:S(2)}) collective-permute-start(f32[72,1024]{1,0:T(8,128)S(1)} %get-tuple-element.33), channel_id=1, source_target_pairs={{32,0},{64,32},{96,64},{128,96},{160,128},{192,160},{224,192},{256... | collective-permute-start | bytes 884744 | tf_op jit(solution)/shard_map/ppermute | solution.py:535
  9.3 6.1 %collective-permute-start.2 = (f32[24,1024]{1,0:T(8,128)S(1)}, f32[24,1024]{1,0:T(8,128)S(1)}, u32[]{:S(2)}, u32[]{:S(2)}) collective-permute-start(f32[24,1024]{1,0:T(8,128)S(1)} %get-tuple-element.34), channel_id=1, source_target_pairs={{0,1},{1,2},{2,3},{3,4},{4,5},{5,6},{6,7},{7,8},{8,9},{9,10},{10,1... | collective-permute-start | bytes 294920 | tf_op jit(solution)/shard_map/ppermute | solution.py:535
  18.6 8.7 %collective-permute-done.3.refs_9_.refs_5_.refs_11_ = f32[24,1024]{1,0:T(8,128)S(1)} collective-permute-done((f32[24,1024]{1,0:T(8,128)S(1)}, f32[24,1024]{1,0:T(8,128)S(1)}, u32[]{:S(2)}, u32[]{:S(2)}) %collective-permute-start.3) | collective-permute-done | bytes 98336 | tf_op jit(solution)/shard_map/ppermute | solution.py:535
  28.8 6.1 %all-to-all-start = ((f32[8,2,32,128]{3,2,1,0:T(8,128)}), f32[8,2,32,128]{3,2,1,0:T(8,128)S(1)}, u32[]{:S(2)}, u32[]{:S(2)}) async-start(f32[8,2,32,128]{3,2,1,0:T(8,128)} %shard_map.102), calls=%async_computation | async-start | bytes 524288 | tf_op jit(solution)/shard_map/all_to_all | solution.py:550
  34.9 9.5 %all-to-all-done.refs_0_ = f32[8,2,32,128]{3,2,1,0:T(8,128)S(1)} async-done(((f32[8,2,32,128]{3,2,1,0:T(8,128)}), f32[8,2,32,128]{3,2,1,0:T(8,128)S(1)}, u32[]{:S(2)}, u32[]{:S(2)}) %all-to-all-start) | async-done | bytes 262176 | tf_op jit(solution)/shard_map/all_to_all | solution.py:550
  45.5 3.5 %all-to-all-start.1 = ((f32[8,2,32,128]{3,2,1,0:T(8,128)}), f32[8,2,32,128]{3,2,1,0:T(8,128)S(1)}, u32[]{:S(2)}, u32[]{:S(2)}) async-start(f32[8,2,32,128]{3,2,1,0:T(8,128)} %shard_map.103), calls=%async_computation.1 | async-start | bytes 524288 | tf_op jit(solution)/shard_map/all_to_all | solution.py:550
  50.7 8.0 %all-to-all-done.1.refs_1_ = f32[8,2,32,128]{3,2,1,0:T(8,128)S(1)} async-done(((f32[8,2,32,128]{3,2,1,0:T(8,128)}), f32[8,2,32,128]{3,2,1,0:T(8,128)S(1)}, u32[]{:S(2)}, u32[]{:S(2)}) %all-to-all-start.1) | async-done | bytes 262176 | tf_op jit(solution)/shard_map/all_to_all | solution.py:550
  58.8 2.1 collective-permute-start.5
  60.9 2.4 collective-permute-start.4
  63.3 3.2 %collective-permute-done.5.refs_2_.refs_3_ = f32[80,1024]{1,0:T(8,128)S(1)} collective-permute-done((f32[80,1024]{1,0:T(8,128)S(1)}, f32[80,1024]{1,0:T(8,128)S(1)}, u32[]{:S(2)}, u32[]{:S(2)}) %collective-permute-start.5) | collective-permute-done | bytes 327712 | tf_op jit(solution)/shard_map/ppermute | solution.py:535
  66.5 5.1 %collective-permute-done.4.refs_1_.refs_2_ = f32[80,1024]{1,0:T(8,128)S(1)} collective-permute-done((f32[80,1024]{1,0:T(8,128)S(1)}, f32[80,1024]{1,0:T(8,128)S(1)}, u32[]{:S(2)}, u32[]{:S(2)}) %collective-permute-start.4) | collective-permute-done | bytes 327712 | tf_op jit(solution)/shard_map/ppermute | solution.py:535
  72.2 2.1 collective-permute-start.6
  76.8 6.9 %collective-permute-done.7.refs_5_ = f32[32,1024]{1,0:T(8,128)S(1)} collective-permute-done((f32[32,1024]{1,0:T(8,128)S(1)}, f32[32,1024]{1,0:T(8,128)S(1)}, u32[]{:S(2)}, u32[]{:S(2)}) %collective-permute-start.7) | collective-permute-done | bytes 131104 | tf_op jit(solution)/shard_map/ppermute | solution.py:535
  88.0 2.4 collective-permute-start.8
  90.4 3.9 %collective-permute-done.8.refs_1_ = f32[24,512]{1,0:T(8,128)S(1)} collective-permute-done((f32[24,512]{1,0:T(8,128)S(1)}, f32[24,512]{1,0:T(8,128)S(1)}, u32[]{:S(2)}, u32[]{:S(2)}) %collective-permute-start.8) | collective-permute-done | bytes 49184 | tf_op jit(solution)/shard_map/ppermute | solution.py:535
  94.4 27.1 %all_to_all.35 = f32[16,16,512]{2,1,0:T(8,128)S(1)} all-to-all(f32[16,16,512]{2,1,0:T(8,128)S(1)} %shard_map.108), channel_id=1, replica_groups={{0,1,2,3,4,5,6,7,8,9,10,11,12,13,14,15},{16,17,18,19,20,21,22,23,24,25,..., dimensions={0} | all-to-all | bytes 1048576 | tf_op jit(solution)/shard_map/all_to_all | solution.py:550
  123.6 10.7 %all-to-all-start.3 = ((f32[512,1,128]{2,1,0:T(1,128)}), f32[512,1,128]{2,1,0:T(1,128)S(1)}, u32[]{:S(2)}, u32[]{:S(2)}) async-start(f32[512,1,128]{2,1,0:T(1,128)} %bitcast.6), calls=%async_computation.3 | async-start | bytes 524288 | tf_op jit(solution)/shard_map/all_to_all | solution.py:542
  135.1 3.5 %collective-permute-start.12 = (f32[24,512]{1,0:T(8,128)S(1)}, f32[24,512]{1,0:T(8,128)S(1)}, u32[]{:S(2)}, u32[]{:S(2)}) collective-permute-start(f32[24,512]{1,0:T(8,128)S(1)} %shard_map.111.refs_1_), channel_id=1, source_target_pairs={{32,0},{64,32},{96,64},{128,96},{160,128},{192,160},{224,192},{256... | collective-permute-start | bytes 147464 | tf_op jit(solution)/shard_map/ppermute | solution.py:535
  138.6 1.9 collective-permute-start.11
  140.6 4.5 %collective-permute-done.11.refs_2_ = f32[24,512]{1,0:T(8,128)S(1)} collective-permute-done((f32[24,512]{1,0:T(8,128)S(1)}, f32[24,512]{1,0:T(8,128)S(1)}, u32[]{:S(2)}, u32[]{:S(2)}) %collective-permute-start.11) | collective-permute-done | bytes 49184 | tf_op jit(solution)/shard_map/ppermute | solution.py:535
  145.1 5.6 %all-to-all-done.3 = f32[512,1,128]{2,1,0:T(1,128)S(1)} async-done(((f32[512,1,128]{2,1,0:T(1,128)}), f32[512,1,128]{2,1,0:T(1,128)S(1)}, u32[]{:S(2)}, u32[]{:S(2)}) %all-to-all-start.3) | async-done | bytes 262176 | tf_op jit(solution)/shard_map/all_to_all | solution.py:542
  151.3 2.9 %collective-permute-start.14 = (f32[24,512]{1,0:T(8,128)S(1)}, f32[24,512]{1,0:T(8,128)S(1)}, u32[]{:S(2)}, u32[]{:S(2)}) collective-permute-start(f32[24,512]{1,0:T(8,128)S(1)} %shard_map.112.refs_0_.refs_2_), channel_id=1, source_target_pairs={{32,0},{64,32},{96,64},{128,96},{160,128},{192,160},{224,192},{256... | collective-permute-start | bytes 147464 | tf_op jit(solution)/shard_map/ppermute | solution.py:535
  154.2 1.9 collective-permute-start.13
  156.1 4.4 %collective-permute-done.13.refs_1_ = f32[24,512]{1,0:T(8,128)S(1)} collective-permute-done((f32[24,512]{1,0:T(8,128)S(1)}, f32[24,512]{1,0:T(8,128)S(1)}, u32[]{:S(2)}, u32[]{:S(2)}) %collective-permute-start.13) | collective-permute-done | bytes 49184 | tf_op jit(solution)/shard_map/ppermute | solution.py:535
  160.7 39.9 %all_to_all.36 = f32[32,16,512]{2,1,0:T(8,128)S(1)} all-to-all(f32[32,16,512]{2,1,0:T(8,128)S(1)} %shard_map.113), channel_id=1, replica_groups=mesh['py'=16,'px'=32] {'px'}, dimensions={0} | all-to-all | bytes 2097152 | tf_op jit(solution)/shard_map/all_to_all | solution.py:550
  201.1 2.0 collective-permute-start.16
  203.2 2.4 collective-permute-start.15
  205.6 3.9 %collective-permute-done.15.refs_1_ = f32[24,512]{1,0:T(8,128)S(1)} collective-permute-done((f32[24,512]{1,0:T(8,128)S(1)}, f32[24,512]{1,0:T(8,128)S(1)}, u32[]{:S(2)}, u32[]{:S(2)}) %collective-permute-start.15) | collective-permute-done | bytes 49184 | tf_op jit(solution)/shard_map/ppermute | solution.py:535
  213.8 4.5 %collective-permute-start.18 = (f32[32,1024]{1,0:T(8,128)S(1)}, f32[32,1024]{1,0:T(8,128)S(1)}, u32[]{:S(2)}, u32[]{:S(2)}) collective-permute-start(f32[32,1024]{1,0:T(8,128)S(1)} %get-tuple-element.52), channel_id=1, source_target_pairs={{32,0},{64,32},{96,64},{128,96},{160,128},{192,160},{224,192},{256... | collective-permute-start | bytes 393224 | tf_op jit(solution)/shard_map/ppermute | solution.py:535
  221.2 16.4 %all_to_all.37.refs_0_ = f32[8,2,32,128]{3,2,1,0:T(8,128)S(1)} all-to-all(f32[8,2,32,128]{3,2,1,0:T(8,128)S(1)} %shard_map.116), channel_id=1, replica_groups={{0,1,2,3,4,5,6,7},{8,9,10,11,12,13,14,15},{16,17,18,19,20,21,22,23},{24..., dimensions={0} | all-to-all | bytes 524288 | tf_op jit(solution)/shard_map/all_to_all | solution.py:550
  238.0 15.4 %all_to_all.38.refs_1_ = f32[8,2,32,128]{3,2,1,0:T(8,128)S(1)} all-to-all(f32[8,2,32,128]{3,2,1,0:T(8,128)S(1)} %shard_map.117), channel_id=1, replica_groups={{0,1,2,3,4,5,6,7},{8,9,10,11,12,13,14,15},{16,17,18,19,20,21,22,23},{24..., dimensions={0} | all-to-all | bytes 524288 | tf_op jit(solution)/shard_map/all_to_all | solution.py:550
  (96 shorter events, 30.0 us)
Async XLA Ops:
  0.0 34.9 %copy-start = (f32[4,256,256]{2,1,0:T(8,128)S(1)}, f32[4,256,256]{2,1,0:T(8,128)}, u32[]{:S(2)}) copy-start(f32[4,256,256]{2,1,0:T(8,128)} %param.16) | copy-start | bytes 3145732
  2.8 24.5 %collective-permute-start = (f32[72,1024]{1,0:T(8,128)S(1)}, f32[72,1024]{1,0:T(8,128)S(1)}, u32[]{:S(2)}, u32[]{:S(2)}) collective-permute-start(f32[72,1024]{1,0:T(8,128)S(1)} %get-tuple-element.32), channel_id=1, source_target_pairs={{0,32},{32,64},{64,96},{96,128},{128,160},{160,192},{192,224},{224... | collective-permute-start | bytes 884744 | tf_op jit(solution)/shard_map/ppermute | solution.py:535
  4.7 22.6 %collective-permute-start.1 = (f32[72,1024]{1,0:T(8,128)S(1)}, f32[72,1024]{1,0:T(8,128)S(1)}, u32[]{:S(2)}, u32[]{:S(2)}) collective-permute-start(f32[72,1024]{1,0:T(8,128)S(1)} %get-tuple-element.33), channel_id=1, source_target_pairs={{32,0},{64,32},{96,64},{128,96},{160,128},{192,160},{224,192},{256... | collective-permute-start | bytes 884744 | tf_op jit(solution)/shard_map/ppermute | solution.py:535
  9.3 9.3 %collective-permute-start.2 = (f32[24,1024]{1,0:T(8,128)S(1)}, f32[24,1024]{1,0:T(8,128)S(1)}, u32[]{:S(2)}, u32[]{:S(2)}) collective-permute-start(f32[24,1024]{1,0:T(8,128)S(1)} %get-tuple-element.34), channel_id=1, source_target_pairs={{0,1},{1,2},{2,3},{3,4},{4,5},{5,6},{6,7},{7,8},{8,9},{9,10},{10,1... | collective-permute-start | bytes 294920 | tf_op jit(solution)/shard_map/ppermute | solution.py:535
  15.4 11.9 %collective-permute-start.3 = (f32[24,1024]{1,0:T(8,128)S(1)}, f32[24,1024]{1,0:T(8,128)S(1)}, u32[]{:S(2)}, u32[]{:S(2)}) collective-permute-start(f32[24,1024]{1,0:T(8,128)S(1)} %get-tuple-element.35), channel_id=1, source_target_pairs={{1,0},{2,1},{3,2},{4,3},{5,4},{6,5},{7,6},{8,7},{9,8},{10,9},{11,1... | collective-permute-start | bytes 294920 | tf_op jit(solution)/shard_map/ppermute | solution.py:535
  28.8 15.6 %all-to-all-start = ((f32[8,2,32,128]{3,2,1,0:T(8,128)}), f32[8,2,32,128]{3,2,1,0:T(8,128)S(1)}, u32[]{:S(2)}, u32[]{:S(2)}) async-start(f32[8,2,32,128]{3,2,1,0:T(8,128)} %shard_map.102), calls=%async_computation | async-start | bytes 524288 | tf_op jit(solution)/shard_map/all_to_all | solution.py:550
  45.5 13.3 %all-to-all-start.1 = ((f32[8,2,32,128]{3,2,1,0:T(8,128)}), f32[8,2,32,128]{3,2,1,0:T(8,128)S(1)}, u32[]{:S(2)}, u32[]{:S(2)}) async-start(f32[8,2,32,128]{3,2,1,0:T(8,128)} %shard_map.103), calls=%async_computation.1 | async-start | bytes 524288 | tf_op jit(solution)/shard_map/all_to_all | solution.py:550
  58.8 24.9 %copy-start.3 = (f32[2,256,256]{2,1,0:T(8,128)S(1)}, f32[2,256,256]{2,1,0:T(8,128)}, u32[]{:S(2)}) copy-start(f32[2,256,256]{2,1,0:T(8,128)} %refs_8_.1) | copy-start | bytes 1572868
  58.8 7.7 %collective-permute-start.5 = (f32[80,1024]{1,0:T(8,128)S(1)}, f32[80,1024]{1,0:T(8,128)S(1)}, u32[]{:S(2)}, u32[]{:S(2)}) collective-permute-start(f32[80,1024]{1,0:T(8,128)S(1)} %shard_map.105.refs_0_.refs_1_), channel_id=1, source_target_pairs={{32,0},{64,32},{96,64},{128,96},{160,128},{192,160},{224,192},{256... | collective-permute-start | bytes 983048 | tf_op jit(solution)/shard_map/ppermute | solution.py:535
  60.9 10.7 %collective-permute-start.4 = (f32[80,1024]{1,0:T(8,128)S(1)}, f32[80,1024]{1,0:T(8,128)S(1)}, u32[]{:S(2)}, u32[]{:S(2)}) collective-permute-start(f32[80,1024]{1,0:T(8,128)S(1)} %shard_map.105.refs_0_.refs_1_), channel_id=1, source_target_pairs={{0,32},{32,64},{64,96},{96,128},{128,160},{160,192},{192,224},{224... | collective-permute-start | bytes 983048 | tf_op jit(solution)/shard_map/ppermute | solution.py:535
  72.2 4.6 %collective-permute-start.6 = (f32[32,1024]{1,0:T(8,128)S(1)}, f32[32,1024]{1,0:T(8,128)S(1)}, u32[]{:S(2)}, u32[]{:S(2)}) collective-permute-start(f32[32,1024]{1,0:T(8,128)S(1)} %get-tuple-element.38), channel_id=1, source_target_pairs={{0,1},{1,2},{2,3},{3,4},{4,5},{5,6},{6,7},{7,8},{8,9},{9,10},{10,1... | collective-permute-start | bytes 393224 | tf_op jit(solution)/shard_map/ppermute | solution.py:535
  74.3 9.4 %collective-permute-start.7 = (f32[32,1024]{1,0:T(8,128)S(1)}, f32[32,1024]{1,0:T(8,128)S(1)}, u32[]{:S(2)}, u32[]{:S(2)}) collective-permute-start(f32[32,1024]{1,0:T(8,128)S(1)} %get-tuple-element.39), channel_id=1, source_target_pairs={{1,0},{2,1},{3,2},{4,3},{5,4},{6,5},{7,6},{8,7},{9,8},{10,9},{11,1... | collective-permute-start | bytes 393224 | tf_op jit(solution)/shard_map/ppermute | solution.py:535
  86.0 35.5 %copy-start.11 = (f32[4,48,1024]{2,1,0:T(8,128)}, f32[4,48,1024]{2,1,0:T(8,128)S(1)}, u32[]{:S(2)}) copy-start(f32[4,48,1024]{2,1,0:T(8,128)S(1)} %get-tuple-element.46.refs_3_) | copy-start | bytes 2359300
  86.0 35.8 %copy-start.7 = (f32[24,512]{1,0:T(8,128)}, f32[24,512]{1,0:T(8,128)S(1)}, u32[]{:S(2)}) copy-start(f32[24,512]{1,0:T(8,128)S(1)} %get-tuple-element.44.refs_4_.refs_2_.refs_5_) | copy-start | bytes 147460
  86.0 35.8 %copy-start.9 = (f32[24,512]{1,0:T(8,128)}, f32[24,512]{1,0:T(8,128)S(1)}, u32[]{:S(2)}) copy-start(f32[24,512]{1,0:T(8,128)S(1)} %get-tuple-element.43.refs_3_.refs_1_.refs_4_) | copy-start | bytes 147460
  86.1 4.3 %collective-permute-start.9 = (f32[24,512]{1,0:T(8,128)S(1)}, f32[24,512]{1,0:T(8,128)S(1)}, u32[]{:S(2)}, u32[]{:S(2)}) collective-permute-start(f32[24,512]{1,0:T(8,128)S(1)} %get-tuple-element.42.refs_0_.refs_2_), channel_id=1, source_target_pairs={{32,0},{64,32},{96,64},{128,96},{160,128},{192,160},{224,192},{256... | collective-permute-start | bytes 147464 | tf_op jit(solution)/shard_map/ppermute | solution.py:535
  88.0 6.3 %collective-permute-start.8 = (f32[24,512]{1,0:T(8,128)S(1)}, f32[24,512]{1,0:T(8,128)S(1)}, u32[]{:S(2)}, u32[]{:S(2)}) collective-permute-start(f32[24,512]{1,0:T(8,128)S(1)} %get-tuple-element.42.refs_0_.refs_2_), channel_id=1, source_target_pairs={{0,32},{32,64},{64,96},{96,128},{128,160},{160,192},{192,224},{224... | collective-permute-start | bytes 147464 | tf_op jit(solution)/shard_map/ppermute | solution.py:535
  94.4 27.1 %copy-start.4 = (f32[2,256,256]{2,1,0:T(8,128)S(1)}, f32[2,256,256]{2,1,0:T(8,128)}, u32[]{:S(2)}) copy-start(f32[2,256,256]{2,1,0:T(8,128)} %param.18) | copy-start | bytes 1572868
  123.6 27.2 %all-to-all-start.3 = ((f32[512,1,128]{2,1,0:T(1,128)}), f32[512,1,128]{2,1,0:T(1,128)S(1)}, u32[]{:S(2)}, u32[]{:S(2)}) async-start(f32[512,1,128]{2,1,0:T(1,128)} %bitcast.6), calls=%async_computation.3 | async-start | bytes 524288 | tf_op jit(solution)/shard_map/all_to_all | solution.py:542
  134.2 16.5 %copy-start.8 = (f32[24,512]{1,0:T(8,128)S(1)}, f32[24,512]{1,0:T(8,128)}, u32[]{:S(2)}) copy-start(f32[24,512]{1,0:T(8,128)} %copy-done.7) | copy-start | bytes 147460
  134.2 16.5 %copy-start.10 = (f32[24,512]{1,0:T(8,128)S(1)}, f32[24,512]{1,0:T(8,128)}, u32[]{:S(2)}) copy-start(f32[24,512]{1,0:T(8,128)} %copy-done.9) | copy-start | bytes 147460
  134.3 16.5 %copy-start.15 = (f32[8,512]{1,0:T(8,128)S(1)}, f32[8,512]{1,0:T(8,128)}, u32[]{:S(2)}) copy-start(f32[8,512]{1,0:T(8,128)} %copy-done.13) | copy-start | bytes 49156
  134.3 0.8 collective-permute-start.10
  135.1 5.5 %collective-permute-start.12 = (f32[24,512]{1,0:T(8,128)S(1)}, f32[24,512]{1,0:T(8,128)S(1)}, u32[]{:S(2)}, u32[]{:S(2)}) collective-permute-start(f32[24,512]{1,0:T(8,128)S(1)} %shard_map.111.refs_1_), channel_id=1, source_target_pairs={{32,0},{64,32},{96,64},{128,96},{160,128},{192,160},{224,192},{256... | collective-permute-start | bytes 147464 | tf_op jit(solution)/shard_map/ppermute | solution.py:535
  138.6 6.5 %collective-permute-start.11 = (f32[24,512]{1,0:T(8,128)S(1)}, f32[24,512]{1,0:T(8,128)S(1)}, u32[]{:S(2)}, u32[]{:S(2)}) collective-permute-start(f32[24,512]{1,0:T(8,128)S(1)} %shard_map.111.refs_1_), channel_id=1, source_target_pairs={{0,32},{32,64},{64,96},{96,128},{128,160},{160,192},{192,224},{224... | collective-permute-start | bytes 147464 | tf_op jit(solution)/shard_map/ppermute | solution.py:535
  151.3 4.8 %collective-permute-start.14 = (f32[24,512]{1,0:T(8,128)S(1)}, f32[24,512]{1,0:T(8,128)S(1)}, u32[]{:S(2)}, u32[]{:S(2)}) collective-permute-start(f32[24,512]{1,0:T(8,128)S(1)} %shard_map.112.refs_0_.refs_2_), channel_id=1, source_target_pairs={{32,0},{64,32},{96,64},{128,96},{160,128},{192,160},{224,192},{256... | collective-permute-start | bytes 147464 | tf_op jit(solution)/shard_map/ppermute | solution.py:535
  154.2 6.3 %collective-permute-start.13 = (f32[24,512]{1,0:T(8,128)S(1)}, f32[24,512]{1,0:T(8,128)S(1)}, u32[]{:S(2)}, u32[]{:S(2)}) collective-permute-start(f32[24,512]{1,0:T(8,128)S(1)} %shard_map.112.refs_0_.refs_2_), channel_id=1, source_target_pairs={{0,32},{32,64},{64,96},{96,128},{128,160},{160,192},{192,224},{224... | collective-permute-start | bytes 147464 | tf_op jit(solution)/shard_map/ppermute | solution.py:535
  160.7 48.8 %copy-start.12 = (f32[4,48,1024]{2,1,0:T(8,128)S(1)}, f32[4,48,1024]{2,1,0:T(8,128)}, u32[]{:S(2)}) copy-start(f32[4,48,1024]{2,1,0:T(8,128)} %copy-done.11) | copy-start | bytes 2359300
  201.1 4.5 %collective-permute-start.16 = (f32[24,512]{1,0:T(8,128)S(1)}, f32[24,512]{1,0:T(8,128)S(1)}, u32[]{:S(2)}, u32[]{:S(2)}) collective-permute-start(f32[24,512]{1,0:T(8,128)S(1)} %shard_map.114.refs_0_), channel_id=1, source_target_pairs={{32,0},{64,32},{96,64},{128,96},{160,128},{192,160},{224,192},{256... | collective-permute-start | bytes 147464 | tf_op jit(solution)/shard_map/ppermute | solution.py:535
  203.2 6.3 %collective-permute-start.15 = (f32[24,512]{1,0:T(8,128)S(1)}, f32[24,512]{1,0:T(8,128)S(1)}, u32[]{:S(2)}, u32[]{:S(2)}) collective-permute-start(f32[24,512]{1,0:T(8,128)S(1)} %shard_map.114.refs_0_), channel_id=1, source_target_pairs={{0,32},{32,64},{64,96},{96,128},{128,160},{160,192},{192,224},{224... | collective-permute-start | bytes 147464 | tf_op jit(solution)/shard_map/ppermute | solution.py:535
  211.9 7.2 %collective-permute-start.17 = (f32[32,1024]{1,0:T(8,128)S(1)}, f32[32,1024]{1,0:T(8,128)S(1)}, u32[]{:S(2)}, u32[]{:S(2)}) collective-permute-start(f32[32,1024]{1,0:T(8,128)S(1)} %get-tuple-element.51), channel_id=1, source_target_pairs={{0,32},{32,64},{64,96},{96,128},{128,160},{160,192},{192,224},{224... | collective-permute-start | bytes 393224 | tf_op jit(solution)/shard_map/ppermute | solution.py:535
  213.8 7.0 %collective-permute-start.18 = (f32[32,1024]{1,0:T(8,128)S(1)}, f32[32,1024]{1,0:T(8,128)S(1)}, u32[]{:S(2)}, u32[]{:S(2)}) collective-permute-start(f32[32,1024]{1,0:T(8,128)S(1)} %get-tuple-element.52), channel_id=1, source_target_pairs={{32,0},{64,32},{96,64},{128,96},{160,128},{192,160},{224,192},{256... | collective-permute-start | bytes 393224 | tf_op jit(solution)/shard_map/ppermute | solution.py:535
  (20 other events, 89.0 us)

commit v6 on v5

--- a/solution.py
+++ b/solution.py
@@ -1,10 +1,11 @@
+import functools
+
 import jax
 import jax.numpy as jnp
 from jax import lax
 from jax.experimental import pallas as pl
 from jax.experimental.pallas import tpu as pltpu
 from jax.sharding import PartitionSpec as P
-
 
 shift_term = 0.1
 f32 = jnp.float32
@@ -298,8 +299,8 @@
         picked = [us[j + 1][edge : edge + 1] for j in range(4)]
         out[8:16] = rows_of(picked + [us[j + 1][next_row : next_row + 1] for j in range(4)])
         out[16:24] = rows_of([rs[j][edge : edge + 1] for j in range(4)])
-        out[24:32, 0:MZ] = u[72:80, 0:MZ]
-        out[24:32, MZ:FZ] = u[64:72, 0:MZ] if edge == 0 else u[64:72, MZ:FZ]
+        out[24:32, 0:MZ] = u[64:72, 0:MZ] if edge == 0 else u[64:72, MZ:FZ]
+        out[24:32, MZ:FZ] = jnp.zeros((8, MZ), f32)
 
 
 def to_middle(px, py, q, u, below, above, left, right, force, rho, y_below, y_above, x_left, x_right, cx, cx_mid, cyz_mid, lines, u_ext, f_ext, r_ext, cx_ext, r_mid, f_mid, v_out, told):
@@ -307,8 +308,6 @@
     cx_ext[...] = columns
     told[0:16] = below[64:80]
     told[16:32] = above[64:80]
-    told[32:40] = right[24:32]
-    told[40:48] = left[24:32]
     us = [below[32:64], u[0:32], u[32:64], above[0:32]]
     rs = [y_below[32:64], rho[0], rho[1], y_above[32:64]]
     cross = []
@@ -337,7 +336,7 @@
             before = rows_at([(7, x_left[k + at : k + at + 1])])
             after = rows_at([(0, x_right[k + at : k + at + 1])])
             out[at] = jnp.concatenate([before, own[at], after], axis=0)
-    dense = [left[24:32, MZ:FZ], u[64:72, 0:MZ], u[64:72, MZ:FZ], right[24:32, MZ:FZ]]
+    dense = [left[24:32, 0:MZ], u[64:72, 0:MZ], u[64:72, MZ:FZ], right[24:32, 0:MZ]]
     r_mid[...] = roll(jnp.concatenate(dense, axis=0), MH - 8, 0)[0:ME]
     rhs = restrict_columns(restrict_rows(total))
     rhs = jnp.where(inside_middle(px), rhs, 0.0)
@@ -360,51 +359,45 @@
         out[i] = part
 
 
-def solve_x_middle(px, py, gathered, lines, v, out):
+def rows_for_x(px, py, lines, out):
+    place, row_of_four = px % 4, px // 4
     total = MX * N_PX
-    pieces = []
-    starts = (
-        (jnp.maximum(MX * px - 8, 0), 8),
-        (MX * px, MX),
-        (jnp.minimum(MX * px + MX, total - 8), 8),
-    )
-    for start, size in starts:
-        rows = dyn(lines, start, size)
-        block = (start // 256) * 256
-        pieces.append(dot(rows, dyn(gathered, block, 256)))
-    full = jnp.concatenate(pieces, axis=0)
-    part = roll(full, MH - 8, 0)[0:ME]
-    out[...] = v[...] + jnp.where(inside_middle(px), part, 0.0)
-
-
-def solve_x_block(px, py, gathered, lines, v, out):
-    total = MX * N_PX
-    pieces = []
-    starts = (
-        (jnp.maximum(MX * px - 8, 0), 8),
-        (MX * px, MX),
-        (jnp.minimum(MX * px + MX, total - 8), 8),
-    )
-    for start, size in starts:
-        pieces.append(dyn(lines, start, size))
-    full = dot(jnp.concatenate(pieces, axis=0), gathered[...])
-    part = roll(full, MH - 8, 0)[0:ME]
-    row = iota((ME, MZ), 0) + MX * px - MH
-    first = 256 * (px // 16)
-    held = (row >= first) & (row < first + 256)
-    out[...] = jnp.where(held, v[...] + part, 0.0)
-
-
-def mend(px, py, v, other, out):
-    row = iota((ME, MZ), 0)
-    theirs = other[...]
-    up = jnp.where((row >= MH + MX) & (px == 15), roll(theirs, MX, 0), 0.0)
-    down = jnp.where((row < MH) & (px == 16), roll(theirs, -MX, 0), 0.0)
-    out[...] = v[...] + (up + down)
-
-
-def block_mean(px, py, v, f_mid, r_mid, cx_mid, cyz_mid, told, column, out):
+    parts = []
+    for i in range(8):
+        base = MX * (4 * i + place)
+        pieces = [
+            dyn(lines, jnp.maximum(base - 8, 0), 8),
+            dyn(lines, base, MX),
+            dyn(lines, jnp.minimum(base + MX, total - 8), 8),
+        ]
+        rows = roll(jnp.concatenate(pieces, axis=0), MH - 8, 0)[0:ME]
+        at = iota((ME, 256), 0) + base - MH
+        first = 256 * (row_of_four // 4)
+        parts.append(jnp.where((at >= first) & (at < first + 256), rows, 0.0))
+    full = jnp.concatenate(parts, axis=0)
+    held = None
+    for i in range(4):
+        cut = jnp.where(row_of_four % 4 == i, full[:, 64 * i : 64 * (i + 1)], 0.0)
+        held = cut if held is None else held + cut
+    out[...] = held
+
+
+def spread_x(px, py, gathered, rows, out):
+    solved = dot(rows[...], gathered[...])
+    for i in range(8):
+        out[i] = solved[ME * i : ME * (i + 1)]
+
+
+def gain_x(px, py, v, parts, out):
+    total = v[...]
+    for i in range(8):
+        total = total + parts[i]
+    out[...] = total
+
+
+def block_mean(px, py, before, parts, f_mid, r_mid, cx_mid, cyz_mid, told, column, v, out):
     rho, cx, cy, cz = middle_parts(r_mid, cx_mid, cyz_mid)
+    gain_x(px, py, before, parts, v)
     own = v[...]
     applied = operate(own, near_x(own), 0.0, rho, cx, cy, cz)
     row = iota((ME, MZ), 0)
@@ -418,9 +411,6 @@
     for at in (0, 16):
         share = mean(told[at : at + 8, 0:MZ] * inner[0:8] + told[at : at + 8, MZ:FZ] * inner[8:16])
         sent = sent + told[at + 8 : at + 9, 0:MZ] * (share * told[at + 8 : at + 9, MZ : MZ + 1])
-    for at, edge, inner_row, mine in ((32, MH + MX, MH + MX - 1, px == 15), (40, MH - 1, MH, px == 16)):
-        line = r_mid[edge : edge + 1] * cx_mid[edge : edge + 1, 0:1] * v[inner_row : inner_row + 1]
-        sent = sent + told[at : at + 1, 0:MZ] * jnp.where(mine, mean(line), 0.0)
     lane = iota((8, MZ), 1)
     at_x, at_y = lane % N_PX, lane // N_PX
     wide = jnp.broadcast_to(sent, (8, MZ))
@@ -518,6 +508,7 @@
             in_specs=[whole] * len(args),
             out_specs=[whole] * len(shapes),
             compiler_params=pltpu.CompilerParams(vmem_limit_bytes=24 * 1024 * 1024),
+            name=stage.__name__,
         )(*args)
         return outs if len(shapes) > 1 else outs[0]
 
@@ -534,13 +525,17 @@
         down = [(j, i) for i, j in up]
         return lax.ppermute(high, axis, up), lax.ppermute(low, axis, down)
 
-    def across(self, array):
-        return lax.ppermute(array, "px", [(15, 16), (16, 15)])
-
     def everyone(self, rows):
         sent = rows.reshape(N_PX * N_PY, 1, 128)
         got = lax.all_to_all(sent, ("py", "px"), 0, 0, tiled=True)
         return got.reshape(N_PX * N_PY, 128)
+
+    def solve_x(self, every, rows):
+        fours = [list(range(k, k + 4)) for k in range(0, N_PX, 4)]
+        eights = [list(range(k, N_PX, 4)) for k in range(4)]
+        every = lax.all_to_all(every, "px", 0, 0, axis_index_groups=fours, tiled=True)
+        parts = self.run(spread_x, [(8, ME, MZ)], every.reshape(4 * MX, MZ), rows)
+        return lax.all_to_all(parts, "px", 0, 0, axis_index_groups=eights, tiled=True)
 
     def swap(self, axis, array, group):
         n = lax.axis_size(axis)
@@ -565,6 +560,7 @@
     y_below, y_above = d.beside("py", lower, upper)
     x_left, x_right = d.beside("px", low, high)
     block = d.block_of(lines_x0)
+    rows_x = d.run(rows_for_x, [(8 * ME, 64)], rows_x1)
     u = d.run(own_lines, [own], force, rho, cx, sy, cz, lines_z0)
     slabs = d.run(
         first_half, [slab],
@@ -587,28 +583,22 @@
     left, right = d.beside("px", low, high)
     u_ext, f_ext, r_ext, cx_ext, r_mid, f_mid, v, told = d.run(
         to_middle,
-        [(4, FE, FZ), (2, FE, FZ), (2, FE, FZ), (FE, 128), mid, mid, mid, (48, FZ)],
+        [(4, FE, FZ), (2, FE, FZ), (2, FE, FZ), (FE, 128), mid, mid, mid, (32, FZ)],
         q, u, below, above, left, right, force, rho, y_below, y_above, x_left, x_right,
         cx, cx_mid, cyz_mid, lines_z1,
     )
     statics = (f_mid, r_mid, cx_mid, cyz_mid)
 
     below, above = d.beside("py", v, v)
-    every = d.run(middle_scaled, [(16, MX, MZ)], v, below, above, *statics)
-    every = d.swap("px", every, 16)
-    every = d.local(lambda a: a.reshape(256, MZ), every)
-    v = d.run(solve_x_block, [mid], every, rows_x1, v)
-    other = d.across(v)
-    sent = d.run(block_mean, [(N_PX * N_PY, 128)], v, *statics, told, column)
-    parts = d.everyone(sent)
-    v = d.run(mend, [mid], v, other)
+    parts = d.solve_x(d.run(middle_scaled, [(4, MX, MZ)], v, below, above, *statics), rows_x)
+    v, sent = d.run(block_mean, [mid, (N_PX * N_PY, 128)], v, parts, *statics, told, column)
+    with jax.named_scope("means"):
+        parts = d.everyone(sent)
     below, above = d.beside("py", v, v)
     v = d.run(second_half, [mid], parts, v, below, above, *statics, lines_z1)
     below, above = d.beside("py", v, v)
-    every = d.run(middle_scaled, [(N_PX, MX, MZ)], v, below, above, *statics)
-    every = d.swap("px", every, N_PX)
-    every = d.local(lambda a: a.reshape(MX * N_PX, MZ), every)
-    v = d.run(solve_x_middle, [mid], every, rows_x1, v)
+    parts = d.solve_x(d.run(middle_scaled, [(4, MX, MZ)], v, below, above, *statics), rows_x)
+    v = d.run(gain_x, [mid], v, parts)
 
     below, above = d.beside("py", v, v)
     u, lower, upper = d.run(
@@ -637,10 +627,10 @@
         P(),
         P(("py", "px"), None),
     )
-
-    def step(*args):
-        return cycle(Device(), *args)
-
     return jax.shard_map(
-        step, mesh=mesh, in_specs=placed, out_specs=P("px", "py", None), check_vma=False
-    )
+        functools.partial(cycle, Device()),
+        mesh=mesh,
+        in_specs=placed,
+        out_specs=P("px", "py", None),
+        check_vma=False,
+    )

time: 255 us -> 254 us (level)
  blocking collectives: 98.8 us -> 79.9 us
  starting transfers between devices: 68.3 us -> 81.1 us
  local copies, waits for them, and re-layouts: 7.59 us -> 11.6 us
    all_to_all x4 -> x2, blocking collectives: 98.8 us -> 29.9 us  [swap(): lax.all_to_all(array, axis, 0, 0, axis_index_groups=groups, tiled=True)]
    all_to_all x0 -> x3, blocking collectives: none -> 50.1 us  [the longest x2 38 us: solve_x(): lax.all_to_all(parts, 'px', 0, 0, axis_index_groups=eights, tiled=True)]
    ppermute x18, waiting for transfers between devices: 44.3 us -> 34 us  [beside(): return (lax.ppermute(high, axis, up), lax.ppermute(low, axis, down))]
    ppermute x18, starting transfers between devices: 47.2 us -> 56.6 us  [beside(): return (lax.ppermute(high, axis, up), lax.ppermute(low, axis, down))]
    all_to_all x0 -> x1, waiting for transfers between devices: none -> 7.78 us  [solve_x(): lax.all_to_all(every, 'px', 0, 0, axis_index_groups=fours, tiled=True)]
    all_to_all x0 -> x1, starting transfers between devices: none -> 5.52 us  [solve_x(): lax.all_to_all(every, 'px', 0, 0, axis_index_groups=fours, tiled=True)]
    unnamed x60 -> x68, local copies, waits for them, and re-layouts: 7.57 us -> 11.6 us
    pallas_call x19 -> x20, Pallas kernels: 11.5 us -> 12 us  [run(): pl.pallas_call(kernel, out_shape=[jax.ShapeDtypeStruct(s, f32) for s in s...]
  transfers between devices with their start and end apart: 22 -> 22, of which waited for: 14 -> 16; matrix products, arithmetic and copies ran while one was open for 0% -> 0% of each run, Pallas kernels for 0% -> 1%
where the time goes in v6:
time: 254 us; the launch traced here: 253 us
  starting transfers between devices  81.1 us (32%)
  blocking collectives  79.9 us (31%)
  waiting for transfers between devices  67.5 us (27%)
  Pallas kernels  12 us (5%)
  local copies, waits for them, and re-layouts  11.6 us (5%)
    ppermute x18, starting transfers between devices, beside(): return (lax.ppermute(high, axis, up), lax.ppermute(low, axis, down))  56.6 us
    all_to_all x2, blocking collectives, solve_x(): lax.all_to_all(parts, 'px', 0, 0, axis_index_groups=eights, tiled=True)  38 us
    ppermute x18, waiting for transfers between devices, beside(): return (lax.ppermute(high, axis, up), lax.ppermute(low, axis, down))  34 us
    all_to_all x2, blocking collectives, swap(): lax.all_to_all(array, axis, 0, 0, axis_index_groups=groups, tiled=True)  29.9 us
    all_to_all x2, waiting for transfers between devices, swap(): lax.all_to_all(array, axis, 0, 0, axis_index_groups=groups, tiled=True)  17.6 us
    all_to_all x1, blocking collectives, solve_x(): lax.all_to_all(every, 'px', 0, 0, axis_index_groups=fours, tiled=True)  12.1 us
    pallas_call x20, Pallas kernels, run(): pl.pallas_call(kernel, out_shape=[jax.ShapeDtypeStruct(s, f32) for s in s...  12 us
    unnamed x68, local copies, waits for them, and re-layouts  11.6 us
  transfers between devices with their start and end apart: 22, of which 16 were waited for; matrix products, arithmetic and copies ran while one was open for 0% of the time, Pallas kernels for 1%

profile of v6, /device:TPU:2, one launch (start us, length us, event | category | flops | bytes accessed | tf_op | source)
XLA Modules:
  0.0 252.6 jit_solution(15124100397528988300)
XLA Ops:
  2.8 1.9 collective-permute-start
  4.7 4.5 %collective-permute-start.1 = (f32[72,1024]{1,0:T(8,128)S(1)}, f32[72,1024]{1,0:T(8,128)S(1)}, u32[]{:S(2)}, u32[]{:S(2)}) collective-permute-start(f32[72,1024]{1,0:T(8,128)S(1)} %get-tuple-element.35), channel_id=1, source_target_pairs={{32,0},{64,32},{96,64},{128,96},{160,128},{192,160},{224,192},{256... | collective-permute-start | bytes 884744 | tf_op jit(solution)/shard_map/ppermute | solution.py:526
  9.3 6.1 %collective-permute-start.2 = (f32[24,1024]{1,0:T(8,128)S(1)}, f32[24,1024]{1,0:T(8,128)S(1)}, u32[]{:S(2)}, u32[]{:S(2)}) collective-permute-start(f32[24,1024]{1,0:T(8,128)S(1)} %get-tuple-element.36), channel_id=1, source_target_pairs={{0,1},{1,2},{2,3},{3,4},{4,5},{5,6},{6,7},{7,8},{8,9},{9,10},{10,1... | collective-permute-start | bytes 294920 | tf_op jit(solution)/shard_map/ppermute | solution.py:526
  18.6 8.7 %collective-permute-done.3.refs_9_.refs_5_.refs_11_ = f32[24,1024]{1,0:T(8,128)S(1)} collective-permute-done((f32[24,1024]{1,0:T(8,128)S(1)}, f32[24,1024]{1,0:T(8,128)S(1)}, u32[]{:S(2)}, u32[]{:S(2)}) %collective-permute-start.3) | collective-permute-done | bytes 98336 | tf_op jit(solution)/shard_map/ppermute | solution.py:526
  28.8 6.1 %all-to-all-start = ((f32[8,2,32,128]{3,2,1,0:T(8,128)}), f32[8,2,32,128]{3,2,1,0:T(8,128)S(1)}, u32[]{:S(2)}, u32[]{:S(2)}) async-start(f32[8,2,32,128]{3,2,1,0:T(8,128)} %first_half.1), calls=%async_computation | async-start | bytes 524288 | tf_op jit(solution)/shard_map/all_to_all | solution.py:545
  34.9 9.5 %all-to-all-done.refs_0_ = f32[8,2,32,128]{3,2,1,0:T(8,128)S(1)} async-done(((f32[8,2,32,128]{3,2,1,0:T(8,128)}), f32[8,2,32,128]{3,2,1,0:T(8,128)S(1)}, u32[]{:S(2)}, u32[]{:S(2)}) %all-to-all-start) | async-done | bytes 262176 | tf_op jit(solution)/shard_map/all_to_all | solution.py:545
  45.5 3.5 %all-to-all-start.1 = ((f32[8,2,32,128]{3,2,1,0:T(8,128)}), f32[8,2,32,128]{3,2,1,0:T(8,128)S(1)}, u32[]{:S(2)}, u32[]{:S(2)}) async-start(f32[8,2,32,128]{3,2,1,0:T(8,128)} %solve_x_fine.2), calls=%async_computation.1 | async-start | bytes 524288 | tf_op jit(solution)/shard_map/all_to_all | solution.py:545
  50.7 8.0 %all-to-all-done.1.refs_1_ = f32[8,2,32,128]{3,2,1,0:T(8,128)S(1)} async-done(((f32[8,2,32,128]{3,2,1,0:T(8,128)}), f32[8,2,32,128]{3,2,1,0:T(8,128)S(1)}, u32[]{:S(2)}, u32[]{:S(2)}) %all-to-all-start.1) | async-done | bytes 262176 | tf_op jit(solution)/shard_map/all_to_all | solution.py:545
  58.8 2.1 collective-permute-start.4
  60.9 4.5 %collective-permute-start.5 = (f32[80,1024]{1,0:T(8,128)S(1)}, f32[80,1024]{1,0:T(8,128)S(1)}, u32[]{:S(2)}, u32[]{:S(2)}) collective-permute-start(f32[80,1024]{1,0:T(8,128)S(1)} %add_slabs.1.refs_0_.refs_1_), channel_id=1, source_target_pairs={{32,0},{64,32},{96,64},{128,96},{160,128},{192,160},{224,192},{256... | collective-permute-start | bytes 983048 | tf_op jit(solution)/shard_map/ppermute | solution.py:526
  65.4 2.8 %collective-permute-done.4.refs_1_.refs_2_ = f32[80,1024]{1,0:T(8,128)S(1)} collective-permute-done((f32[80,1024]{1,0:T(8,128)S(1)}, f32[80,1024]{1,0:T(8,128)S(1)}, u32[]{:S(2)}, u32[]{:S(2)}) %collective-permute-start.4) | collective-permute-done | bytes 327712 | tf_op jit(solution)/shard_map/ppermute | solution.py:526
  70.6 2.4 collective-permute-start.6
  74.4 2.2 collective-permute-done.6.refs_4_
  76.5 9.0 %collective-permute-done.7.refs_5_ = f32[32,1024]{1,0:T(8,128)S(1)} collective-permute-done((f32[32,1024]{1,0:T(8,128)S(1)}, f32[32,1024]{1,0:T(8,128)S(1)}, u32[]{:S(2)}, u32[]{:S(2)}) %collective-permute-start.7) | collective-permute-done | bytes 131104 | tf_op jit(solution)/shard_map/ppermute | solution.py:526
  89.4 2.0 collective-permute-start.8
  91.4 4.5 %collective-permute-start.9 = (f32[24,512]{1,0:T(8,128)S(1)}, f32[24,512]{1,0:T(8,128)S(1)}, u32[]{:S(2)}, u32[]{:S(2)}) collective-permute-start(f32[24,512]{1,0:T(8,128)S(1)} %get-tuple-element.44.refs_0_), channel_id=1, source_target_pairs={{32,0},{64,32},{96,64},{128,96},{160,128},{192,160},{224,192},{256... | collective-permute-start | bytes 147464 | tf_op jit(solution)/shard_map/ppermute | solution.py:526
  100.2 5.5 %all-to-all-start.2 = ((f32[4,16,512]{2,1,0:T(8,128)}), f32[4,16,512]{2,1,0:T(8,128)S(1)}, u32[]{:S(2)}, u32[]{:S(2)}) async-start(f32[4,16,512]{2,1,0:T(8,128)} %middle_scaled.2), calls=%async_computation.2 | async-start | bytes 262144 | tf_op jit(solution)/shard_map/all_to_all | solution.py:536
  106.9 7.8 %all-to-all-done.2 = f32[4,16,512]{2,1,0:T(8,128)S(1)} async-done(((f32[4,16,512]{2,1,0:T(8,128)}), f32[4,16,512]{2,1,0:T(8,128)S(1)}, u32[]{:S(2)}, u32[]{:S(2)}) %all-to-all-start.2) | async-done | bytes 131104 | tf_op jit(solution)/shard_map/all_to_all | solution.py:536
  115.1 20.7 %all_to_all.45.refs_1_ = f32[8,24,512]{2,1,0:T(8,128)S(1)} all-to-all(f32[8,24,512]{2,1,0:T(8,128)S(1)} %spread_x.2), channel_id=1, replica_groups={{0,4,8,12,16,20,24,28},{1,5,9,13,17,21,25,29},{2,6,10,14,18,22,26,30},{..., dimensions={0} | all-to-all | bytes 786432 | tf_op jit(solution)/shard_map/all_to_all | solution.py:538
  137.1 9.3 %all-to-all-start.4 = ((f32[512,1,128]{2,1,0:T(1,128)}), f32[512,1,128]{2,1,0:T(1,128)S(1)}, u32[]{:S(2)}, u32[]{:S(2)}) async-start(f32[512,1,128]{2,1,0:T(1,128)} %bitcast.6), calls=%async_computation.4 | async-start | bytes 524288 | tf_op jit(solution)/shard_map/means/all_to_all | solution.py:530
  146.4 2.0 collective-permute-start.10
  148.4 4.4 %collective-permute-start.11 = (f32[24,512]{1,0:T(8,128)S(1)}, f32[24,512]{1,0:T(8,128)S(1)}, u32[]{:S(2)}, u32[]{:S(2)}) collective-permute-start(f32[24,512]{1,0:T(8,128)S(1)} %get-tuple-element.49.refs_1_), channel_id=1, source_target_pairs={{32,0},{64,32},{96,64},{128,96},{160,128},{192,160},{224,192},{256... | collective-permute-start | bytes 147464 | tf_op jit(solution)/shard_map/ppermute | solution.py:526
  154.8 8.1 %all-to-all-done.4 = f32[512,1,128]{2,1,0:T(1,128)S(1)} async-done(((f32[512,1,128]{2,1,0:T(1,128)}), f32[512,1,128]{2,1,0:T(1,128)S(1)}, u32[]{:S(2)}, u32[]{:S(2)}) %all-to-all-start.4) | async-done | bytes 262176 | tf_op jit(solution)/shard_map/means/all_to_all | solution.py:530
  165.4 4.5 %collective-permute-start.13 = (f32[24,512]{1,0:T(8,128)S(1)}, f32[24,512]{1,0:T(8,128)S(1)}, u32[]{:S(2)}, u32[]{:S(2)}) collective-permute-start(f32[24,512]{1,0:T(8,128)S(1)} %second_half.1.refs_0_), channel_id=1, source_target_pairs={{32,0},{64,32},{96,64},{128,96},{160,128},{192,160},{224,192},{256... | collective-permute-start | bytes 147464 | tf_op jit(solution)/shard_map/ppermute | solution.py:526
  171.8 12.1 %all_to_all.46 = f32[4,16,512]{2,1,0:T(8,128)S(1)} all-to-all(f32[4,16,512]{2,1,0:T(8,128)S(1)} %middle_scaled.3), channel_id=1, replica_groups={{0,1,2,3},{4,5,6,7},{8,9,10,11},{12,13,14,15},{16,17,18,19},{20,21,22,2..., dimensions={0} | all-to-all | bytes 262144 | tf_op jit(solution)/shard_map/all_to_all | solution.py:536
  184.2 17.3 %all_to_all.47.refs_1_ = f32[8,24,512]{2,1,0:T(8,128)S(1)} all-to-all(f32[8,24,512]{2,1,0:T(8,128)S(1)} %spread_x.3), channel_id=1, replica_groups={{0,4,8,12,16,20,24,28},{1,5,9,13,17,21,25,29},{2,6,10,14,18,22,26,30},{..., dimensions={0} | all-to-all | bytes 786432 | tf_op jit(solution)/shard_map/all_to_all | solution.py:538
  201.5 2.1 collective-permute-start.14
  203.6 4.5 %collective-permute-start.15 = (f32[24,512]{1,0:T(8,128)S(1)}, f32[24,512]{1,0:T(8,128)S(1)}, u32[]{:S(2)}, u32[]{:S(2)}) collective-permute-start(f32[24,512]{1,0:T(8,128)S(1)} %gain_x.1.refs_0_), channel_id=1, source_target_pairs={{32,0},{64,32},{96,64},{128,96},{160,128},{192,160},{224,192},{256... | collective-permute-start | bytes 147464 | tf_op jit(solution)/shard_map/ppermute | solution.py:526
  212.3 4.0 %collective-permute-start.16 = (f32[32,1024]{1,0:T(8,128)S(1)}, f32[32,1024]{1,0:T(8,128)S(1)}, u32[]{:S(2)}, u32[]{:S(2)}) collective-permute-start(f32[32,1024]{1,0:T(8,128)S(1)} %get-tuple-element.55), channel_id=1, source_target_pairs={{0,32},{32,64},{64,96},{96,128},{128,160},{160,192},{192,224},{224... | collective-permute-start | bytes 393224 | tf_op jit(solution)/shard_map/ppermute | solution.py:526
  216.3 2.5 collective-permute-start.17
  221.6 15.2 %all_to_all.48.refs_0_ = f32[8,2,32,128]{3,2,1,0:T(8,128)S(1)} all-to-all(f32[8,2,32,128]{3,2,1,0:T(8,128)S(1)} %last_scaled.1), channel_id=1, replica_groups={{0,1,2,3,4,5,6,7},{8,9,10,11,12,13,14,15},{16,17,18,19,20,21,22,23},{24..., dimensions={0} | all-to-all | bytes 524288 | tf_op jit(solution)/shard_map/all_to_all | solution.py:545
  237.2 14.6 %all_to_all.49.refs_1_ = f32[8,2,32,128]{3,2,1,0:T(8,128)S(1)} all-to-all(f32[8,2,32,128]{3,2,1,0:T(8,128)S(1)} %solve_x_fine.3), channel_id=1, replica_groups={{0,1,2,3,4,5,6,7},{8,9,10,11,12,13,14,15},{16,17,18,19,20,21,22,23},{24..., dimensions={0} | all-to-all | bytes 524288 | tf_op jit(solution)/shard_map/all_to_all | solution.py:545
  (106 shorter events, 39.5 us)
Async XLA Ops:
  0.0 34.9 %copy-start = (f32[4,256,256]{2,1,0:T(8,128)S(1)}, f32[4,256,256]{2,1,0:T(8,128)}, u32[]{:S(2)}) copy-start(f32[4,256,256]{2,1,0:T(8,128)} %param.16) | copy-start | bytes 3145732
  2.8 24.5 %collective-permute-start = (f32[72,1024]{1,0:T(8,128)S(1)}, f32[72,1024]{1,0:T(8,128)S(1)}, u32[]{:S(2)}, u32[]{:S(2)}) collective-permute-start(f32[72,1024]{1,0:T(8,128)S(1)} %get-tuple-element.34), channel_id=1, source_target_pairs={{0,32},{32,64},{64,96},{96,128},{128,160},{160,192},{192,224},{224... | collective-permute-start | bytes 884744 | tf_op jit(solution)/shard_map/ppermute | solution.py:526
  4.7 22.6 %collective-permute-start.1 = (f32[72,1024]{1,0:T(8,128)S(1)}, f32[72,1024]{1,0:T(8,128)S(1)}, u32[]{:S(2)}, u32[]{:S(2)}) collective-permute-start(f32[72,1024]{1,0:T(8,128)S(1)} %get-tuple-element.35), channel_id=1, source_target_pairs={{32,0},{64,32},{96,64},{128,96},{160,128},{192,160},{224,192},{256... | collective-permute-start | bytes 884744 | tf_op jit(solution)/shard_map/ppermute | solution.py:526
  9.3 9.3 %collective-permute-start.2 = (f32[24,1024]{1,0:T(8,128)S(1)}, f32[24,1024]{1,0:T(8,128)S(1)}, u32[]{:S(2)}, u32[]{:S(2)}) collective-permute-start(f32[24,1024]{1,0:T(8,128)S(1)} %get-tuple-element.36), channel_id=1, source_target_pairs={{0,1},{1,2},{2,3},{3,4},{4,5},{5,6},{6,7},{7,8},{8,9},{9,10},{10,1... | collective-permute-start | bytes 294920 | tf_op jit(solution)/shard_map/ppermute | solution.py:526
  15.4 11.9 %collective-permute-start.3 = (f32[24,1024]{1,0:T(8,128)S(1)}, f32[24,1024]{1,0:T(8,128)S(1)}, u32[]{:S(2)}, u32[]{:S(2)}) collective-permute-start(f32[24,1024]{1,0:T(8,128)S(1)} %get-tuple-element.37), channel_id=1, source_target_pairs={{1,0},{2,1},{3,2},{4,3},{5,4},{6,5},{7,6},{8,7},{9,8},{10,9},{11,1... | collective-permute-start | bytes 294920 | tf_op jit(solution)/shard_map/ppermute | solution.py:526
  28.8 15.6 %all-to-all-start = ((f32[8,2,32,128]{3,2,1,0:T(8,128)}), f32[8,2,32,128]{3,2,1,0:T(8,128)S(1)}, u32[]{:S(2)}, u32[]{:S(2)}) async-start(f32[8,2,32,128]{3,2,1,0:T(8,128)} %first_half.1), calls=%async_computation | async-start | bytes 524288 | tf_op jit(solution)/shard_map/all_to_all | solution.py:545
  45.5 13.3 %all-to-all-start.1 = ((f32[8,2,32,128]{3,2,1,0:T(8,128)}), f32[8,2,32,128]{3,2,1,0:T(8,128)S(1)}, u32[]{:S(2)}, u32[]{:S(2)}) async-start(f32[8,2,32,128]{3,2,1,0:T(8,128)} %solve_x_fine.2), calls=%async_computation.1 | async-start | bytes 524288 | tf_op jit(solution)/shard_map/all_to_all | solution.py:545
  58.8 26.7 %copy-start.3 = (f32[2,256,256]{2,1,0:T(8,128)S(1)}, f32[2,256,256]{2,1,0:T(8,128)}, u32[]{:S(2)}) copy-start(f32[2,256,256]{2,1,0:T(8,128)} %refs_8_.1) | copy-start | bytes 1572868
  58.8 9.4 %collective-permute-start.4 = (f32[80,1024]{1,0:T(8,128)S(1)}, f32[80,1024]{1,0:T(8,128)S(1)}, u32[]{:S(2)}, u32[]{:S(2)}) collective-permute-start(f32[80,1024]{1,0:T(8,128)S(1)} %add_slabs.1.refs_0_.refs_1_), channel_id=1, source_target_pairs={{0,32},{32,64},{64,96},{96,128},{128,160},{160,192},{192,224},{224... | collective-permute-start | bytes 983048 | tf_op jit(solution)/shard_map/ppermute | solution.py:526
  60.9 9.1 %collective-permute-start.5 = (f32[80,1024]{1,0:T(8,128)S(1)}, f32[80,1024]{1,0:T(8,128)S(1)}, u32[]{:S(2)}, u32[]{:S(2)}) collective-permute-start(f32[80,1024]{1,0:T(8,128)S(1)} %add_slabs.1.refs_0_.refs_1_), channel_id=1, source_target_pairs={{32,0},{64,32},{96,64},{128,96},{160,128},{192,160},{224,192},{256... | collective-permute-start | bytes 983048 | tf_op jit(solution)/shard_map/ppermute | solution.py:526
  70.6 5.9 %collective-permute-start.6 = (f32[32,1024]{1,0:T(8,128)S(1)}, f32[32,1024]{1,0:T(8,128)S(1)}, u32[]{:S(2)}, u32[]{:S(2)}) collective-permute-start(f32[32,1024]{1,0:T(8,128)S(1)} %get-tuple-element.40), channel_id=1, source_target_pairs={{0,1},{1,2},{2,3},{3,4},{4,5},{5,6},{6,7},{7,8},{8,9},{9,10},{10,1... | collective-permute-start | bytes 393224 | tf_op jit(solution)/shard_map/ppermute | solution.py:526
  73.1 12.4 %collective-permute-start.7 = (f32[32,1024]{1,0:T(8,128)S(1)}, f32[32,1024]{1,0:T(8,128)S(1)}, u32[]{:S(2)}, u32[]{:S(2)}) collective-permute-start(f32[32,1024]{1,0:T(8,128)S(1)} %get-tuple-element.41), channel_id=1, source_target_pairs={{1,0},{2,1},{3,2},{4,3},{5,4},{6,5},{7,6},{8,7},{9,8},{10,9},{11,1... | collective-permute-start | bytes 393224 | tf_op jit(solution)/shard_map/ppermute | solution.py:526
  89.4 6.5 %collective-permute-start.8 = (f32[24,512]{1,0:T(8,128)S(1)}, f32[24,512]{1,0:T(8,128)S(1)}, u32[]{:S(2)}, u32[]{:S(2)}) collective-permute-start(f32[24,512]{1,0:T(8,128)S(1)} %get-tuple-element.44.refs_0_), channel_id=1, source_target_pairs={{0,32},{32,64},{64,96},{96,128},{128,160},{160,192},{192,224},{224... | collective-permute-start | bytes 147464 | tf_op jit(solution)/shard_map/ppermute | solution.py:526
  91.4 6.2 %collective-permute-start.9 = (f32[24,512]{1,0:T(8,128)S(1)}, f32[24,512]{1,0:T(8,128)S(1)}, u32[]{:S(2)}, u32[]{:S(2)}) collective-permute-start(f32[24,512]{1,0:T(8,128)S(1)} %get-tuple-element.44.refs_0_), channel_id=1, source_target_pairs={{32,0},{64,32},{96,64},{128,96},{160,128},{192,160},{224,192},{256... | collective-permute-start | bytes 147464 | tf_op jit(solution)/shard_map/ppermute | solution.py:526
  100.2 14.5 %all-to-all-start.2 = ((f32[4,16,512]{2,1,0:T(8,128)}), f32[4,16,512]{2,1,0:T(8,128)S(1)}, u32[]{:S(2)}, u32[]{:S(2)}) async-start(f32[4,16,512]{2,1,0:T(8,128)} %middle_scaled.2), calls=%async_computation.2 | async-start | bytes 262144 | tf_op jit(solution)/shard_map/all_to_all | solution.py:536
  115.0 20.7 %copy-start.7 = (f32[24,512]{1,0:T(8,128)S(1)}, f32[24,512]{1,0:T(8,128)}, u32[]{:S(2)}) copy-start(f32[24,512]{1,0:T(8,128)} %copy-done.6) | copy-start | bytes 147460
  115.0 20.7 %copy-start.9 = (f32[24,512]{1,0:T(8,128)S(1)}, f32[24,512]{1,0:T(8,128)}, u32[]{:S(2)}) copy-start(f32[24,512]{1,0:T(8,128)} %copy-done.8) | copy-start | bytes 147460
  115.0 20.7 %copy-start.15 = (f32[8,512]{1,0:T(8,128)S(1)}, f32[8,512]{1,0:T(8,128)}, u32[]{:S(2)}) copy-start(f32[8,512]{1,0:T(8,128)} %copy-done.13) | copy-start | bytes 49156
  115.0 20.7 %copy-start.18 = (f32[24,128]{1,0:T(8,128)S(1)}, f32[24,128]{1,0:T(8,128)}, u32[]{:S(2)}) copy-start(f32[24,128]{1,0:T(8,128)} %copy-done.16) | copy-start | bytes 36868
  115.0 20.7 %copy-start.22 = (f32[24,512]{1,0:T(8,128)S(1)}, f32[24,512]{1,0:T(8,128)}, u32[]{:S(2)}) copy-start(f32[24,512]{1,0:T(8,128)} %copy-done.21) | copy-start | bytes 147460
  115.0 20.7 %copy-start.26 = (f32[32,1024]{1,0:T(8,128)S(1)}, f32[32,1024]{1,0:T(8,128)}, u32[]{:S(2)}) copy-start(f32[32,1024]{1,0:T(8,128)} %copy-done.25) | copy-start | bytes 393220
  137.1 25.8 %all-to-all-start.4 = ((f32[512,1,128]{2,1,0:T(1,128)}), f32[512,1,128]{2,1,0:T(1,128)S(1)}, u32[]{:S(2)}, u32[]{:S(2)}) async-start(f32[512,1,128]{2,1,0:T(1,128)} %bitcast.6), calls=%async_computation.4 | async-start | bytes 524288 | tf_op jit(solution)/shard_map/means/all_to_all | solution.py:530
  146.4 7.5 %collective-permute-start.10 = (f32[24,512]{1,0:T(8,128)S(1)}, f32[24,512]{1,0:T(8,128)S(1)}, u32[]{:S(2)}, u32[]{:S(2)}) collective-permute-start(f32[24,512]{1,0:T(8,128)S(1)} %get-tuple-element.49.refs_1_), channel_id=1, source_target_pairs={{0,32},{32,64},{64,96},{96,128},{128,160},{160,192},{192,224},{224... | collective-permute-start | bytes 147464 | tf_op jit(solution)/shard_map/ppermute | solution.py:526
  148.4 6.3 %collective-permute-start.11 = (f32[24,512]{1,0:T(8,128)S(1)}, f32[24,512]{1,0:T(8,128)S(1)}, u32[]{:S(2)}, u32[]{:S(2)}) collective-permute-start(f32[24,512]{1,0:T(8,128)S(1)} %get-tuple-element.49.refs_1_), channel_id=1, source_target_pairs={{32,0},{64,32},{96,64},{128,96},{160,128},{192,160},{224,192},{256... | collective-permute-start | bytes 147464 | tf_op jit(solution)/shard_map/ppermute | solution.py:526
  163.4 6.5 %collective-permute-start.12 = (f32[24,512]{1,0:T(8,128)S(1)}, f32[24,512]{1,0:T(8,128)S(1)}, u32[]{:S(2)}, u32[]{:S(2)}) collective-permute-start(f32[24,512]{1,0:T(8,128)S(1)} %second_half.1.refs_0_), channel_id=1, source_target_pairs={{0,32},{32,64},{64,96},{96,128},{128,160},{160,192},{192,224},{224... | collective-permute-start | bytes 147464 | tf_op jit(solution)/shard_map/ppermute | solution.py:526
  165.4 6.3 %collective-permute-start.13 = (f32[24,512]{1,0:T(8,128)S(1)}, f32[24,512]{1,0:T(8,128)S(1)}, u32[]{:S(2)}, u32[]{:S(2)}) collective-permute-start(f32[24,512]{1,0:T(8,128)S(1)} %second_half.1.refs_0_), channel_id=1, source_target_pairs={{32,0},{64,32},{96,64},{128,96},{160,128},{192,160},{224,192},{256... | collective-permute-start | bytes 147464 | tf_op jit(solution)/shard_map/ppermute | solution.py:526
  171.6 38.2 %copy-start.11 = (f32[4,48,1024]{2,1,0:T(8,128)S(1)}, f32[4,48,1024]{2,1,0:T(8,128)}, u32[]{:S(2)}) copy-start(f32[4,48,1024]{2,1,0:T(8,128)} %copy-done.10) | copy-start | bytes 2359300
  171.8 38.1 %copy-start.2 = (f32[4,256,256]{2,1,0:T(8,128)S(1)}, f32[4,256,256]{2,1,0:T(8,128)}, u32[]{:S(2)}) copy-start(f32[4,256,256]{2,1,0:T(8,128)} %refs_9_.1) | copy-start | bytes 3145732
  201.5 6.6 %collective-permute-start.14 = (f32[24,512]{1,0:T(8,128)S(1)}, f32[24,512]{1,0:T(8,128)S(1)}, u32[]{:S(2)}, u32[]{:S(2)}) collective-permute-start(f32[24,512]{1,0:T(8,128)S(1)} %gain_x.1.refs_0_), channel_id=1, source_target_pairs={{0,32},{32,64},{64,96},{96,128},{128,160},{160,192},{192,224},{224... | collective-permute-start | bytes 147464 | tf_op jit(solution)/shard_map/ppermute | solution.py:526
  203.6 6.3 %collective-permute-start.15 = (f32[24,512]{1,0:T(8,128)S(1)}, f32[24,512]{1,0:T(8,128)S(1)}, u32[]{:S(2)}, u32[]{:S(2)}) collective-permute-start(f32[24,512]{1,0:T(8,128)S(1)} %gain_x.1.refs_0_), channel_id=1, source_target_pairs={{32,0},{64,32},{96,64},{128,96},{160,128},{192,160},{224,192},{256... | collective-permute-start | bytes 147464 | tf_op jit(solution)/shard_map/ppermute | solution.py:526
  212.3 7.2 %collective-permute-start.16 = (f32[32,1024]{1,0:T(8,128)S(1)}, f32[32,1024]{1,0:T(8,128)S(1)}, u32[]{:S(2)}, u32[]{:S(2)}) collective-permute-start(f32[32,1024]{1,0:T(8,128)S(1)} %get-tuple-element.55), channel_id=1, source_target_pairs={{0,32},{32,64},{64,96},{96,128},{128,160},{160,192},{192,224},{224... | collective-permute-start | bytes 393224 | tf_op jit(solution)/shard_map/ppermute | solution.py:526
  216.3 5.0 %collective-permute-start.17 = (f32[32,1024]{1,0:T(8,128)S(1)}, f32[32,1024]{1,0:T(8,128)S(1)}, u32[]{:S(2)}, u32[]{:S(2)}) collective-permute-start(f32[32,1024]{1,0:T(8,128)S(1)} %get-tuple-element.56), channel_id=1, source_target_pairs={{32,0},{64,32},{96,64},{128,96},{160,128},{192,160},{224,192},{256... | collective-permute-start | bytes 393224 | tf_op jit(solution)/shard_map/ppermute | solution.py:526
  (24 other events, 94.0 us)

commit v7 on v6

--- a/solution.py
+++ b/solution.py
@@ -1,11 +1,10 @@
-import functools
-
 import jax
 import jax.numpy as jnp
 from jax import lax
 from jax.experimental import pallas as pl
 from jax.experimental.pallas import tpu as pltpu
 from jax.sharding import PartitionSpec as P
+
 
 shift_term = 0.1
 f32 = jnp.float32
@@ -298,9 +297,10 @@
         next_row = edge + step
         picked = [us[j + 1][edge : edge + 1] for j in range(4)]
         out[8:16] = rows_of(picked + [us[j + 1][next_row : next_row + 1] for j in range(4)])
-        out[16:24] = rows_of([rs[j][edge : edge + 1] for j in range(4)])
-        out[24:32, 0:MZ] = u[64:72, 0:MZ] if edge == 0 else u[64:72, MZ:FZ]
-        out[24:32, MZ:FZ] = jnp.zeros((8, MZ), f32)
+        middle = u[64:68, 0:MZ] if edge == 0 else u[68:72, MZ:FZ]
+        pairs = [jnp.concatenate([middle[2 * i : 2 * i + 1], middle[2 * i + 1 : 2 * i + 2]], axis=1) for i in range(2)]
+        coarse = jnp.concatenate([u[72:73, 0:MZ], u[72:73, 0:MZ]], axis=1)
+        out[16:24] = rows_of([rs[j][edge : edge + 1] for j in range(4)] + pairs + [coarse])
 
 
 def to_middle(px, py, q, u, below, above, left, right, force, rho, y_below, y_above, x_left, x_right, cx, cx_mid, cyz_mid, lines, u_ext, f_ext, r_ext, cx_ext, r_mid, f_mid, v_out, told):
@@ -308,6 +308,8 @@
     cx_ext[...] = columns
     told[0:16] = below[64:80]
     told[16:32] = above[64:80]
+    told[32:40] = jnp.broadcast_to(right[22:23], (8, FZ))
+    told[40:48] = jnp.broadcast_to(left[22:23], (8, FZ))
     us = [below[32:64], u[0:32], u[32:64], above[0:32]]
     rs = [y_below[32:64], rho[0], rho[1], y_above[32:64]]
     cross = []
@@ -336,7 +338,15 @@
             before = rows_at([(7, x_left[k + at : k + at + 1])])
             after = rows_at([(0, x_right[k + at : k + at + 1])])
             out[at] = jnp.concatenate([before, own[at], after], axis=0)
-    dense = [left[24:32, 0:MZ], u[64:72, 0:MZ], u[64:72, MZ:FZ], right[24:32, 0:MZ]]
+    dense = []
+    for side, first in ((left, 4), (right, 0)):
+        rows = []
+        for i in range(2):
+            line = side[20 + i : 21 + i]
+            rows.append((first + 2 * i, line[:, 0:MZ]))
+            rows.append((first + 2 * i + 1, line[:, MZ:FZ]))
+        dense.append(rows_at(rows))
+    dense[1:1] = [u[64:72, 0:MZ], u[64:72, MZ:FZ]]
     r_mid[...] = roll(jnp.concatenate(dense, axis=0), MH - 8, 0)[0:ME]
     rhs = restrict_columns(restrict_rows(total))
     rhs = jnp.where(inside_middle(px), rhs, 0.0)
@@ -395,9 +405,34 @@
     out[...] = total
 
 
-def block_mean(px, py, before, parts, f_mid, r_mid, cx_mid, cyz_mid, told, column, v, out):
+def solve_x_block(px, py, gathered, lines, v, out):
+    total = MX * N_PX
+    pieces = []
+    starts = (
+        (jnp.maximum(MX * px - 8, 0), 8),
+        (MX * px, MX),
+        (jnp.minimum(MX * px + MX, total - 8), 8),
+    )
+    for start, size in starts:
+        pieces.append(dyn(lines, start, size))
+    full = dot(jnp.concatenate(pieces, axis=0), gathered[...])
+    part = roll(full, MH - 8, 0)[0:ME]
+    row = iota((ME, MZ), 0) + MX * px - MH
+    first = 256 * (px // 16)
+    held = (row >= first) & (row < first + 256)
+    out[...] = jnp.where(held, v[...] + part, 0.0)
+
+
+def mend(px, py, v, other, out):
+    row = iota((ME, MZ), 0)
+    theirs = other[...]
+    up = jnp.where((row >= MH + MX) & (px == 15), roll(theirs, MX, 0), 0.0)
+    down = jnp.where((row < MH) & (px == 16), roll(theirs, -MX, 0), 0.0)
+    out[...] = v[...] + (up + down)
+
+
+def block_mean(px, py, v, f_mid, r_mid, cx_mid, cyz_mid, told, column, out):
     rho, cx, cy, cz = middle_parts(r_mid, cx_mid, cyz_mid)
-    gain_x(px, py, before, parts, v)
     own = v[...]
     applied = operate(own, near_x(own), 0.0, rho, cx, cy, cz)
     row = iota((ME, MZ), 0)
@@ -411,6 +446,9 @@
     for at in (0, 16):
         share = mean(told[at : at + 8, 0:MZ] * inner[0:8] + told[at : at + 8, MZ:FZ] * inner[8:16])
         sent = sent + told[at + 8 : at + 9, 0:MZ] * (share * told[at + 8 : at + 9, MZ : MZ + 1])
+    for at, edge, inner_row, mine in ((32, MH + MX, MH + MX - 1, px == 15), (40, MH - 1, MH, px == 16)):
+        line = r_mid[edge : edge + 1] * cx_mid[edge : edge + 1, 0:1] * v[inner_row : inner_row + 1]
+        sent = sent + told[at : at + 1, 0:MZ] * jnp.where(mine, mean(line), 0.0)
     lane = iota((8, MZ), 1)
     at_x, at_y = lane % N_PX, lane // N_PX
     wide = jnp.broadcast_to(sent, (8, MZ))
@@ -508,7 +546,6 @@
             in_specs=[whole] * len(args),
             out_specs=[whole] * len(shapes),
             compiler_params=pltpu.CompilerParams(vmem_limit_bytes=24 * 1024 * 1024),
-            name=stage.__name__,
         )(*args)
         return outs if len(shapes) > 1 else outs[0]
 
@@ -524,6 +561,9 @@
         up = [(i, i + 1) for i in range(n - 1)]
         down = [(j, i) for i, j in up]
         return lax.ppermute(high, axis, up), lax.ppermute(low, axis, down)
+
+    def across(self, array):
+        return lax.ppermute(array, "px", [(15, 16), (16, 15)])
 
     def everyone(self, rows):
         sent = rows.reshape(N_PX * N_PY, 1, 128)
@@ -577,23 +617,27 @@
     u = d.run(add_slabs, [(80, FZ)], u, slabs, told)
     below, above = d.beside("py", u, u)
     q, low, high = d.run(
-        half_residual, [(FX, FZ)] * 3,
+        half_residual, [(FX, FZ), (24, FZ), (24, FZ)],
         u, below, above, force, rho, y_below, y_above, cx, sy, cz,
     )
     left, right = d.beside("px", low, high)
     u_ext, f_ext, r_ext, cx_ext, r_mid, f_mid, v, told = d.run(
         to_middle,
-        [(4, FE, FZ), (2, FE, FZ), (2, FE, FZ), (FE, 128), mid, mid, mid, (32, FZ)],
+        [(4, FE, FZ), (2, FE, FZ), (2, FE, FZ), (FE, 128), mid, mid, mid, (48, FZ)],
         q, u, below, above, left, right, force, rho, y_below, y_above, x_left, x_right,
         cx, cx_mid, cyz_mid, lines_z1,
     )
     statics = (f_mid, r_mid, cx_mid, cyz_mid)
 
     below, above = d.beside("py", v, v)
-    parts = d.solve_x(d.run(middle_scaled, [(4, MX, MZ)], v, below, above, *statics), rows_x)
-    v, sent = d.run(block_mean, [mid, (N_PX * N_PY, 128)], v, parts, *statics, told, column)
-    with jax.named_scope("means"):
-        parts = d.everyone(sent)
+    every = d.run(middle_scaled, [(16, MX, MZ)], v, below, above, *statics)
+    every = d.swap("px", every, 16)
+    every = d.local(lambda a: a.reshape(256, MZ), every)
+    v = d.run(solve_x_block, [mid], every, rows_x1, v)
+    other = d.across(v)
+    sent = d.run(block_mean, [(N_PX * N_PY, 128)], v, *statics, told, column)
+    parts = d.everyone(sent)
+    v = d.run(mend, [mid], v, other)
     below, above = d.beside("py", v, v)
     v = d.run(second_half, [mid], parts, v, below, above, *statics, lines_z1)
     below, above = d.beside("py", v, v)
@@ -627,10 +671,10 @@
         P(),
         P(("py", "px"), None),
     )
+
+    def step(*args):
+        return cycle(Device(), *args)
+
     return jax.shard_map(
-        functools.partial(cycle, Device()),
-        mesh=mesh,
-        in_specs=placed,
-        out_specs=P("px", "py", None),
-        check_vma=False,
-    )
+        step, mesh=mesh, in_specs=placed, out_specs=P("px", "py", None), check_vma=False
+    )

time: 254 us -> 253 us (level)
  blocking collectives: 79.9 us -> 84 us
  local copies, waits for them, and re-layouts: 11.6 us -> 9.05 us
    all_to_all x2 -> x3, blocking collectives: 29.9 us -> 59 us  [swap(): lax.all_to_all(array, axis, 0, 0, axis_index_groups=groups, tiled=True)]
    all_to_all x2 -> x1, blocking collectives: 38 us -> 24.9 us  [solve_x(): lax.all_to_all(parts, 'px', 0, 0, axis_index_groups=eights, tiled=True)]
    all_to_all x1 -> x0, blocking collectives: 12.1 us -> none  [solve_x(): lax.all_to_all(every, 'px', 0, 0, axis_index_groups=fours, tiled=True)]
    unnamed x68 -> x60, local copies, waits for them, and re-layouts: 11.6 us -> 9.03 us
    pallas_call x20 -> x21, Pallas kernels: 12 us -> 12.1 us  [run(): pl.pallas_call(kernel, out_shape=[jax.ShapeDtypeStruct(s, f32) for s in s...]
  transfers between devices with their start and end apart: 22 -> 23, of which waited for: 16 -> 16; matrix products, arithmetic and copies ran while one was open for 0% -> 0% of each run, Pallas kernels for 1% -> 1%
where the time goes in v7:
time: 253 us; the launch traced here: 252 us
  blocking collectives  84 us (33%)
  starting transfers between devices  80.6 us (32%)
  waiting for transfers between devices  65.7 us (26%)
  Pallas kernels  12.1 us (5%)
  local copies, waits for them, and re-layouts  9.05 us (4%)
    all_to_all x3, blocking collectives, swap(): lax.all_to_all(array, axis, 0, 0, axis_index_groups=groups, tiled=True)  59 us
    ppermute x18, starting transfers between devices, beside(): return (lax.ppermute(high, axis, up), lax.ppermute(low, axis, down))  56.6 us
    ppermute x18, waiting for transfers between devices, beside(): return (lax.ppermute(high, axis, up), lax.ppermute(low, axis, down))  32.3 us
    all_to_all x1, blocking collectives, solve_x(): lax.all_to_all(parts, 'px', 0, 0, axis_index_groups=eights, tiled=True)  24.9 us
    all_to_all x2, waiting for transfers between devices, swap(): lax.all_to_all(array, axis, 0, 0, axis_index_groups=groups, tiled=True)  17.5 us
    pallas_call x21, Pallas kernels, run(): pl.pallas_call(kernel, out_shape=[jax.ShapeDtypeStruct(s, f32) for s in s...  12.1 us
    all_to_all x1, starting transfers between devices, everyone(): got = lax.all_to_all(sent, ('py', 'px'), 0, 0, tiled=True)  10.3 us
    all_to_all x2, starting transfers between devices, swap(): lax.all_to_all(array, axis, 0, 0, axis_index_groups=groups, tiled=True)  9.6 us
  transfers between devices with their start and end apart: 23, of which 16 were waited for; matrix products, arithmetic and copies ran while one was open for 0% of the time, Pallas kernels for 1%

profile of v7, /device:TPU:2, one launch (start us, length us, event | category | flops | bytes accessed | tf_op | source)
XLA Modules:
  0.0 251.9 jit_solution(5580242327846010102)
XLA Ops:
  2.8 1.9 collective-permute-start
  4.7 4.5 %collective-permute-start.1 = (f32[72,1024]{1,0:T(8,128)S(1)}, f32[72,1024]{1,0:T(8,128)S(1)}, u32[]{:S(2)}, u32[]{:S(2)}) collective-permute-start(f32[72,1024]{1,0:T(8,128)S(1)} %get-tuple-element.33), channel_id=1, source_target_pairs={{32,0},{64,32},{96,64},{128,96},{160,128},{192,160},{224,192},{256... | collective-permute-start | bytes 884744 | tf_op jit(solution)/shard_map/ppermute | solution.py:563
  9.3 6.1 %collective-permute-start.2 = (f32[24,1024]{1,0:T(8,128)S(1)}, f32[24,1024]{1,0:T(8,128)S(1)}, u32[]{:S(2)}, u32[]{:S(2)}) collective-permute-start(f32[24,1024]{1,0:T(8,128)S(1)} %get-tuple-element.34), channel_id=1, source_target_pairs={{0,1},{1,2},{2,3},{3,4},{4,5},{5,6},{6,7},{7,8},{8,9},{9,10},{10,1... | collective-permute-start | bytes 294920 | tf_op jit(solution)/shard_map/ppermute | solution.py:563
  18.6 8.7 %collective-permute-done.3.refs_9_.refs_5_.refs_11_ = f32[24,1024]{1,0:T(8,128)S(1)} collective-permute-done((f32[24,1024]{1,0:T(8,128)S(1)}, f32[24,1024]{1,0:T(8,128)S(1)}, u32[]{:S(2)}, u32[]{:S(2)}) %collective-permute-start.3) | collective-permute-done | bytes 98336 | tf_op jit(solution)/shard_map/ppermute | solution.py:563
  28.8 6.1 %all-to-all-start = ((f32[8,2,32,128]{3,2,1,0:T(8,128)}), f32[8,2,32,128]{3,2,1,0:T(8,128)S(1)}, u32[]{:S(2)}, u32[]{:S(2)}) async-start(f32[8,2,32,128]{3,2,1,0:T(8,128)} %shard_map.102), calls=%async_computation | async-start | bytes 524288 | tf_op jit(solution)/shard_map/all_to_all | solution.py:585
  34.9 9.5 %all-to-all-done.refs_0_ = f32[8,2,32,128]{3,2,1,0:T(8,128)S(1)} async-done(((f32[8,2,32,128]{3,2,1,0:T(8,128)}), f32[8,2,32,128]{3,2,1,0:T(8,128)S(1)}, u32[]{:S(2)}, u32[]{:S(2)}) %all-to-all-start) | async-done | bytes 262176 | tf_op jit(solution)/shard_map/all_to_all | solution.py:585
  45.5 3.5 %all-to-all-start.1 = ((f32[8,2,32,128]{3,2,1,0:T(8,128)}), f32[8,2,32,128]{3,2,1,0:T(8,128)S(1)}, u32[]{:S(2)}, u32[]{:S(2)}) async-start(f32[8,2,32,128]{3,2,1,0:T(8,128)} %shard_map.103), calls=%async_computation.1 | async-start | bytes 524288 | tf_op jit(solution)/shard_map/all_to_all | solution.py:585
  50.7 8.0 %all-to-all-done.1.refs_1_ = f32[8,2,32,128]{3,2,1,0:T(8,128)S(1)} async-done(((f32[8,2,32,128]{3,2,1,0:T(8,128)}), f32[8,2,32,128]{3,2,1,0:T(8,128)S(1)}, u32[]{:S(2)}, u32[]{:S(2)}) %all-to-all-start.1) | async-done | bytes 262176 | tf_op jit(solution)/shard_map/all_to_all | solution.py:585
  58.8 2.1 collective-permute-start.4
  60.9 4.5 %collective-permute-start.5 = (f32[80,1024]{1,0:T(8,128)S(1)}, f32[80,1024]{1,0:T(8,128)S(1)}, u32[]{:S(2)}, u32[]{:S(2)}) collective-permute-start(f32[80,1024]{1,0:T(8,128)S(1)} %shard_map.105.refs_0_.refs_1_), channel_id=1, source_target_pairs={{32,0},{64,32},{96,64},{128,96},{160,128},{192,160},{224,192},{256... | collective-permute-start | bytes 983048 | tf_op jit(solution)/shard_map/ppermute | solution.py:563
  65.4 2.8 %collective-permute-done.4.refs_1_.refs_2_ = f32[80,1024]{1,0:T(8,128)S(1)} collective-permute-done((f32[80,1024]{1,0:T(8,128)S(1)}, f32[80,1024]{1,0:T(8,128)S(1)}, u32[]{:S(2)}, u32[]{:S(2)}) %collective-permute-start.4) | collective-permute-done | bytes 327712 | tf_op jit(solution)/shard_map/ppermute | solution.py:563
  70.6 2.4 collective-permute-start.6
  75.8 7.9 %collective-permute-done.7.refs_5_ = f32[24,1024]{1,0:T(8,128)S(1)} collective-permute-done((f32[24,1024]{1,0:T(8,128)S(1)}, f32[24,1024]{1,0:T(8,128)S(1)}, u32[]{:S(2)}, u32[]{:S(2)}) %collective-permute-start.7) | collective-permute-done | bytes 98336 | tf_op jit(solution)/shard_map/ppermute | solution.py:563
  86.3 2.1 collective-permute-start.8
  88.4 4.4 %collective-permute-start.9 = (f32[24,512]{1,0:T(8,128)S(1)}, f32[24,512]{1,0:T(8,128)S(1)}, u32[]{:S(2)}, u32[]{:S(2)}) collective-permute-start(f32[24,512]{1,0:T(8,128)S(1)} %get-tuple-element.42.refs_0_.refs_2_), channel_id=1, source_target_pairs={{32,0},{64,32},{96,64},{128,96},{160,128},{192,160},{224,192},{256... | collective-permute-start | bytes 147464 | tf_op jit(solution)/shard_map/ppermute | solution.py:563
  94.7 29.2 %all_to_all.40 = f32[16,16,512]{2,1,0:T(8,128)S(1)} all-to-all(f32[16,16,512]{2,1,0:T(8,128)S(1)} %shard_map.108), channel_id=1, replica_groups={{0,1,2,3,4,5,6,7,8,9,10,11,12,13,14,15},{16,17,18,19,20,21,22,23,24,25,..., dimensions={0} | all-to-all | bytes 1048576 | tf_op jit(solution)/shard_map/all_to_all | solution.py:585
  125.9 10.3 %all-to-all-start.3 = ((f32[512,1,128]{2,1,0:T(1,128)}), f32[512,1,128]{2,1,0:T(1,128)S(1)}, u32[]{:S(2)}, u32[]{:S(2)}) async-start(f32[512,1,128]{2,1,0:T(1,128)} %bitcast.6), calls=%async_computation.3 | async-start | bytes 524288 | tf_op jit(solution)/shard_map/all_to_all | solution.py:570
  137.0 2.0 collective-permute-start.11
  139.0 4.4 %collective-permute-start.12 = (f32[24,512]{1,0:T(8,128)S(1)}, f32[24,512]{1,0:T(8,128)S(1)}, u32[]{:S(2)}, u32[]{:S(2)}) collective-permute-start(f32[24,512]{1,0:T(8,128)S(1)} %shard_map.111.refs_1_), channel_id=1, source_target_pairs={{32,0},{64,32},{96,64},{128,96},{160,128},{192,160},{224,192},{256... | collective-permute-start | bytes 147464 | tf_op jit(solution)/shard_map/ppermute | solution.py:563
  145.5 7.2 %all-to-all-done.3 = f32[512,1,128]{2,1,0:T(1,128)S(1)} async-done(((f32[512,1,128]{2,1,0:T(1,128)}), f32[512,1,128]{2,1,0:T(1,128)S(1)}, u32[]{:S(2)}, u32[]{:S(2)}) %all-to-all-start.3) | async-done | bytes 262176 | tf_op jit(solution)/shard_map/all_to_all | solution.py:570
  153.2 1.9 collective-permute-start.13
  155.1 4.5 %collective-permute-start.14 = (f32[24,512]{1,0:T(8,128)S(1)}, f32[24,512]{1,0:T(8,128)S(1)}, u32[]{:S(2)}, u32[]{:S(2)}) collective-permute-start(f32[24,512]{1,0:T(8,128)S(1)} %shard_map.112.refs_0_), channel_id=1, source_target_pairs={{32,0},{64,32},{96,64},{128,96},{160,128},{192,160},{224,192},{256... | collective-permute-start | bytes 147464 | tf_op jit(solution)/shard_map/ppermute | solution.py:563
  162.2 3.3 %all-to-all-start.4 = ((f32[4,16,512]{2,1,0:T(8,128)}), f32[4,16,512]{2,1,0:T(8,128)S(1)}, u32[]{:S(2)}, u32[]{:S(2)}) async-start(f32[4,16,512]{2,1,0:T(8,128)} %shard_map.113), calls=%async_computation.4 | async-start | bytes 262144 | tf_op jit(solution)/shard_map/all_to_all | solution.py:576
  165.7 8.8 %all-to-all-done.4 = f32[4,16,512]{2,1,0:T(8,128)S(1)} async-done(((f32[4,16,512]{2,1,0:T(8,128)}), f32[4,16,512]{2,1,0:T(8,128)S(1)}, u32[]{:S(2)}, u32[]{:S(2)}) %all-to-all-start.4) | async-done | bytes 131104 | tf_op jit(solution)/shard_map/all_to_all | solution.py:576
  174.7 24.9 %all_to_all.41.refs_1_ = f32[8,24,512]{2,1,0:T(8,128)S(1)} all-to-all(f32[8,24,512]{2,1,0:T(8,128)S(1)} %shard_map.115), channel_id=1, replica_groups={{0,4,8,12,16,20,24,28},{1,5,9,13,17,21,25,29},{2,6,10,14,18,22,26,30},{..., dimensions={0} | all-to-all | bytes 786432 | tf_op jit(solution)/shard_map/all_to_all | solution.py:578
  199.7 2.1 collective-permute-start.15
  201.8 4.5 %collective-permute-start.16 = (f32[24,512]{1,0:T(8,128)S(1)}, f32[24,512]{1,0:T(8,128)S(1)}, u32[]{:S(2)}, u32[]{:S(2)}) collective-permute-start(f32[24,512]{1,0:T(8,128)S(1)} %shard_map.116.refs_0_), channel_id=1, source_target_pairs={{32,0},{64,32},{96,64},{128,96},{160,128},{192,160},{224,192},{256... | collective-permute-start | bytes 147464 | tf_op jit(solution)/shard_map/ppermute | solution.py:563
  211.6 4.0 %collective-permute-start.17 = (f32[32,1024]{1,0:T(8,128)S(1)}, f32[32,1024]{1,0:T(8,128)S(1)}, u32[]{:S(2)}, u32[]{:S(2)}) collective-permute-start(f32[32,1024]{1,0:T(8,128)S(1)} %get-tuple-element.51), channel_id=1, source_target_pairs={{0,32},{32,64},{64,96},{96,128},{128,160},{160,192},{192,224},{224... | collective-permute-start | bytes 393224 | tf_op jit(solution)/shard_map/ppermute | solution.py:563
  215.6 2.5 collective-permute-start.18
  218.8 1.8 collective-permute-done.18.refs_2_
  221.0 15.2 %all_to_all.42.refs_0_ = f32[8,2,32,128]{3,2,1,0:T(8,128)S(1)} all-to-all(f32[8,2,32,128]{3,2,1,0:T(8,128)S(1)} %shard_map.118), channel_id=1, replica_groups={{0,1,2,3,4,5,6,7},{8,9,10,11,12,13,14,15},{16,17,18,19,20,21,22,23},{24..., dimensions={0} | all-to-all | bytes 524288 | tf_op jit(solution)/shard_map/all_to_all | solution.py:585
  236.5 14.6 %all_to_all.43.refs_1_ = f32[8,2,32,128]{3,2,1,0:T(8,128)S(1)} all-to-all(f32[8,2,32,128]{3,2,1,0:T(8,128)S(1)} %shard_map.119), channel_id=1, replica_groups={{0,1,2,3,4,5,6,7},{8,9,10,11,12,13,14,15},{16,17,18,19,20,21,22,23},{24..., dimensions={0} | all-to-all | bytes 524288 | tf_op jit(solution)/shard_map/all_to_all | solution.py:585
  (100 shorter events, 35.6 us)
Async XLA Ops:
  0.0 34.9 %copy-start = (f32[4,256,256]{2,1,0:T(8,128)S(1)}, f32[4,256,256]{2,1,0:T(8,128)}, u32[]{:S(2)}) copy-start(f32[4,256,256]{2,1,0:T(8,128)} %param.16) | copy-start | bytes 3145732
  2.8 24.5 %collective-permute-start = (f32[72,1024]{1,0:T(8,128)S(1)}, f32[72,1024]{1,0:T(8,128)S(1)}, u32[]{:S(2)}, u32[]{:S(2)}) collective-permute-start(f32[72,1024]{1,0:T(8,128)S(1)} %get-tuple-element.32), channel_id=1, source_target_pairs={{0,32},{32,64},{64,96},{96,128},{128,160},{160,192},{192,224},{224... | collective-permute-start | bytes 884744 | tf_op jit(solution)/shard_map/ppermute | solution.py:563
  4.7 22.6 %collective-permute-start.1 = (f32[72,1024]{1,0:T(8,128)S(1)}, f32[72,1024]{1,0:T(8,128)S(1)}, u32[]{:S(2)}, u32[]{:S(2)}) collective-permute-start(f32[72,1024]{1,0:T(8,128)S(1)} %get-tuple-element.33), channel_id=1, source_target_pairs={{32,0},{64,32},{96,64},{128,96},{160,128},{192,160},{224,192},{256... | collective-permute-start | bytes 884744 | tf_op jit(solution)/shard_map/ppermute | solution.py:563
  9.3 9.3 %collective-permute-start.2 = (f32[24,1024]{1,0:T(8,128)S(1)}, f32[24,1024]{1,0:T(8,128)S(1)}, u32[]{:S(2)}, u32[]{:S(2)}) collective-permute-start(f32[24,1024]{1,0:T(8,128)S(1)} %get-tuple-element.34), channel_id=1, source_target_pairs={{0,1},{1,2},{2,3},{3,4},{4,5},{5,6},{6,7},{7,8},{8,9},{9,10},{10,1... | collective-permute-start | bytes 294920 | tf_op jit(solution)/shard_map/ppermute | solution.py:563
  15.4 11.9 %collective-permute-start.3 = (f32[24,1024]{1,0:T(8,128)S(1)}, f32[24,1024]{1,0:T(8,128)S(1)}, u32[]{:S(2)}, u32[]{:S(2)}) collective-permute-start(f32[24,1024]{1,0:T(8,128)S(1)} %get-tuple-element.35), channel_id=1, source_target_pairs={{1,0},{2,1},{3,2},{4,3},{5,4},{6,5},{7,6},{8,7},{9,8},{10,9},{11,1... | collective-permute-start | bytes 294920 | tf_op jit(solution)/shard_map/ppermute | solution.py:563
  28.8 15.6 %all-to-all-start = ((f32[8,2,32,128]{3,2,1,0:T(8,128)}), f32[8,2,32,128]{3,2,1,0:T(8,128)S(1)}, u32[]{:S(2)}, u32[]{:S(2)}) async-start(f32[8,2,32,128]{3,2,1,0:T(8,128)} %shard_map.102), calls=%async_computation | async-start | bytes 524288 | tf_op jit(solution)/shard_map/all_to_all | solution.py:585
  45.5 13.3 %all-to-all-start.1 = ((f32[8,2,32,128]{3,2,1,0:T(8,128)}), f32[8,2,32,128]{3,2,1,0:T(8,128)S(1)}, u32[]{:S(2)}, u32[]{:S(2)}) async-start(f32[8,2,32,128]{3,2,1,0:T(8,128)} %shard_map.103), calls=%async_computation.1 | async-start | bytes 524288 | tf_op jit(solution)/shard_map/all_to_all | solution.py:585
  58.8 24.9 %copy-start.3 = (f32[2,256,256]{2,1,0:T(8,128)S(1)}, f32[2,256,256]{2,1,0:T(8,128)}, u32[]{:S(2)}) copy-start(f32[2,256,256]{2,1,0:T(8,128)} %refs_8_.1) | copy-start | bytes 1572868
  58.8 9.4 %collective-permute-start.4 = (f32[80,1024]{1,0:T(8,128)S(1)}, f32[80,1024]{1,0:T(8,128)S(1)}, u32[]{:S(2)}, u32[]{:S(2)}) collective-permute-start(f32[80,1024]{1,0:T(8,128)S(1)} %shard_map.105.refs_0_.refs_1_), channel_id=1, source_target_pairs={{0,32},{32,64},{64,96},{96,128},{128,160},{160,192},{192,224},{224... | collective-permute-start | bytes 983048 | tf_op jit(solution)/shard_map/ppermute | solution.py:563
  60.9 9.1 %collective-permute-start.5 = (f32[80,1024]{1,0:T(8,128)S(1)}, f32[80,1024]{1,0:T(8,128)S(1)}, u32[]{:S(2)}, u32[]{:S(2)}) collective-permute-start(f32[80,1024]{1,0:T(8,128)S(1)} %shard_map.105.refs_0_.refs_1_), channel_id=1, source_target_pairs={{32,0},{64,32},{96,64},{128,96},{160,128},{192,160},{224,192},{256... | collective-permute-start | bytes 983048 | tf_op jit(solution)/shard_map/ppermute | solution.py:563
  70.6 5.2 %collective-permute-start.6 = (f32[24,1024]{1,0:T(8,128)S(1)}, f32[24,1024]{1,0:T(8,128)S(1)}, u32[]{:S(2)}, u32[]{:S(2)}) collective-permute-start(f32[24,1024]{1,0:T(8,128)S(1)} %get-tuple-element.38), channel_id=1, source_target_pairs={{0,1},{1,2},{2,3},{3,4},{4,5},{5,6},{6,7},{7,8},{8,9},{9,10},{10,1... | collective-permute-start | bytes 294920 | tf_op jit(solution)/shard_map/ppermute | solution.py:563
  73.0 10.6 %collective-permute-start.7 = (f32[24,1024]{1,0:T(8,128)S(1)}, f32[24,1024]{1,0:T(8,128)S(1)}, u32[]{:S(2)}, u32[]{:S(2)}) collective-permute-start(f32[24,1024]{1,0:T(8,128)S(1)} %get-tuple-element.39), channel_id=1, source_target_pairs={{1,0},{2,1},{3,2},{4,3},{5,4},{6,5},{7,6},{8,7},{9,8},{10,9},{11,1... | collective-permute-start | bytes 294920 | tf_op jit(solution)/shard_map/ppermute | solution.py:563
  86.3 37.8 %copy-start.7 = (f32[24,512]{1,0:T(8,128)}, f32[24,512]{1,0:T(8,128)S(1)}, u32[]{:S(2)}) copy-start(f32[24,512]{1,0:T(8,128)S(1)} %get-tuple-element.44.refs_4_.refs_2_.refs_5_) | copy-start | bytes 147460
  86.3 37.8 %copy-start.9 = (f32[24,512]{1,0:T(8,128)}, f32[24,512]{1,0:T(8,128)S(1)}, u32[]{:S(2)}) copy-start(f32[24,512]{1,0:T(8,128)S(1)} %get-tuple-element.43.refs_3_.refs_1_.refs_4_) | copy-start | bytes 147460
  86.3 6.5 %collective-permute-start.8 = (f32[24,512]{1,0:T(8,128)S(1)}, f32[24,512]{1,0:T(8,128)S(1)}, u32[]{:S(2)}, u32[]{:S(2)}) collective-permute-start(f32[24,512]{1,0:T(8,128)S(1)} %get-tuple-element.42.refs_0_.refs_2_), channel_id=1, source_target_pairs={{0,32},{32,64},{64,96},{96,128},{128,160},{160,192},{192,224},{224... | collective-permute-start | bytes 147464 | tf_op jit(solution)/shard_map/ppermute | solution.py:563
  88.4 6.1 %collective-permute-start.9 = (f32[24,512]{1,0:T(8,128)S(1)}, f32[24,512]{1,0:T(8,128)S(1)}, u32[]{:S(2)}, u32[]{:S(2)}) collective-permute-start(f32[24,512]{1,0:T(8,128)S(1)} %get-tuple-element.42.refs_0_.refs_2_), channel_id=1, source_target_pairs={{32,0},{64,32},{96,64},{128,96},{160,128},{192,160},{224,192},{256... | collective-permute-start | bytes 147464 | tf_op jit(solution)/shard_map/ppermute | solution.py:563
  94.7 29.2 %copy-start.4 = (f32[2,256,256]{2,1,0:T(8,128)S(1)}, f32[2,256,256]{2,1,0:T(8,128)}, u32[]{:S(2)}) copy-start(f32[2,256,256]{2,1,0:T(8,128)} %param.18) | copy-start | bytes 1572868
  125.9 26.8 %all-to-all-start.3 = ((f32[512,1,128]{2,1,0:T(1,128)}), f32[512,1,128]{2,1,0:T(1,128)S(1)}, u32[]{:S(2)}, u32[]{:S(2)}) async-start(f32[512,1,128]{2,1,0:T(1,128)} %bitcast.6), calls=%async_computation.3 | async-start | bytes 524288 | tf_op jit(solution)/shard_map/all_to_all | solution.py:570
  136.1 16.5 %copy-start.8 = (f32[24,512]{1,0:T(8,128)S(1)}, f32[24,512]{1,0:T(8,128)}, u32[]{:S(2)}) copy-start(f32[24,512]{1,0:T(8,128)} %copy-done.7) | copy-start | bytes 147460
  136.1 16.5 %copy-start.10 = (f32[24,512]{1,0:T(8,128)S(1)}, f32[24,512]{1,0:T(8,128)}, u32[]{:S(2)}) copy-start(f32[24,512]{1,0:T(8,128)} %copy-done.9) | copy-start | bytes 147460
  136.2 16.5 %copy-start.15 = (f32[8,512]{1,0:T(8,128)S(1)}, f32[8,512]{1,0:T(8,128)}, u32[]{:S(2)}) copy-start(f32[8,512]{1,0:T(8,128)} %copy-done.13) | copy-start | bytes 49156
  136.2 0.8 collective-permute-start.10
  137.0 7.1 %collective-permute-start.11 = (f32[24,512]{1,0:T(8,128)S(1)}, f32[24,512]{1,0:T(8,128)S(1)}, u32[]{:S(2)}, u32[]{:S(2)}) collective-permute-start(f32[24,512]{1,0:T(8,128)S(1)} %shard_map.111.refs_1_), channel_id=1, source_target_pairs={{0,32},{32,64},{64,96},{96,128},{128,160},{160,192},{192,224},{224... | collective-permute-start | bytes 147464 | tf_op jit(solution)/shard_map/ppermute | solution.py:563
  139.0 6.4 %collective-permute-start.12 = (f32[24,512]{1,0:T(8,128)S(1)}, f32[24,512]{1,0:T(8,128)S(1)}, u32[]{:S(2)}, u32[]{:S(2)}) collective-permute-start(f32[24,512]{1,0:T(8,128)S(1)} %shard_map.111.refs_1_), channel_id=1, source_target_pairs={{32,0},{64,32},{96,64},{128,96},{160,128},{192,160},{224,192},{256... | collective-permute-start | bytes 147464 | tf_op jit(solution)/shard_map/ppermute | solution.py:563
  153.2 6.5 %collective-permute-start.13 = (f32[24,512]{1,0:T(8,128)S(1)}, f32[24,512]{1,0:T(8,128)S(1)}, u32[]{:S(2)}, u32[]{:S(2)}) collective-permute-start(f32[24,512]{1,0:T(8,128)S(1)} %shard_map.112.refs_0_), channel_id=1, source_target_pairs={{0,32},{32,64},{64,96},{96,128},{128,160},{160,192},{192,224},{224... | collective-permute-start | bytes 147464 | tf_op jit(solution)/shard_map/ppermute | solution.py:563
  155.1 6.3 %collective-permute-start.14 = (f32[24,512]{1,0:T(8,128)S(1)}, f32[24,512]{1,0:T(8,128)S(1)}, u32[]{:S(2)}, u32[]{:S(2)}) collective-permute-start(f32[24,512]{1,0:T(8,128)S(1)} %shard_map.112.refs_0_), channel_id=1, source_target_pairs={{32,0},{64,32},{96,64},{128,96},{160,128},{192,160},{224,192},{256... | collective-permute-start | bytes 147464 | tf_op jit(solution)/shard_map/ppermute | solution.py:563
  162.2 12.3 %all-to-all-start.4 = ((f32[4,16,512]{2,1,0:T(8,128)}), f32[4,16,512]{2,1,0:T(8,128)S(1)}, u32[]{:S(2)}, u32[]{:S(2)}) async-start(f32[4,16,512]{2,1,0:T(8,128)} %shard_map.113), calls=%async_computation.4 | async-start | bytes 262144 | tf_op jit(solution)/shard_map/all_to_all | solution.py:576
  165.7 42.4 %copy-start.2 = (f32[4,256,256]{2,1,0:T(8,128)S(1)}, f32[4,256,256]{2,1,0:T(8,128)}, u32[]{:S(2)}) copy-start(f32[4,256,256]{2,1,0:T(8,128)} %refs_9_.1) | copy-start | bytes 3145732
  199.7 6.6 %collective-permute-start.15 = (f32[24,512]{1,0:T(8,128)S(1)}, f32[24,512]{1,0:T(8,128)S(1)}, u32[]{:S(2)}, u32[]{:S(2)}) collective-permute-start(f32[24,512]{1,0:T(8,128)S(1)} %shard_map.116.refs_0_), channel_id=1, source_target_pairs={{0,32},{32,64},{64,96},{96,128},{128,160},{160,192},{192,224},{224... | collective-permute-start | bytes 147464 | tf_op jit(solution)/shard_map/ppermute | solution.py:563
  201.8 6.3 %collective-permute-start.16 = (f32[24,512]{1,0:T(8,128)S(1)}, f32[24,512]{1,0:T(8,128)S(1)}, u32[]{:S(2)}, u32[]{:S(2)}) collective-permute-start(f32[24,512]{1,0:T(8,128)S(1)} %shard_map.116.refs_0_), channel_id=1, source_target_pairs={{32,0},{64,32},{96,64},{128,96},{160,128},{192,160},{224,192},{256... | collective-permute-start | bytes 147464 | tf_op jit(solution)/shard_map/ppermute | solution.py:563
  211.6 7.2 %collective-permute-start.17 = (f32[32,1024]{1,0:T(8,128)S(1)}, f32[32,1024]{1,0:T(8,128)S(1)}, u32[]{:S(2)}, u32[]{:S(2)}) collective-permute-start(f32[32,1024]{1,0:T(8,128)S(1)} %get-tuple-element.51), channel_id=1, source_target_pairs={{0,32},{32,64},{64,96},{96,128},{128,160},{160,192},{192,224},{224... | collective-permute-start | bytes 393224 | tf_op jit(solution)/shard_map/ppermute | solution.py:563
  215.6 5.0 %collective-permute-start.18 = (f32[32,1024]{1,0:T(8,128)S(1)}, f32[32,1024]{1,0:T(8,128)S(1)}, u32[]{:S(2)}, u32[]{:S(2)}) collective-permute-start(f32[32,1024]{1,0:T(8,128)S(1)} %get-tuple-element.52), channel_id=1, source_target_pairs={{32,0},{64,32},{96,64},{128,96},{160,128},{192,160},{224,192},{256... | collective-permute-start | bytes 393224 | tf_op jit(solution)/shard_map/ppermute | solution.py:563
  (21 other events, 92.2 us)
